TPU v7x, 32 devices: a whole 2x2x4 slice. The times are simulated.
32 devices in a mesh: seq: 8 (over y, x, core), head: 4 (over z).
Axes of the slice: x: 2, y: 2, z: 4, core: 2. Of those that a mesh axis runs over, the one named last changes fastest.
Arguments:
- qk: bfloat16 [16384, 2048], P('seq', 'head'), may hold values from -480 to 480, as said below
- values: bfloat16 [16384, 2048], P('seq', 'head'), may hold values from -6 to 6
- bucket: int32 [64, 16], replicated, may hold values from 0 to 1
- pair_row: int32 [8, 8, 3], P('seq'), may hold values from 0 to 7, as said below
- pair_col: int32 [8, 8, 3], P('seq'), may hold values from 0 to 7, as said below
- pair_count: int32 [8, 8], P('seq'), may hold values from 0 to 3, as said below
- w_out: bfloat16 [2048, 2048], P('head'), may hold values from -0.125 to 0.125
Outputs:
- projected: bfloat16 [16384, 2048], P(('seq', 'head'))
Inputs may be any that keep to these rules, and one draw needn't show every extreme that they name: `pair_row`: every value is a local block index of the shard it refers to. `pair_col`: every value is a local block index; a pair never joins a block with itself. `pair_count`: some shard has 3 live slots towards every shard in every draw. `qk`: row scales of the vectors may differ widely.
All inputs are finite; a program needn't handle non-finite values.
Results may differ from a plain program's by a relative error of at most 0.014.
Values may be sent and summed in bfloat16 or wider, within the bound.
No kernel may reach another device: no remote copies, remote signals or barrier semaphores. Data moves between devices by JAX's collectives and lax.ppermute only.
A program may use at most 128 MiB of HBM per device.

v0:
```python
import math

import jax
import jax.numpy as jnp
from jax import lax
from jax.sharding import PartitionSpec as P

HD = 128
BLOCK = 256


NEG = -1e30


def inverse_norms(block):
    wide = block.astype(jnp.float32)
    return (lax.rsqrt(jnp.mean(wide * wide, axis=-1) + 1e-06) / math.sqrt(block.shape[-1])).T


def softmax_side(scores, axis):
    top = jnp.max(scores, axis=axis)
    weights = jnp.exp(scores - jnp.expand_dims(top, axis))
    total = jnp.sum(weights, axis=axis)
    return (top, total, weights.astype(jnp.bfloat16))


def pair_parts(q_a, v_a, q_b, v_b, keep):
    gram = jnp.einsum("shd,thd->hst", q_a, q_b, preferred_element_type=jnp.float32)
    srow = gram * inverse_norms(q_b)[:, None, :]
    scol = gram * inverse_norms(q_a)[:, :, None]
    mrow, lrow, prow = softmax_side(srow, 2)
    acc_row = jnp.einsum("hst,thd->shd", prow, v_b, preferred_element_type=jnp.float32)
    mcol, lcol, pcol = softmax_side(scol, 1)
    acc_col = jnp.einsum("hst,shd->thd", pcol, v_a, preferred_element_type=jnp.float32)
    mrow = jnp.where(keep[:, None], mrow, NEG)
    lrow = jnp.where(keep[:, None], lrow, 0.0)
    acc_row = jnp.where(keep[None, :, None], acc_row, 0.0)
    mcol = jnp.where(keep[:, None], mcol, NEG)
    lcol = jnp.where(keep[:, None], lcol, 0.0)
    acc_col = jnp.where(keep[None, :, None], acc_col, 0.0)
    return ((mrow, lrow, acc_row), (mcol, lcol, acc_col))


def diagonal_parts(q_a, v_a):
    gram = jnp.einsum("shd,thd->hst", q_a, q_a, preferred_element_type=jnp.float32)
    srow = gram * inverse_norms(q_a)[:, None, :]
    eye = jnp.arange(q_a.shape[0])[:, None] == jnp.arange(q_a.shape[0])[None, :]
    srow = jnp.where(eye[None], NEG, srow)
    mrow, lrow, prow = softmax_side(srow, 2)
    acc_row = jnp.einsum("hst,thd->shd", prow, v_a, preferred_element_type=jnp.float32)
    return (mrow, lrow, acc_row)


def group_parts(item):
    q_a, v_a, q_b, v_b, keep = item
    return jax.vmap(pair_parts)(q_a, v_a, q_b, v_b, keep)


def body(qk, values, bucket, pair_row, pair_col, pair_count, w_out):
    shards = lax.axis_size("seq")
    seq_dev, width = qk.shape
    heads_here = width // HD
    blocks_here = seq_dev // BLOCK
    slots = pair_row.shape[2]
    total_slots = shards * slots
    q_blocks = qk.reshape(blocks_here, BLOCK, heads_here, HD)
    v_blocks = values.reshape(blocks_here, BLOCK, heads_here, HD)
    wanted = lax.all_to_all(pair_col, "seq", split_axis=1, concat_axis=0, tiled=True).reshape(
        total_slots
    )
    sent_q = q_blocks[wanted].reshape(shards, slots, BLOCK, heads_here, HD)
    sent_v = v_blocks[wanted].reshape(shards, slots, BLOCK, heads_here, HD)
    got_q, got_v = (
        lax.all_to_all(sent_q, "seq", split_axis=0, concat_axis=0, tiled=True),
        lax.all_to_all(sent_v, "seq", split_axis=0, concat_axis=0, tiled=True),
    )
    row_index = pair_row.reshape(total_slots)
    seq_id = lax.axis_index("seq")
    head_id = lax.axis_index("head")
    my_buckets = lax.dynamic_slice_in_dim(bucket, head_id * heads_here, heads_here, 1)
    row_glob = seq_id * blocks_here + row_index
    owner = jnp.repeat(jnp.arange(shards, dtype=jnp.int32), slots)
    col_glob = owner * blocks_here + pair_col.reshape(total_slots)
    live = (jnp.arange(slots, dtype=jnp.int32)[None, :] < pair_count[0][:, None]).reshape(
        total_slots
    )
    keep = live[:, None] & (my_buckets[row_glob] == my_buckets[col_glob])
    mine_q = q_blocks[row_index].reshape(shards, slots, BLOCK, heads_here, HD)
    mine_v = v_blocks[row_index].reshape(shards, slots, BLOCK, heads_here, HD)
    row_side, col_side = lax.map(
        group_parts, (mine_q, mine_v, got_q, got_v, keep.reshape(shards, slots, heads_here))
    )
    back_m, back_l, back_acc = lax.all_to_all(
        col_side, "seq", split_axis=0, concat_axis=0, tiled=True
    )
    diag_m, diag_l, diag_acc = jax.vmap(diagonal_parts)(q_blocks, v_blocks)
    index_all = jnp.concatenate([row_index, wanted], axis=0)
    m_all = jnp.concatenate(
        [
            row_side[0].reshape(total_slots, heads_here, BLOCK),
            back_m.reshape(total_slots, heads_here, BLOCK),
        ],
        axis=0,
    )
    l_all = jnp.concatenate(
        [
            row_side[1].reshape(total_slots, heads_here, BLOCK),
            back_l.reshape(total_slots, heads_here, BLOCK),
        ],
        axis=0,
    )
    acc_all = jnp.concatenate(
        [
            row_side[2].reshape(total_slots, BLOCK, heads_here, HD),
            back_acc.reshape(total_slots, BLOCK, heads_here, HD),
        ],
        axis=0,
    )
    onehot = index_all[:, None] == jnp.arange(blocks_here, dtype=jnp.int32)[None, :]
    m_tot = jnp.maximum(
        diag_m, jnp.max(jnp.where(onehot[:, :, None, None], m_all[:, None], NEG), axis=0)
    )
    m_at = jnp.sum(jnp.where(onehot[:, :, None, None], m_tot[None], 0.0), axis=1)
    scale_all = jnp.exp(m_all - m_at)
    onehot_f = onehot.astype(jnp.float32)
    scale_diag = jnp.exp(diag_m - m_tot)
    l_tot = diag_l * scale_diag + jnp.einsum(
        "kb,khs->bhs", onehot_f, l_all * scale_all, precision=lax.Precision.HIGHEST
    )
    weighted = acc_all * jnp.transpose(scale_all, (0, 2, 1))[..., None]
    acc_tot = diag_acc * jnp.transpose(scale_diag, (0, 2, 1))[..., None]
    acc_tot = acc_tot + jnp.einsum(
        "kb,kshd->bshd", onehot_f, weighted, precision=lax.Precision.HIGHEST
    )
    attn = (
        (acc_tot / jnp.transpose(l_tot, (0, 2, 1))[..., None])
        .reshape(seq_dev, width)
        .astype(jnp.bfloat16)
    )
    mixed = lax.all_to_all(attn, "head", split_axis=0, concat_axis=1, tiled=True)
    summed = jnp.dot(
        mixed, lax.all_gather(w_out, "head", axis=0, tiled=True), preferred_element_type=jnp.float32
    )
    return summed.astype(jnp.bfloat16)


def solution(mesh):
    return jax.shard_map(
        body,
        mesh=mesh,
        in_specs=(
            P("seq", "head"),
            P("seq", "head"),
            P(),
            P("seq", None, None),
            P("seq", None, None),
            P("seq", None),
            P("head", None),
        ),
        out_specs=P(("seq", "head"), None),
        check_vma=False,
    )
```

profile of v0, /device:TPU:2, one launch (start us, length us, event | category | flops | bytes accessed | tf_op | source)
XLA Modules:
  0.0 551.0 jit_solution(3559827569345628649)
XLA Ops:
  7.9 4.3 all-to-all-start
  12.2 4.0 reshape.322
  18.3 4.4 gather_fusion.3
  22.7 4.7 all-to-all-start.1
  27.4 4.0 reshape.323
  31.4 3.4 copy.213
  34.8 5.9 %gather_fusion.4 = bf16[24,256,4,128]{3,1,2,0:T(8,128)(2,1)} fusion(bf16[8,256,4,128]{3,1,2,0:T(8,128)(2,1)} %copy.213, s32[1024]{0:T(1024)S(1)} %pad_clamp_fusion), kind=kCustom, calls=%fused_computation.4 | custom fusion | bytes 12583008 | tf_op jit(solution)/shard_map/gather | solution.py:72
  40.8 8.6 %copy.225 = bf16[8,3,256,4,128]{2,4,3,1,0:T(8,128)(2,1)} copy(bf16[8,3,256,4,128]{4,2,3,1,0:T(8,128)(2,1)} %bitcast.132) | data formatting | bytes 12582912 | tf_op jit(solution)/shard_map/reshape | solution.py:72
  49.4 48.2 %all-to-all-done.1 = bf16[8,3,256,4,128]{4,2,3,1,0:T(8,128)(2,1)} async-done(((bf16[8,3,256,4,128]{4,2,3,1,0:T(8,128)(2,1)}), bf16[8,3,256,4,128]{4,2,3,1,0:T(8,128)(2,1)}, u32[]{:S(2)}, u32[]{:S(2)}) %all-to-all-start.1) | async-done | bytes 6291488 | tf_op jit(solution)/shard_map/all_to_all | solution.py:74
  97.6 6.2 %all-to-all-start.2 = ((bf16[8,3,256,4,128]{2,4,3,1,0:T(8,128)(2,1)}), bf16[8,3,256,4,128]{2,4,3,1,0:T(8,128)(2,1)}, u32[]{:S(2)}, u32[]{:S(2)}) async-start(bf16[8,3,256,4,128]{2,4,3,1,0:T(8,128)(2,1)} %copy.225), calls=%async_computation.2 | async-start | bytes 12582912 | tf_op jit(solution)/shard_map/all_to_all | solution.py:75
  104.0 4.4 gather_fusion.2
  108.4 5.9 %gather_fusion.5 = bf16[24,256,4,128]{3,1,2,0:T(8,128)(2,1)} fusion(bf16[8,256,4,128]{3,1,2,0:T(8,128)(2,1)} %copy.213, s32[1024]{0:T(1024)S(1)} %get-tuple-element.203), kind=kCustom, calls=%fused_computation.5 | custom fusion | bytes 12583008 | tf_op jit(solution)/shard_map/gather | solution.py:89
  116.2 57.7 %all-to-all-done.2 = bf16[8,3,256,4,128]{2,4,3,1,0:T(8,128)(2,1)} async-done(((bf16[8,3,256,4,128]{2,4,3,1,0:T(8,128)(2,1)}), bf16[8,3,256,4,128]{2,4,3,1,0:T(8,128)(2,1)}, u32[]{:S(2)}, u32[]{:S(2)}) %all-to-all-start.2) | async-done | bytes 6291488 | tf_op jit(solution)/shard_map/all_to_all | solution.py:75
  173.9 103.8 %while.20 = (s32[]{:T(128)}, f32[8,3,4,256]{3,2,1,0:T(4,128)S(1)}, f32[8,3,4,256]{3,2,1,0:T(4,128)S(1)}, f32[8,3,256,4,128]{2,4,3,1,0:T(8,128)}, f32[8,3,4,256]{...) while((s32[]{:T(128)}, f32[8,3,4,256]{3,2,1,0:T(4,128)S(1)}, ...), condition=%wide.region_9.10_spmd, body=%wide.region_2.9_spmd.sunk | while | flops 619720704 | bytes 20795064 | solution.py:90
  277.7 7.6 %all_to_all.50 = f32[8,3,4,256]{3,2,1,0:T(4,128)S(1)} all-to-all(f32[8,3,4,256]{3,2,1,0:T(4,128)S(1)} %get-tuple-element.73), channel_id=1, replica_groups=mesh['seq'=8,'head'=4] {'seq'}, dimensions={0} | all-to-all | bytes 196608 | tf_op jit(solution)/shard_map/all_to_all | solution.py:93
  285.4 7.6 %all_to_all.51 = f32[8,3,4,256]{3,2,1,0:T(4,128)S(1)} all-to-all(f32[8,3,4,256]{3,2,1,0:T(4,128)S(1)} %get-tuple-element.77), channel_id=1, replica_groups=mesh['seq'=8,'head'=4] {'seq'}, dimensions={0} | all-to-all | bytes 196608 | tf_op jit(solution)/shard_map/all_to_all | solution.py:93
  292.9 6.8 %all-to-all-start.4 = ((f32[8,3,256,4,128]{2,4,3,1,0:T(8,128)}), f32[8,3,256,4,128]{2,4,3,1,0:T(8,128)}, u32[]{:S(2)}, u32[]{:S(2)}) async-start(f32[8,3,256,4,128]{2,4,3,1,0:T(8,128)} %get-tuple-element.75), calls=%async_computation.4 | async-start | bytes 25165824 | tf_op jit(solution)/shard_map/all_to_all | solution.py:93
  314.3 13.2 %copy.230 = f32[24,256,4,128]{3,0,2,1:T(8,128)} copy(f32[24,256,4,128]{1,3,2,0:T(8,128)} %bitcast.134) | data formatting | bytes 25165824 | tf_op jit(solution)/shard_map/reshape | solution.py:114
  329.1 108.3 %all-to-all-done.4 = f32[8,3,256,4,128]{2,4,3,1,0:T(8,128)} async-done(((f32[8,3,256,4,128]{2,4,3,1,0:T(8,128)}), f32[8,3,256,4,128]{2,4,3,1,0:T(8,128)}, u32[]{:S(2)}, u32[]{:S(2)}) %all-to-all-start.4) | async-done | bytes 12582944 | tf_op jit(solution)/shard_map/all_to_all | solution.py:93
  437.3 12.9 %copy.231 = f32[24,256,4,128]{3,0,2,1:T(8,128)} copy(f32[24,256,4,128]{1,3,2,0:T(8,128)} %bitcast.33) | data formatting | bytes 25165824 | tf_op jit(solution)/shard_map/reshape | solution.py:115
  450.3 15.0 %fusion.33 = f32[8,256,4,128]{3,0,2,1:T(8,128)S(1)} fusion(f32[24,256,4,128]{3,0,2,1:T(8,128)} %copy.231, f32[24,256,4,128]{3,0,2,1:T(8,128)} %copy.230, f32[48,256,4]{0,2,1:T(4,128)S(1)} %copy.233, s32[48]{0:T(128)S(1)} %pad_add_fusion), kind=kOutput, calls=%fused_computation.49 | convolution fusion | flops 616563072 | bytes 29556928 | tf_op jit(solution)/shard_map/kb,kshd->bshd/dot_general | solution.py:132
  465.3 9.4 %fusion.44 = bf16[8,256,4,128]{3,1,2,0:T(8,128)(2,1)S(1)} fusion(f32[8,256,4,128]{3,0,2,1:T(8,128)S(1)} %fusion.33, f32[8,256,4]{1,2,0:T(4,128)S(1)} %copy.237, f32[8,256,4]{1,2,0:T(4,128)S(1)} %copy.229, f32[8,4,256,256]{2,3,1,0:T(8,128)} %copy-done.3, f32[8,4,256]{2,1,0:T(4,128)S(1)} %get-tuple-element.201, f32[8,4,256]{2,1,0:T(4,128)S(1)} %copy.210, ...), kind=kOutput, calls=%fused_computation.62 | convolution fusion | flops 549453824 | bytes 16973824 | tf_op jit(solution)/shard_map/vmap(hst,thd->shd)/dot_general | solution.py:50
  478.6 53.3 %all_to_all.52 = bf16[4,512,512]{2,1,0:T(8,128)(2,1)S(1)} all-to-all(bf16[4,512,512]{2,1,0:T(8,128)(2,1)} %convert_element_type.32), channel_id=1, replica_groups=mesh['seq'=8,'head'=4] {'head'}, dimensions={0} | all-to-all | bytes 4194304 | tf_op jit(solution)/shard_map/all_to_all | solution.py:140
  534.2 9.9 %convolution_convert_fusion = bf16[512,2048]{1,0:T(8,128)(2,1)} fusion(bf16[512,2048]{0,1:T(8,128)(2,1)} %bitcast.136, bf16[2048,2048]{1,0:T(8,128)(2,1)} %all-gather.2.cloned.1.call-done), kind=kOutput, calls=%fused_computation.68 | convolution fusion | flops 4296015872 | bytes 12582912 | tf_op jit(solution)/shard_map/dot_general | solution.py:141
  (150 shorter events, 131.3 us)
Async XLA Ops:
  6.5 107.8 %copy-start = (s32[64,16]{0,1:T(8,128)S(1)}, s32[64,16]{0,1:T(8,128)}, u32[]{:S(2)}) copy-start(s32[64,16]{0,1:T(8,128)} %param.11) | copy-start | bytes 12292
  7.9 10.3 %all-to-all-start = ((s32[1,8,3]{2,0,1:T(1,128)}), s32[1,8,3]{2,0,1:T(1,128)S(1)}, u32[]{:S(2)}, u32[]{:S(2)}) async-start(s32[1,8,3]{2,0,1:T(1,128)} %copy.216), calls=%async_computation | async-start | bytes 8192 | tf_op jit(solution)/shard_map/all_to_all | solution.py:68
  22.7 74.8 %all-to-all-start.1 = ((bf16[8,3,256,4,128]{4,2,3,1,0:T(8,128)(2,1)}), bf16[8,3,256,4,128]{4,2,3,1,0:T(8,128)(2,1)}, u32[]{:S(2)}, u32[]{:S(2)}) async-start(bf16[8,3,256,4,128]{4,2,3,1,0:T(8,128)(2,1)} %bitcast.131), calls=%async_computation.1 | async-start | bytes 12582912 | tf_op jit(solution)/shard_map/all_to_all | solution.py:74
  49.4 54.3 %copy-start.5 = (s32[1,8,3]{1,0,2:T(1,128)S(1)}, s32[1,8,3]{1,0,2:T(1,128)}, u32[]{:S(2)}) copy-start(s32[1,8,3]{1,0,2:T(1,128)} %param.13) | copy-start | bytes 292
  49.4 54.4 %copy-start.6 = (s32[1,8,3]{1,0,2:T(1,128)S(1)}, s32[1,8,3]{1,0,2:T(1,128)}, u32[]{:S(2)}) copy-start(s32[1,8,3]{1,0,2:T(1,128)} %param.12) | copy-start | bytes 292
  97.6 76.3 %all-to-all-start.2 = ((bf16[8,3,256,4,128]{2,4,3,1,0:T(8,128)(2,1)}), bf16[8,3,256,4,128]{2,4,3,1,0:T(8,128)(2,1)}, u32[]{:S(2)}, u32[]{:S(2)}) async-start(bf16[8,3,256,4,128]{2,4,3,1,0:T(8,128)(2,1)} %copy.225), calls=%async_computation.2 | async-start | bytes 12582912 | tf_op jit(solution)/shard_map/all_to_all | solution.py:75
  108.4 7.6 %copy-start.7 = (s32[1,8]{1,0:T(1,128)S(1)}, s32[1,8]{1,0:T(1,128)}, u32[]{:S(2)}) copy-start(s32[1,8]{1,0:T(1,128)} %param.14) | copy-start | bytes 100
  292.9 7.6 %copy-start.2 = (bf16[8,256,4,128]{3,2,1,0:T(4,128)(2,1)S(1)}, bf16[8,256,4,128]{3,2,1,0:T(4,128)(2,1)}, u32[]{:S(2)}) copy-start(bf16[8,256,4,128]{3,2,1,0:T(4,128)(2,1)} %reshape.322) | copy-start | bytes 6291460
  292.9 144.4 %all-to-all-start.4 = ((f32[8,3,256,4,128]{2,4,3,1,0:T(8,128)}), f32[8,3,256,4,128]{2,4,3,1,0:T(8,128)}, u32[]{:S(2)}, u32[]{:S(2)}) async-start(f32[8,3,256,4,128]{2,4,3,1,0:T(8,128)} %get-tuple-element.75), calls=%async_computation.4 | async-start | bytes 25165824 | tf_op jit(solution)/shard_map/all_to_all | solution.py:93
  299.8 234.5 %all-gather.2.cloned.1.call-start = ((), (), s32[]{:S(2)}) async-start(), calls=%async_computation.7 | async-start | bytes 10485760 | tf_op jit(solution)/shard_map/all_gather | solution.py:142
  306.8 3.2 copy-start.3
  450.3 15.0 %copy-start.4 = (bf16[8,256,4,128]{3,2,1,0:T(4,128)(2,1)S(1)}, bf16[8,256,4,128]{3,2,1,0:T(4,128)(2,1)}, u32[]{:S(2)}) copy-start(bf16[8,256,4,128]{3,2,1,0:T(4,128)(2,1)} %reshape.323) | copy-start | bytes 6291460
  534.2 9.9 %copy-start.1 = (s32[64,16]{0,1:T(8,128)S(1)}, s32[64,16]{0,1:T(8,128)}, u32[]{:S(2)}) copy-start(s32[64,16]{0,1:T(8,128)} %param.11) | copy-start | bytes 12292
Sparse Core Ops, SparseCore 0:
  302.1 150.7 all-gather.1
where the time goes:
time: 553 us; the launch traced here: 551 us
  waiting for transfers between devices  215 us (39%)
  matrix products  107 us (19%)
  local copies, waits for them, and re-layouts  85.3 us (15%)
  blocking collectives  68.5 us (12%)
  other arithmetic  39.5 us (7%)
  starting transfers between devices  21.9 us (4%)
  between operations  13.6 us (2%)
    all_to_all x1, waiting for transfers between devices, body(): lax.all_to_all(col_side, 'seq', split_axis=0, concat_axis=0, tiled=True)  108 us
    all_to_all x1, waiting for transfers between devices, body(): lax.all_to_all(sent_v, 'seq', split_axis=0, concat_axis=0, tiled=True)  57.7 us
    all_to_all x1, blocking collectives, body(): lax.all_to_all(attn, 'head', split_axis=0, concat_axis=1, tiled=True)  53.3 us
    all_to_all x1, waiting for transfers between devices, body(): lax.all_to_all(sent_q, 'seq', split_axis=0, concat_axis=0, tiled=True)  48.2 us
    dot_general x8, matrix products, pair_parts(): jnp.einsum('hst,shd->thd', pcol, v_a, preferred_element_type=jnp.float32)  25.6 us
    dot_general x8, matrix products, pair_parts(): jnp.einsum('hst,thd->shd', prow, v_b, preferred_element_type=jnp.float32)  25.1 us
    reduce_sum x9, other arithmetic, inverse_norms(): jnp.mean(wide * wide, axis=-1) + 1e-06  20.1 us
    dot_general x8, matrix products, pair_parts(): jnp.einsum('shd,thd->hst', q_a, q_b, preferred_element_type=jnp.float32)  19.9 us
  transfers between devices with their start and end apart: 5, of which 3 were waited for; matrix products, arithmetic and copies ran while one was open for 20% of the time, Pallas kernels for 0%

commit v1 on v0

v1 whole, which is shorter than its diff:
```python
import functools
import math

import jax
import jax.numpy as jnp
from jax import lax
from jax.experimental import pallas as pl
from jax.experimental.pallas import tpu as pltpu
from jax.sharding import PartitionSpec as P

HD = 128
BLOCK = 256
NEG = -1e30
BF16 = jnp.bfloat16
F32 = jnp.float32
SMEM = pl.BlockSpec(memory_space=pltpu.SMEM)
HBM = pl.BlockSpec(memory_space=pl.ANY)


def pack_kernel(q_ref, v_ref, o_ref):
    heads, groups, _, _, rows, _ = o_ref.shape
    for h in range(heads):
        for g in range(groups):
            at = (pl.ds(g * rows, rows), pl.ds(h * HD, HD))
            o_ref[h, g, 0, 0] = q_ref[at]
            o_ref[h, g, 1, 0] = v_ref[at]


def pack(qk, values, spans, groups):
    tokens, width = qk.shape
    heads, span = width // HD, tokens // spans
    rows = span // groups
    block = pl.BlockSpec((span, width), lambda i: (i, 0))
    return pl.pallas_call(
        pack_kernel,
        grid=(spans,),
        in_specs=[block, block],
        out_specs=pl.BlockSpec(
            (heads, groups, 2, 1, rows, HD), lambda i: (0, 0, 0, i, 0, 0)
        ),
        out_shape=jax.ShapeDtypeStruct((heads, groups, 2, spans, rows, HD), BF16),
        cost_estimate=pl.CostEstimate(
            flops=0, bytes_accessed=8 * tokens * width, transcendentals=0
        ),
        name="pack",
    )(qk, values)


def gather_tables(pair_row, pair_col, pair_count, shards):
    mine = jnp.concatenate(
        [pair_row.reshape(-1), pair_col.reshape(-1), pair_count.reshape(-1)]
    )
    have = mine[None]
    me = lax.axis_index("seq")
    step = 1
    while step < shards:
        got = lax.ppermute(have, "seq", [(i, i ^ step) for i in range(shards)])
        low = (me & step) == 0
        have = jnp.concatenate(
            [jnp.where(low, have, got), jnp.where(low, got, have)], axis=0
        )
        step *= 2
    return have.reshape(-1)


def lists_kernel(shards, slots, blocks, cap, tab_ref, bucket_ref, count_ref, list_ref):
    per = shards * slots

    def clear(b, _):
        count_ref[b] = 0
        return 0

    lax.fori_loop(0, shards * blocks, clear, 0)

    def visit(pair, _):
        shard = pair // per
        rest = pair - shard * per
        other = rest // slots
        slot = rest - other * slots
        base = shard * (2 * per + shards)
        a = shard * blocks + tab_ref[base + rest]
        b = other * blocks + tab_ref[base + per + rest]
        live = slot < tab_ref[base + 2 * per + other]

        @pl.when(live & (bucket_ref[a] == bucket_ref[b]))
        def _():
            at = count_ref[a]
            list_ref[a * cap + at] = b
            count_ref[a] = at + 1
            bt = count_ref[b]
            list_ref[b * cap + bt] = a
            count_ref[b] = bt + 1

        return 0

    lax.fori_loop(0, shards * per, visit, 0)


def make_lists(tables, buckets, shards, slots, blocks):
    cap = 2 * shards * slots
    nblk = shards * blocks
    return pl.pallas_call(
        functools.partial(lists_kernel, shards, slots, blocks, cap),
        in_specs=[SMEM, SMEM],
        out_specs=[SMEM, SMEM],
        out_shape=[
            jax.ShapeDtypeStruct((nblk,), jnp.int32),
            jax.ShapeDtypeStruct((nblk * cap,), jnp.int32),
        ],
        name="lists",
    )(tables, buckets)


def attend_kernel(groups, cap, group_ref, count_ref, list_ref, *refs):
    pieces = refs[:groups]
    o_ref, q_ref, v_ref, inv_ref, s_ref, top_ref, sum_ref, acc_ref, sem = refs[groups:]
    units, span, _ = q_ref.shape
    rows = span // groups
    shards, spans = units // pieces[0].shape[2], pieces[0].shape[2]
    blocks_per = span // BLOCK
    me = group_ref[0]

    copies = []
    for r in range(groups):
        piece = lax.rem(me + r, groups)
        for part, ref in enumerate((q_ref, v_ref)):
            for s in range(shards):
                copies.append(
                    pltpu.make_async_copy(
                        pieces[r].at[s, part],
                        ref.at[pl.ds(s * spans, spans), pl.ds(piece * rows, rows), :],
                        sem,
                    )
                )
    for copy in copies:
        copy.start()
    for copy in copies:
        copy.wait()

    def block_at(b):
        unit = b // blocks_per
        return unit, pl.ds(pl.multiple_of((b - unit * blocks_per) * BLOCK, BLOCK), BLOCK)

    ones = jnp.ones((8, HD), BF16)
    contract = (((1,), (1,)), ((), ()))

    def norms(b, _):
        unit, at = block_at(b)
        wide = q_ref[unit, at, :].astype(F32)
        square = wide * wide
        high = square.astype(BF16)
        low = (square - high.astype(F32)).astype(BF16)
        total = lax.dot_general(ones, high, contract, preferred_element_type=F32)
        total += lax.dot_general(ones, low, contract, preferred_element_type=F32)
        scale = math.log2(math.e) / math.sqrt(HD)
        inv_ref[b] = lax.rsqrt(total * (1.0 / HD) + 1e-06) * scale
        return 0

    lax.fori_loop(0, units * blocks_per, norms, 0)

    def unit_body(unit, _):
        query = q_ref[unit, pl.ds(pl.multiple_of(me * rows, rows), rows), :]
        offset = unit * span + me * rows
        own = offset // BLOCK
        n = count_ref[own]

        def scores(b):
            u, at = block_at(b)
            gram = lax.dot_general(
                query, q_ref[u, at, :], contract, preferred_element_type=F32
            )
            return gram * inv_ref[b, 0:1, :]

        shape = (rows, BLOCK)
        diagonal = lax.broadcasted_iota(jnp.int32, shape, 1) == (
            lax.broadcasted_iota(jnp.int32, shape, 0) + (offset - own * BLOCK)
        )
        first = jnp.where(diagonal, NEG, scores(own))
        s_ref[0] = first
        top_ref[...] = jnp.maximum(first[:, :HD], first[:, HD:])

        def score_step(j, _):
            now = scores(list_ref[own * cap + j])
            s_ref[j + 1] = now
            top_ref[...] = jnp.maximum(
                top_ref[...], jnp.maximum(now[:, :HD], now[:, HD:])
            )
            return 0

        lax.fori_loop(0, n, score_step, 0)
        top_ref[...] = jnp.broadcast_to(
            jnp.max(top_ref[...], axis=1, keepdims=True), (rows, HD)
        )

        def weigh(j, b):
            u, at = block_at(b)
            top = top_ref[...]
            left = jnp.exp2(s_ref[j, :, 0:HD] - top)
            right = jnp.exp2(s_ref[j, :, HD : 2 * HD] - top)
            probs = jnp.concatenate([left.astype(BF16), right.astype(BF16)], axis=1)
            return left + right, jnp.dot(
                probs, v_ref[u, at, :], preferred_element_type=F32
            )

        total, acc = weigh(0, own)
        sum_ref[...] = total
        acc_ref[...] = acc

        def weigh_step(j, _):
            total, acc = weigh(j + 1, list_ref[own * cap + j])
            sum_ref[...] += total
            acc_ref[...] += acc
            return 0

        lax.fori_loop(0, n, weigh_step, 0)
        total = jnp.sum(sum_ref[...], axis=1, keepdims=True)
        o_ref[unit] = (acc_ref[...] / total).astype(BF16)
        return 0

    lax.fori_loop(0, units, unit_body, 0)


def attend(group, counts, lists, pieces, cap):
    groups = len(pieces)
    shards, _, spans, rows, _ = pieces[0].shape
    units, span = shards * spans, rows * groups
    nblk = units * span // BLOCK
    jobs = 3 * nblk
    return pl.pallas_call(
        functools.partial(attend_kernel, groups, cap),
        in_specs=[SMEM, SMEM, SMEM] + [HBM] * groups,
        out_specs=pl.BlockSpec(memory_space=pltpu.VMEM),
        out_shape=jax.ShapeDtypeStruct((units, rows, HD), BF16),
        scratch_shapes=[
            pltpu.VMEM((units, span, HD), BF16),
            pltpu.VMEM((units, span, HD), BF16),
            pltpu.VMEM((nblk, 8, BLOCK), F32),
            pltpu.VMEM((cap + 1, rows, BLOCK), F32),
            pltpu.VMEM((rows, HD), F32),
            pltpu.VMEM((rows, HD), F32),
            pltpu.VMEM((rows, HD), F32),
            pltpu.SemaphoreType.DMA,
        ],
        cost_estimate=pl.CostEstimate(
            flops=4 * jobs * rows * BLOCK * HD,
            bytes_accessed=4 * units * span * HD,
            transcendentals=jobs * rows * BLOCK,
        ),
        name="attend",
    )(group, counts, lists, *pieces)


def group_shift(x, shards, groups, r):
    pairs = [
        (i - i % groups + (i % groups + r) % groups, i) for i in range(shards)
    ]
    return lax.ppermute(x, "seq", pairs)


def gather_weights(w_out, shards, groups, member):
    count = lax.axis_size("head")
    here = lax.axis_index("head")
    share = w_out.shape[0] // groups
    take = lambda k: lax.dynamic_slice_in_dim(
        w_out, lax.rem(member + k, groups) * share, share, 0
    )
    mine = take(0)
    ups, downs = {}, {}
    up = down = mine
    for k in range(1, count):
        up = lax.ppermute(up, "head", [(i, i + 1) for i in range(k - 1, count - 1)])
        down = lax.ppermute(down, "head", [(i, i - 1) for i in range(1, count - k + 1)])
        ups[k], downs[k] = up, down
    out = [[take(k) for k in range(groups)]]
    for r in range(1, count):
        piece = jnp.where(here + r < count, downs[r], ups[count - r])
        out.append(
            [piece] + [group_shift(piece, shards, groups, k) for k in range(1, groups)]
        )
    return out


def body(qk, values, bucket, pair_row, pair_col, pair_count, w_out):
    shards = lax.axis_size("seq")
    spans = lax.axis_size("head")
    tokens, width = qk.shape
    heads = width // HD
    groups = shards // heads
    blocks = tokens // BLOCK
    slots = pair_row.shape[2]
    here, z = lax.axis_index("seq"), lax.axis_index("head")
    head, member = here // groups, lax.rem(here, groups)

    sent = pack(qk, values, spans, groups)
    rows = sent.shape[4]
    got = lax.all_to_all(
        sent.reshape(shards, 2, spans, rows, HD), "seq", 0, 0, tiled=True
    )
    pieces = [got] + [group_shift(got, shards, groups, r) for r in range(1, groups)]

    tables = gather_tables(pair_row, pair_col, pair_count, shards)
    buckets = lax.dynamic_slice_in_dim(bucket, z * heads + head, 1, 1).reshape(-1)
    counts, lists = make_lists(tables, buckets, shards, slots, blocks)

    attn = attend(
        member.reshape(1).astype(jnp.int32), counts, lists, pieces, 2 * shards * slots
    )
    weights = gather_weights(w_out, shards, groups, member)

    mixed = lax.all_to_all(attn, ("seq", "head"), 0, 0, tiled=True)
    mixed = mixed.reshape(heads, groups, spans, rows, HD)
    share = w_out.shape[0] // groups
    ordered = jnp.transpose(mixed, (2, 1, 3, 0, 4)).reshape(
        spans, groups * rows, groups, share
    )
    order_z = lax.rem(z + jnp.arange(spans), spans)
    order_g = lax.rem(member + jnp.arange(groups), groups)
    ordered = ordered[order_z][:, :, order_g]
    full = jnp.stack([jnp.stack(pieces_r) for pieces_r in weights])
    summed = jnp.einsum("zrgf,zgfn->rn", ordered, full, preferred_element_type=F32)
    return summed.astype(BF16)


def solution(mesh):
    return jax.shard_map(
        body,
        mesh=mesh,
        in_specs=(
            P("seq", "head"),
            P("seq", "head"),
            P(),
            P("seq", None, None),
            P("seq", None, None),
            P("seq", None),
            P("head", None),
        ),
        out_specs=P(("seq", "head"), None),
        check_vma=False,
    )
```

time: 553 us -> 289 us (0.52)
  waiting for transfers between devices: 215 us -> 96.1 us
  matrix products: 107 us -> 8.6 us
  Pallas kernels: 0 us -> 68.8 us
  local copies, waits for them, and re-layouts: 85.3 us -> 20.6 us
  other arithmetic: 39.5 us -> 10.5 us
  blocking collectives: 68.5 us -> 52.1 us
  between operations: 13.6 us -> 0.19 us
  starting transfers between devices: 21.9 us -> 28 us
    all_to_all x4 -> x1, waiting for transfers between devices: 214 us -> 0.01 us  [body(): mixed = lax.all_to_all(attn, ('seq', 'head'), 0, 0, tiled=True)]
    dot_general x29 -> x1, matrix products: 107 us -> 8.6 us  [body(): jnp.einsum('zrgf,zgfn->rn', ordered, full, preferred_element_type=F32)]
    ppermute x0 -> x13, waiting for transfers between devices: none -> 96.1 us  [the longest x3 88.3 us: gather_weights(): lax.ppermute(down, 'head', [(i, i - 1) for i in range(1, count - k + 1)])]
    pallas_call x0 -> x3, Pallas kernels: none -> 68.8 us  [the longest x1 54.7 us: attend(): pl.pallas_call(functools.partial(attend_kernel, groups, cap), in_specs=[S...]
    reshape x13 -> x7, local copies, waits for them, and re-layouts: 51 us -> 12.4 us  [the longest x2 7.23 us: body(): jnp.transpose(mixed, (2, 1, 3, 0, 4))]
    reduce_sum x19 -> x0, other arithmetic: 37.2 us -> none  [the longest x9 20.1 us: inverse_norms(): jnp.mean(wide * wide, axis=-1) + 1e-06]
    all_to_all x3 -> x1, blocking collectives: 68.5 us -> 52.1 us  [body(): lax.all_to_all(sent.reshape(shards, 2, spans, rows, HD), 'seq', 0, 0, til...]
    ppermute x0 -> x13, starting transfers between devices: none -> 15.3 us  [the longest x3 8.43 us: gather_weights(): up = lax.ppermute(up, 'head', [(i, i + 1) for i in range(k - 1, count - 1)])]
  transfers between devices with their start and end apart: 5 -> 14, of which waited for: 3 -> 6; matrix products, arithmetic and copies ran while one was open for 20% -> 5% of each run, Pallas kernels for 0% -> 22%
where the time goes in v1:
time: 289 us; the launch traced here: 285 us
  waiting for transfers between devices  96.1 us (33%)
  Pallas kernels  68.8 us (24%)
  blocking collectives  52.1 us (18%)
  starting transfers between devices  28 us (10%)
  local copies, waits for them, and re-layouts  20.6 us (7%)
  other arithmetic  10.5 us (4%)
  matrix products  8.6 us (3%)
    ppermute x3, waiting for transfers between devices, gather_weights(): lax.ppermute(down, 'head', [(i, i - 1) for i in range(1, count - k + 1)])  88.3 us
    pallas_call x1, Pallas kernels, attend(): pl.pallas_call(functools.partial(attend_kernel, groups, cap), in_specs=[S...  54.7 us
    all_to_all x1, blocking collectives, body(): lax.all_to_all(sent.reshape(shards, 2, spans, rows, HD), 'seq', 0, 0, til...  52.1 us
    all_to_all x1, starting transfers between devices, body(): mixed = lax.all_to_all(attn, ('seq', 'head'), 0, 0, tiled=True)  12.6 us
    pallas_call x1, Pallas kernels, make_lists(): pl.pallas_call(functools.partial(lists_kernel, shards, slots, blocks, cap...  9.19 us
    dot_general x1, matrix products, body(): jnp.einsum('zrgf,zgfn->rn', ordered, full, preferred_element_type=F32)  8.6 us
    ppermute x3, starting transfers between devices, gather_weights(): up = lax.ppermute(up, 'head', [(i, i + 1) for i in range(k - 1, count - 1)])  8.43 us
    another operation x4, other arithmetic, body(): full = jnp.stack([jnp.stack(pieces_r) for pieces_r in weights])  7.32 us
  transfers between devices with their start and end apart: 14, of which 6 were waited for; matrix products, arithmetic and copies ran while one was open for 5% of the time, Pallas kernels for 22%

profile of v1, /device:TPU:2, one launch (start us, length us, event | category | flops | bytes accessed | tf_op | source)
XLA Modules:
  0.0 284.8 jit_solution(4102163923011046492)
XLA Ops:
  0.0 4.9 %pack.1 = bf16[4,2,2,4,256,128]{5,4,3,2,1,0:T(8,128)(2,1)} custom-call(bf16[2048,512]{1,0:T(8,128)(2,1)} %q_ref.1, bf16[2048,512]{1,0:T(8,128)(2,1)} %v_ref.1), custom_call_target="tpu_custom_call" | custom-call | bytes 8388608 | tf_op jit(solution)/shard_map/pack/pallas_call | solution.py:34
  4.9 52.1 %all_to_all.10.refs_0_ = bf16[8,2,4,256,128]{4,3,2,1,0:T(8,128)(2,1)} all-to-all(bf16[8,2,4,256,128]{4,3,2,1,0:T(8,128)(2,1)} %bitcast.45), channel_id=1, replica_groups=mesh['seq'=8,'head'=4] {'seq'}, dimensions={0} | all-to-all | bytes 8388608 | tf_op jit(solution)/shard_map/all_to_all | solution.py:296
  58.2 5.1 %collective-permute-start.5 = (bf16[256,2048]{1,0:T(8,128)(2,1)}, bf16[256,2048]{1,0:T(8,128)(2,1)}, u32[]{:S(2)}, u32[]{:S(2)}) collective-permute-start(bf16[256,2048]{1,0:T(8,128)(2,1)} %get-tuple-element.10), channel_id=1, source_target_pairs={{0,1},{1,2},{2,3},{4,5},{5,6},{6,7},{8,9},{9,10},{10,11},{12,13},{... | collective-permute-start | bytes 3145736 | tf_op jit(solution)/shard_map/ppermute | solution.py:271
  66.3 1.5 collective-permute-start.1
  67.8 2.1 collective-permute-done.1
  71.1 2.5 collective-permute-done.2
  74.3 9.2 %lists.1 = (s32[64]{0:T(128)}, s32[3072]{0:T(1024)}) custom-call(s32[448]{0:T(512)} %reshape.99.tab_ref, s32[64]{0:T(128)} %fusion.11.bucket_ref), custom_call_target="tpu_custom_call" | custom-call | tf_op jit(solution)/shard_map/lists/pallas_call | solution.py:102
  83.5 2.2 collective-permute-done.5
  85.7 1.7 collective-permute-start.6
  87.4 54.7 %attend.1 = bf16[32,256,128]{2,1,0:T(8,128)(2,1)} custom-call(s32[1]{0:T(128)} %bitcast.group_ref, s32[64]{0:T(128)} %get-tuple-element.7.count_ref, s32[3072]{0:T(1024)} %get-tuple-element.8.list_ref, bf16[8,2,4,256,128]{4,3,2,1,0:T(8,128)(2,1)} %all_to_all.10.refs_0_, bf16[8,2,4,256,128]{4,3,2,1,0:T(8,128)(2,1)} %collective-permute-done.3.refs_1_), custom_call_target="tpu_custom_call" | custom-call | flops 6442450944 | bytes 8388608 | tf_op jit(solution)/shard_map/attend/pallas_call | solution.py:229
  142.1 12.6 %all-to-all-start.1 = ((bf16[32,256,128]{2,1,0:T(8,128)(2,1)}), bf16[32,256,128]{2,1,0:T(8,128)(2,1)S(1)}, u32[]{:S(2)}, u32[]{:S(2)}) async-start(bf16[32,256,128]{2,1,0:T(8,128)(2,1)} %attend.1), calls=%async_computation.1 | async-start | bytes 4194304 | tf_op jit(solution)/shard_map/all_to_all | solution.py:310
  156.1 1.6 collective-permute-start.7
  157.7 55.9 %collective-permute-done.9 = bf16[256,2048]{1,0:T(8,128)(2,1)} collective-permute-done((bf16[256,2048]{1,0:T(8,128)(2,1)}, bf16[256,2048]{1,0:T(8,128)(2,1)}, u32[]{:S(2)}, u32[]{:S(2)}) %collective-permute-start.9) | collective-permute-done | bytes 1048608 | tf_op jit(solution)/shard_map/ppermute | solution.py:272
  218.2 32.4 %collective-permute-done.11 = bf16[256,2048]{1,0:T(8,128)(2,1)S(1)} collective-permute-done((bf16[256,2048]{1,0:T(8,128)(2,1)}, bf16[256,2048]{1,0:T(8,128)(2,1)S(1)}, u32[]{:S(2)}, u32[]{:S(2)}) %collective-permute-start.11) | collective-permute-done | bytes 1048608 | tf_op jit(solution)/shard_map/ppermute | solution.py:272
  251.0 2.8 maximum_bitcast_fusion
  253.7 1.5 maximum_bitcast_fusion.2
  255.2 1.6 maximum_bitcast_fusion.1
  258.3 3.8 %copy.20 = bf16[4,2,4,256,128]{3,1,4,0,2:T(2,128)(2,1)} copy(bf16[4,2,4,256,128]{4,3,2,1,0:T(8,128)(2,1)S(1)} %bitcast.46) | data formatting | bytes 4194304 | tf_op jit(solution)/shard_map/reshape | solution.py:311
  262.1 4.5 %reshape.103 = bf16[4,512,2,256]{1,3,2,0:T(8,128)(2,1)} reshape(bf16[4,2,256,4,128]{2,1,4,3,0:T(2,128)(2,1)} %bitcast.47) | data formatting | bytes 4194304 | tf_op jit(solution)/shard_map/reshape | solution.py:313
  266.5 2.8 copy.21
  269.3 2.0 gather_fusion
  271.3 2.8 copy.22
  274.1 2.1 gather_fusion.1
  276.2 8.6 %bitcast_convert_fusion = bf16[512,2048]{1,0:T(8,128)(2,1)} fusion(bf16[1,2,256,2048]{3,2,0,1:T(8,128)(2,1)} %maximum_bitcast_fusion.3, bf16[1,2,256,2048]{3,2,0,1:T(8,128)(2,1)} %maximum_bitcast_fusion.2, bf16[1,2,256,2048]{3,2,0,1:T(8,128)(2,1)} %maximum_bitcast_fusion.1, bf16[1,2,256,2048]{3,2,0,1:T(8,128)(2,1)} %maximum_bitcast_fusion, ...), kind=kOutput, calls=%fused_computation.10 | convolution fusion | flops 4308598784 | bytes 12582912 | tf_op jit(solution)/shard_map/zrgf,zgfn->rn/dot_general | solution.py:320
  (50 shorter events, 13.7 us)
Async XLA Ops:
  0.0 70.6 %copy-start = (s32[64,16]{0,1:T(8,128)S(1)}, s32[64,16]{0,1:T(8,128)}, u32[]{:S(2)}) copy-start(s32[64,16]{0,1:T(8,128)} %param.9) | copy-start | bytes 12292
  4.9 52.1 %copy-start.1 = (bf16[512,2048]{1,0:T(8,128)(2,1)S(1)}, bf16[512,2048]{1,0:T(8,128)(2,1)}, u32[]{:S(2)}) copy-start(bf16[512,2048]{1,0:T(8,128)(2,1)} %param.13) | copy-start | bytes 6291460
  57.0 30.4 %collective-permute-start.3 = (bf16[8,2,4,256,128]{4,3,2,1,0:T(8,128)(2,1)}, bf16[8,2,4,256,128]{4,3,2,1,0:T(8,128)(2,1)}, u32[]{:S(2)}, u32[]{:S(2)}) collective-permute-start(bf16[8,2,4,256,128]{4,3,2,1,0:T(8,128)(2,1)} %all_to_all.10.refs_0_), channel_id=1, source_target_pairs={{4,0},{0,4},{12,8},{8,12},{20,16},{16,20},{28,24},{24,28},{5,1},{1... | collective-permute-start | bytes 12582920 | tf_op jit(solution)/shard_map/ppermute | solution.py:257
  57.0 7.6 %copy-start.3 = (s32[1,8,3]{1,0,2:T(1,128)S(1)}, s32[1,8,3]{1,0,2:T(1,128)}, u32[]{:S(2)}) copy-start(s32[1,8,3]{1,0,2:T(1,128)} %param.10) | copy-start | bytes 292
  57.0 7.8 %copy-start.4 = (s32[1,8,3]{1,0,2:T(1,128)S(1)}, s32[1,8,3]{1,0,2:T(1,128)}, u32[]{:S(2)}) copy-start(s32[1,8,3]{1,0,2:T(1,128)} %param.11) | copy-start | bytes 292
  57.0 8.0 %copy-start.2 = (s32[1,8]{1,0:T(1,128)S(1)}, s32[1,8]{1,0:T(1,128)}, u32[]{:S(2)}) copy-start(s32[1,8]{1,0:T(1,128)} %param.12) | copy-start | bytes 100
  58.2 27.5 %collective-permute-start.5 = (bf16[256,2048]{1,0:T(8,128)(2,1)}, bf16[256,2048]{1,0:T(8,128)(2,1)}, u32[]{:S(2)}, u32[]{:S(2)}) collective-permute-start(bf16[256,2048]{1,0:T(8,128)(2,1)} %get-tuple-element.10), channel_id=1, source_target_pairs={{0,1},{1,2},{2,3},{4,5},{5,6},{6,7},{8,9},{9,10},{10,11},{12,13},{... | collective-permute-start | bytes 3145736 | tf_op jit(solution)/shard_map/ppermute | solution.py:271
  63.3 91.4 %collective-permute-start.4 = (bf16[256,2048]{1,0:T(8,128)(2,1)}, bf16[256,2048]{1,0:T(8,128)(2,1)}, u32[]{:S(2)}, u32[]{:S(2)}) collective-permute-start(bf16[256,2048]{1,0:T(8,128)(2,1)} %get-tuple-element.10), channel_id=1, source_target_pairs={{1,0},{2,1},{3,2},{5,4},{6,5},{7,6},{9,8},{10,9},{11,10},{13,12},{... | collective-permute-start | bytes 3145736 | tf_op jit(solution)/shard_map/ppermute | solution.py:272
  65.0 1.2 collective-permute-start
  66.3 3.6 %collective-permute-start.1 = (s32[2,56]{1,0:T(2,128)S(1)}, s32[2,56]{1,0:T(2,128)S(1)}, u32[]{:S(2)}, u32[]{:S(2)}) collective-permute-start(s32[2,56]{1,0:T(2,128)S(1)} %pad_add_fusion.2), channel_id=1, source_target_pairs={{0,8},{4,12},{8,0},{12,4},{16,24},{20,28},{24,16},{28,20},{1,9},{5... | collective-permute-start | bytes 1352 | tf_op jit(solution)/shard_map/ppermute | solution.py:57
  70.0 3.7 %collective-permute-start.2 = (s32[4,56]{1,0:T(4,128)S(1)}, s32[4,56]{1,0:T(4,128)S(1)}, u32[]{:S(2)}, u32[]{:S(2)}) collective-permute-start(s32[4,56]{1,0:T(4,128)S(1)} %pad_add_fusion.1), channel_id=1, source_target_pairs={{0,16},{4,20},{8,24},{12,28},{16,0},{20,4},{24,8},{28,12},{1,17},{... | collective-permute-start | bytes 2696 | tf_op jit(solution)/shard_map/ppermute | solution.py:57
  85.7 70.4 %collective-permute-start.6 = (bf16[256,2048]{1,0:T(8,128)(2,1)}, bf16[256,2048]{1,0:T(8,128)(2,1)}, u32[]{:S(2)}, u32[]{:S(2)}) collective-permute-start(bf16[256,2048]{1,0:T(8,128)(2,1)} %collective-permute-done.5), channel_id=1, source_target_pairs={{1,2},{2,3},{5,6},{6,7},{9,10},{10,11},{13,14},{14,15},{17,18},{18... | collective-permute-start | bytes 3145736 | tf_op jit(solution)/shard_map/ppermute | solution.py:271
  142.1 116.2 %all-to-all-start.1 = ((bf16[32,256,128]{2,1,0:T(8,128)(2,1)}), bf16[32,256,128]{2,1,0:T(8,128)(2,1)S(1)}, u32[]{:S(2)}, u32[]{:S(2)}) async-start(bf16[32,256,128]{2,1,0:T(8,128)(2,1)} %attend.1), calls=%async_computation.1 | async-start | bytes 4194304 | tf_op jit(solution)/shard_map/all_to_all | solution.py:310
  154.8 58.8 %collective-permute-start.9 = (bf16[256,2048]{1,0:T(8,128)(2,1)}, bf16[256,2048]{1,0:T(8,128)(2,1)}, u32[]{:S(2)}, u32[]{:S(2)}) collective-permute-start(bf16[256,2048]{1,0:T(8,128)(2,1)} %collective-permute-done.4), channel_id=1, source_target_pairs={{1,0},{2,1},{5,4},{6,5},{9,8},{10,9},{13,12},{14,13},{17,16},{18,1... | collective-permute-start | bytes 3145736 | tf_op jit(solution)/shard_map/ppermute | solution.py:272
  156.1 60.3 %collective-permute-start.7 = (bf16[256,2048]{1,0:T(8,128)(2,1)}, bf16[256,2048]{1,0:T(8,128)(2,1)}, u32[]{:S(2)}, u32[]{:S(2)}) collective-permute-start(bf16[256,2048]{1,0:T(8,128)(2,1)} %collective-permute-done.6), channel_id=1, source_target_pairs={{2,3},{6,7},{10,11},{14,15},{18,19},{22,23},{26,27},{30,31}} | collective-permute-start | bytes 3145736 | tf_op jit(solution)/shard_map/ppermute | solution.py:271
  213.6 37.0 %collective-permute-start.11 = (bf16[256,2048]{1,0:T(8,128)(2,1)}, bf16[256,2048]{1,0:T(8,128)(2,1)S(1)}, u32[]{:S(2)}, u32[]{:S(2)}) collective-permute-start(bf16[256,2048]{1,0:T(8,128)(2,1)} %collective-permute-done.9), channel_id=1, source_target_pairs={{1,0},{5,4},{9,8},{13,12},{17,16},{21,20},{25,24},{29,28}} | collective-permute-start | bytes 3145736 | tf_op jit(solution)/shard_map/ppermute | solution.py:272
  216.3 37.5 %collective-permute-start.10 = (bf16[256,2048]{1,0:T(8,128)(2,1)S(1)}, bf16[256,2048]{1,0:T(8,128)(2,1)S(1)}, u32[]{:S(2)}, u32[]{:S(2)}) collective-permute-start(bf16[256,2048]{1,0:T(8,128)(2,1)S(1)} %broadcast_select_fusion.1), channel_id=1, source_target_pairs={{4,0},{0,4},{12,8},{8,12},{20,16},{16,20},{28,24},{24,28},{5,1},{1... | collective-permute-start | bytes 3145736 | tf_op jit(solution)/shard_map/ppermute | solution.py:257
  217.7 37.6 %collective-permute-start.8 = (bf16[256,2048]{1,0:T(8,128)(2,1)S(1)}, bf16[256,2048]{1,0:T(8,128)(2,1)S(1)}, u32[]{:S(2)}, u32[]{:S(2)}) collective-permute-start(bf16[256,2048]{1,0:T(8,128)(2,1)S(1)} %broadcast_select_fusion.2), channel_id=1, source_target_pairs={{4,0},{0,4},{12,8},{8,12},{20,16},{16,20},{28,24},{24,28},{5,1},{1... | collective-permute-start | bytes 3145736 | tf_op jit(solution)/shard_map/ppermute | solution.py:257
  250.9 5.9 %collective-permute-start.12 = (bf16[256,2048]{1,0:T(8,128)(2,1)S(1)}, bf16[256,2048]{1,0:T(8,128)(2,1)S(1)}, u32[]{:S(2)}, u32[]{:S(2)}) collective-permute-start(bf16[256,2048]{1,0:T(8,128)(2,1)S(1)} %broadcast_select_fusion), channel_id=1, source_target_pairs={{4,0},{0,4},{12,8},{8,12},{20,16},{16,20},{28,24},{24,28},{5,1},{1... | collective-permute-start | bytes 3145736 | tf_op jit(solution)/shard_map/ppermute | solution.py:257

commit v2 on v1

v2 whole, which is shorter than its diff:
```python
import functools
import math

import jax
import jax.numpy as jnp
from jax import lax
from jax.experimental import pallas as pl
from jax.experimental.pallas import tpu as pltpu
from jax.sharding import PartitionSpec as P


HD = 128
BLOCK = 256
NEG = -1e30
LEAD, TAIL = 2, 6
PREP_STEP = 4
BF16 = jnp.bfloat16
F32 = jnp.float32
SMEM = pl.BlockSpec(memory_space=pltpu.SMEM)
HBM = pl.BlockSpec(memory_space=pl.ANY)


def pack_kernel(q_ref, v_ref, o_ref):
    heads, groups, _, _, rows, _ = o_ref.shape
    for h in range(heads):
        for g in range(groups):
            at = (pl.ds(g * rows, rows), pl.ds(h * HD, HD))
            o_ref[h, g, 0, 0] = q_ref[at]
            o_ref[h, g, 1, 0] = v_ref[at]


def pack(qk, values, spans, groups):
    tokens, width = qk.shape
    heads, span = width // HD, tokens // spans
    rows = span // groups
    block = pl.BlockSpec((span, width), lambda i: (i, 0))
    return pl.pallas_call(
        pack_kernel,
        grid=(spans,),
        in_specs=[block, block],
        out_specs=pl.BlockSpec(
            (heads, groups, 2, 1, rows, HD), lambda i: (0, 0, 0, i, 0, 0)
        ),
        out_shape=jax.ShapeDtypeStruct((heads, groups, 2, spans, rows, HD), BF16),
        cost_estimate=pl.CostEstimate(
            flops=0, bytes_accessed=8 * tokens * width, transcendentals=0
        ),
        name="pack",
    )(qk, values)


def gather_tables(pair_row, pair_col, pair_count, shards):
    mine = jnp.concatenate(
        [pair_row.reshape(-1), pair_col.reshape(-1), pair_count.reshape(-1)]
    )
    rest = [
        lax.ppermute(mine, "seq", [((i + r) % shards, i) for i in range(shards)])
        for r in range(1, shards)
    ]
    return jnp.concatenate([mine] + rest)


def job_lists(tables, buckets, spot, shards, slots, blocks, units, span, rows):
    nblk = shards * blocks
    cap = 2 * shards * slots
    limit = job_limit(units, shards, slots)

    def kernel(tab_ref, bucket_ref, spot_ref, count_ref, unit_ref, key_ref, fill, lists):
        def clear(b, _):
            fill[b] = 0
            return 0

        lax.fori_loop(0, nblk, clear, 0)
        per = shards * slots

        def visit(pair, _):
            shard = pair // per
            rest = pair - shard * per
            other = rest // slots
            slot = rest - other * slots
            base = lax.rem(shard + shards - spot_ref[2], shards) * (2 * per + shards)
            a = shard * blocks + tab_ref[base + rest]
            b = other * blocks + tab_ref[base + per + rest]
            live = slot < tab_ref[base + 2 * per + other]

            @pl.when(live & (bucket_ref[a] == bucket_ref[b]))
            def _():
                at = fill[a]
                lists[a * cap + at] = b
                fill[a] = at + 1
                bt = fill[b]
                lists[b * cap + bt] = a
                fill[b] = bt + 1

            return 0

        lax.fori_loop(0, shards * per, visit, 0)

        for i in range(LEAD):
            unit_ref[i] = units
            key_ref[i] = 0

        def per_unit(unit, at):
            own = (unit * span + spot_ref[0] * rows) // BLOCK
            unit_ref[at] = unit
            key_ref[at] = own
            n = fill[own]

            def partner(j, _):
                unit_ref[at + 1 + j] = unit
                key_ref[at + 1 + j] = lists[own * cap + j]
                return 0

            lax.fori_loop(0, n, partner, 0)
            return at + 1 + n

        end = lax.fori_loop(0, units, per_unit, LEAD)
        for i in range(TAIL):
            unit_ref[end + i] = units
            key_ref[end + i] = 0
        count_ref[0] = end - LEAD

    return pl.pallas_call(
        kernel,
        in_specs=[SMEM, SMEM, SMEM],
        out_specs=[SMEM, SMEM, SMEM],
        out_shape=[
            jax.ShapeDtypeStruct((1,), jnp.int32),
            jax.ShapeDtypeStruct((limit,), jnp.int32),
            jax.ShapeDtypeStruct((limit,), jnp.int32),
        ],
        scratch_shapes=[
            pltpu.SMEM((nblk,), jnp.int32),
            pltpu.SMEM((nblk * cap,), jnp.int32),
        ],
        cost_estimate=pl.CostEstimate(
            flops=0, bytes_accessed=32 * 1024 * 1024, transcendentals=0
        ),
        name="job_lists",
    )(tables, buckets, spot)


def job_limit(units, shards, slots):
    return units + 2 * shards * shards * slots + LEAD + TAIL


def attend_kernel(groups, spot_ref, count_ref, unit_ref, key_ref, *refs):
    pieces = refs[:groups]
    o_ref, q_ref, v_ref, vt_ref, inv_ref, s0, s1, x0, x1, p0, p1, a0, a1 = refs[
        groups : groups + 13
    ]
    top_ref, sum_ref, acc_ref, q_sem, v_sem = refs[groups + 13 :]
    units, span, _ = q_ref.shape
    rows = span // groups
    spans = pieces[0].shape[2]
    shards = units // spans
    blocks_per = span // BLOCK
    me = spot_ref[0]
    lanes = [slice(k, min(k + HD, rows)) for k in range(0, rows, HD)]

    copies = ([], [])
    for r in range(groups):
        piece = lax.rem(me + r, groups)
        for part, ref, sem in ((0, q_ref, q_sem), (1, v_ref, v_sem)):
            for s in range(shards):
                copies[part].append(
                    pltpu.make_async_copy(
                        pieces[r].at[s, part],
                        ref.at[pl.ds(s * spans, spans), pl.ds(piece * rows, rows), :],
                        sem,
                    )
                )
    for part in copies:
        for copy in part:
            copy.start()

    def clear(unit, _):
        sum_ref[unit] = jnp.zeros(sum_ref.shape[1:], F32)
        acc_ref[unit] = jnp.zeros(acc_ref.shape[1:], F32)
        return 0

    lax.fori_loop(0, units + 1, clear, 0)
    for part in copies:
        for copy in part:
            copy.wait()

    def block_at(b):
        if blocks_per == 1:
            return b, slice(None)
        unit = b // blocks_per
        return unit, pl.ds(pl.multiple_of((b - unit * blocks_per) * BLOCK, BLOCK), BLOCK)

    ones = jnp.ones((HD, HD), BF16)
    contract = (((1,), (1,)), ((), ()))

    def prepare(i, _):
        for k in range(PREP_STEP):
            b = i * PREP_STEP + k
            unit, at = block_at(b)
            wide = q_ref[unit, at, :].astype(F32)
            square = wide * wide
            high = square.astype(BF16)
            low = (square - high.astype(F32)).astype(BF16)
            total = jnp.dot(high, ones, preferred_element_type=F32)
            total += jnp.dot(low, ones, preferred_element_type=F32)
            scale = math.log2(math.e) / math.sqrt(HD)
            inv_ref[b] = lax.rsqrt(total * (1.0 / HD) + 1e-06) * scale
            vt_ref[b] = v_ref[unit, at, :].T
        return 0

    lax.fori_loop(0, units * blocks_per // PREP_STEP, prepare, 0)

    def tiles(x):
        return x.reshape(x.shape[0] // 8, 8, x.shape[1])

    def score(t, s_ref, x_ref):
        unit, key = jnp.minimum(unit_ref[t], units - 1), key_ref[t]
        first = unit_ref[t - 1] != unit_ref[t]
        query = q_ref[unit, pl.ds(pl.multiple_of(me * rows, rows), rows), :]
        u, at = block_at(key)
        gram = lax.dot_general(q_ref[u, at, :], query, contract, preferred_element_type=F32)
        offset = lax.rem(unit * span + me * rows, BLOCK)
        shift = jnp.where(first, offset, 2 * BLOCK)
        for lane in lanes:
            n = lane.stop - lane.start
            part = gram[:, lane] * inv_ref[key, :, 0:n]
            lo, hi = (lane.start, lane.stop) if rows == BLOCK else (0, BLOCK)
            band = part[lo:hi]
            row = lax.broadcasted_iota(jnp.int32, band.shape, 0) + (lo - lane.start)
            col = lax.broadcasted_iota(jnp.int32, band.shape, 1)
            band = jnp.where(row - col == shift, NEG, band)
            above = [part[:lo]] if lo else []
            below = [part[hi:]] if hi < BLOCK else []
            part = jnp.concatenate(above + [band] + below, axis=0)
            s_ref[:, lane] = part
            most = jnp.max(jnp.max(tiles(part), axis=0), axis=0, keepdims=True)
            x_ref[:, lane] = jnp.broadcast_to(most, (8, n))

    def weigh(t, s_ref, x_ref, p_ref, a_ref):
        unit = unit_ref[t]
        first = unit_ref[t - 1] != unit
        old = jnp.where(first, 2 * NEG, top_ref[...])
        new = jnp.maximum(old, x_ref[...])
        top_ref[...] = new
        scale = jnp.exp2(old - new)
        a_ref[...] = scale
        for lane in lanes:
            prob = jnp.exp2(tiles(s_ref[:, lane]) - new[None, :, lane])
            sum_ref[unit, :, lane] = sum_ref[unit, :, lane] * scale[:, lane] + jnp.sum(
                prob, axis=0
            )
            p_ref[:, lane] = prob.reshape(BLOCK, lane.stop - lane.start).astype(BF16)

    def gather(t, p_ref, a_ref):
        unit, key = unit_ref[t], key_ref[t]
        part = jnp.dot(vt_ref[key], p_ref[...], preferred_element_type=F32)
        kept = tiles(acc_ref[unit]) * a_ref[...][None]
        acc_ref[unit] = kept.reshape(HD, rows) + part

    def pair_step(i, _):
        t = LEAD + 2 * i
        gather(t - 2, p0, a0)
        weigh(t - 1, s1, x1, p1, a1)
        score(t, s0, x0)
        gather(t - 1, p1, a1)
        weigh(t, s0, x0, p0, a0)
        score(t + 1, s1, x1)
        return 0

    lax.fori_loop(0, (count_ref[0] + 1) // 2 + 1, pair_step, 0)

    def finish(unit, _):
        total = 1.0 / jnp.sum(sum_ref[unit], axis=0, keepdims=True)
        o_ref[unit] = (acc_ref[unit] * total).T.astype(BF16)
        return 0

    lax.fori_loop(0, units, finish, 0)


def attend(spot, jobs, pieces):
    groups = len(pieces)
    shards, _, spans, rows, _ = pieces[0].shape
    units, span = shards * spans, rows * groups
    nblk = units * span // BLOCK
    work = 3 * units
    scores = pltpu.VMEM((BLOCK, rows), F32)
    probs = pltpu.VMEM((BLOCK, rows), BF16)
    line = pltpu.VMEM((8, rows), F32)
    return pl.pallas_call(
        functools.partial(attend_kernel, groups),
        in_specs=[SMEM] * 4 + [HBM] * groups,
        out_specs=pl.BlockSpec(memory_space=pltpu.VMEM),
        out_shape=jax.ShapeDtypeStruct((units, rows, HD), BF16),
        scratch_shapes=[
            pltpu.VMEM((units, span, HD), BF16),
            pltpu.VMEM((units, span, HD), BF16),
            pltpu.VMEM((nblk, HD, BLOCK), BF16),
            pltpu.VMEM((nblk, BLOCK, HD), F32),
            *[scores, scores, line, line, probs, probs, line, line],
            line,
            pltpu.VMEM((units + 1, 8, rows), F32),
            pltpu.VMEM((units + 1, HD, rows), F32),
            pltpu.SemaphoreType.DMA,
            pltpu.SemaphoreType.DMA,
        ],
        cost_estimate=pl.CostEstimate(
            flops=4 * work * rows * BLOCK * HD,
            bytes_accessed=4 * units * span * HD,
            transcendentals=work * rows * BLOCK,
        ),
        name="attend",
    )(spot, *jobs, *pieces)


def group_shift(x, shards, groups, r):
    pairs = [(i - i % groups + (i % groups + r) % groups, i) for i in range(shards)]
    return lax.ppermute(x, "seq", pairs)


def gather_weights(w_out, groups, member):
    count = lax.axis_size("head")
    share = w_out.shape[0] // groups
    mine = lax.dynamic_slice_in_dim(w_out, member * share, share, 0)
    return [
        lax.ppermute(mine, "head", [((i + r) % count, i) for i in range(count)])
        for r in range(1, count)
    ]


def project_kernel(spot_ref, x_ref, w_ref, *refs):
    heads, groups, spans, rows, _ = x_ref.shape
    pieces = refs[: (spans - 1) * groups]
    o_ref, wide_ref, w_buf, sem = refs[(spans - 1) * groups :]
    member, z = spot_ref[0], spot_ref[1]
    tile = w_buf.shape[2]
    share = pieces[0].shape[0]
    depth = heads * HD
    step, steps = pl.program_id(0), pl.num_programs(0)

    def copies(i):
        slot = lax.rem(i, 2)
        cols = pl.ds(pl.multiple_of(i * tile, tile), tile)
        out = [
            pltpu.make_async_copy(
                w_ref.at[:, cols],
                w_buf.at[slot, pl.ds(pl.multiple_of(z * depth, depth), depth), :],
                sem.at[slot],
            )
        ]
        for r in range(1, spans):
            for k in range(groups):
                at = lax.rem(z + r, spans) * depth + lax.rem(member + k, groups) * share
                out.append(
                    pltpu.make_async_copy(
                        pieces[(r - 1) * groups + k].at[:, cols],
                        w_buf.at[slot, pl.ds(pl.multiple_of(at, share), share), :],
                        sem.at[slot],
                    )
                )
        return out

    @pl.when(step == 0)
    def _():
        for copy in copies(step):
            copy.start()
        for z_at in range(spans):
            for h in range(heads):
                at = (z_at * heads + h) * HD
                for g in range(groups):
                    wide_ref[g * rows : (g + 1) * rows, at : at + HD] = x_ref[h, g, z_at]

    @pl.when(step + 1 < steps)
    def _():
        for copy in copies(step + 1):
            copy.start()

    for copy in copies(step):
        copy.wait()
    o_ref[...] = jnp.dot(
        wide_ref[...], w_buf[lax.rem(step, 2)], preferred_element_type=F32
    ).astype(BF16)


def project(spot, mixed, w_out, pieces):
    _, groups, spans, rows, _ = mixed.shape
    depth, width = w_out.shape
    tile = min(512, width)
    out_rows = groups * rows
    return pl.pallas_call(
        project_kernel,
        grid=(width // tile,),
        in_specs=[SMEM, pl.BlockSpec(memory_space=pltpu.VMEM)] + [HBM] * (1 + len(pieces)),
        out_specs=pl.BlockSpec((out_rows, tile), lambda i: (0, i)),
        out_shape=jax.ShapeDtypeStruct((out_rows, width), BF16),
        scratch_shapes=[
            pltpu.VMEM((out_rows, spans * depth), BF16),
            pltpu.VMEM((2, spans * depth, tile), BF16),
            pltpu.SemaphoreType.DMA((2,)),
        ],
        cost_estimate=pl.CostEstimate(
            flops=2 * out_rows * spans * depth * width,
            bytes_accessed=2 * spans * depth * width,
            transcendentals=0,
        ),
        name="project",
    )(spot, mixed, w_out, *pieces)


def body(qk, values, bucket, pair_row, pair_col, pair_count, w_out):
    shards = lax.axis_size("seq")
    spans = lax.axis_size("head")
    tokens, width = qk.shape
    heads = width // HD
    groups = shards // heads
    blocks = tokens // BLOCK
    slots = pair_row.shape[2]
    here, z = lax.axis_index("seq"), lax.axis_index("head")
    head, member = here // groups, lax.rem(here, groups)
    spot = jnp.stack([member, z, here]).astype(jnp.int32)

    shares = gather_weights(w_out, groups, member)
    sent = pack(qk, values, spans, groups)
    rows = sent.shape[4]
    got = lax.all_to_all(
        sent.reshape(shards, 2, spans, rows, HD), "seq", 0, 0, tiled=True
    )
    pieces = [got] + [group_shift(got, shards, groups, r) for r in range(1, groups)]

    tables = gather_tables(pair_row, pair_col, pair_count, shards)
    buckets = lax.dynamic_slice_in_dim(bucket, z * heads + head, 1, 1).reshape(-1)
    units = shards * spans
    jobs = job_lists(
        tables, buckets, spot, shards, slots, blocks, units, tokens // spans, rows
    )
    attn = attend(spot, jobs, pieces)
    mixed = lax.all_to_all(attn, ("seq", "head"), 0, 0, tiled=True)
    mixed = mixed.reshape(heads, groups, spans, rows, HD)
    weights = []
    for piece in shares:
        weights += [piece] + [
            group_shift(piece, shards, groups, k) for k in range(1, groups)
        ]
    return project(spot, mixed, w_out, weights)


def solution(mesh):
    return jax.shard_map(
        body,
        mesh=mesh,
        in_specs=(
            P("seq", "head"),
            P("seq", "head"),
            P(),
            P("seq", None, None),
            P("seq", None, None),
            P("seq", None),
            P("head", None),
        ),
        out_specs=P(("seq", "head"), None),
        check_vma=False,
    )
```

time: 289 us -> 275 us (0.952)
  the two profiles are of different devices: /device:TPU:2 before, /device:TPU:17 now
where the time goes in v2:
time: 275 us
  waiting for transfers between devices  137 us (50%)
  Pallas kernels  54.5 us (20%)
  blocking collectives  53.1 us (19%)
  starting transfers between devices  24 us (9%)
  local copies, waits for them, and re-layouts  5.21 us (2%)
    ppermute x3, waiting for transfers between devices, gather_weights(): lax.ppermute(mine, 'head', [((i + r) % count, i) for i in range(count)])  131 us
    all_to_all x1, blocking collectives, body(): lax.all_to_all(sent.reshape(shards, 2, spans, rows, HD), 'seq', 0, 0, til...  53.1 us
    pallas_call x1, Pallas kernels, attend(): pl.pallas_call(functools.partial(attend_kernel, groups), in_specs=[SMEM]...  29.6 us
    all_to_all x1, starting transfers between devices, body(): mixed = lax.all_to_all(attn, ('seq', 'head'), 0, 0, tiled=True)  11.9 us
    pallas_call x1, Pallas kernels, job_lists(): pl.pallas_call(kernel, in_specs=[SMEM, SMEM, SMEM], out_specs=[SMEM, SMEM...  10.4 us
    pallas_call x1, Pallas kernels, project(): pl.pallas_call(project_kernel, grid=(width // tile,), in_specs=[SMEM, pl....  9.57 us
    ppermute x7, starting transfers between devices, gather_tables(): lax.ppermute(mine, 'seq', [((i + r) % shards, i) for i in range(shards)])  5.8 us
  transfers between devices with their start and end apart: 15, of which 6 were waited for; matrix products, arithmetic and copies ran while one was open for 1% of the time, Pallas kernels for 4%

profile of v2, /device:TPU:17, one launch (start us, length us, event | category | flops | bytes accessed | tf_op | source)
XLA Modules:
  0.0 274.6 jit_solution(3610851712432730042)
XLA Ops:
  0.0 4.9 %pack.1 = bf16[4,2,2,4,256,128]{5,4,3,2,1,0:T(8,128)(2,1)} custom-call(bf16[2048,512]{1,0:T(8,128)(2,1)} %q_ref.1, bf16[2048,512]{1,0:T(8,128)(2,1)} %v_ref.1), custom_call_target="tpu_custom_call" | custom-call | bytes 8388608 | tf_op jit(solution)/shard_map/pack/pallas_call | solution.py:37
  5.0 53.1 %all_to_all.10.refs_0_ = bf16[8,2,4,256,128]{4,3,2,1,0:T(8,128)(2,1)} all-to-all(bf16[8,2,4,256,128]{4,3,2,1,0:T(8,128)(2,1)} %bitcast.8), channel_id=1, replica_groups=mesh['seq'=8,'head'=4] {'seq'}, dimensions={0} | all-to-all | bytes 8388608 | tf_op jit(solution)/shard_map/all_to_all | solution.py:424
  58.1 1.2 collective-permute-start.7
  60.0 2.9 %collective-permute-start.2 = (s32[56]{0:T(128)S(1)}, s32[56]{0:T(128)S(1)}, u32[]{:S(2)}, u32[]{:S(2)}) collective-permute-start(s32[56]{0:T(128)S(1)} %pad_add_fusion.1), channel_id=1, source_target_pairs={{12,0},{16,4},{20,8},{24,12},{28,16},{0,20},{4,24},{8,28},{13,1},{... | collective-permute-start | bytes 680 | tf_op jit(solution)/shard_map/ppermute | solution.py:57
  63.7 2.7 collective-permute-done
  67.2 1.5 collective-permute-start.6
  68.7 0.6 pad_add_fusion.spot_ref
  69.4 1.0 collective-permute-done.4
  70.3 0.7 concatenate.8.tab_ref
  71.0 10.4 %job_lists.1 = (s32[1]{0:T(128)}, s32[424]{0:T(512)}, s32[424]{0:T(512)}) custom-call(s32[448]{0:T(512)} %concatenate.8.tab_ref, s32[64]{0:T(128)} %dynamic-slice_bitcast_fusion.bucket_ref, s32[3]{0:T(128)} %pad_add_fusion.spot_ref), custom_call_target="tpu_custom_call" | custom-call | bytes 33554432 | tf_op jit(solution)/shard_map/job_lists/pallas_call | solution.py:123
  81.4 29.6 %attend.1 = bf16[32,256,128]{2,1,0:T(8,128)(2,1)} custom-call(s32[3]{0:T(128)} %pad_add_fusion.spot_ref, s32[1]{0:T(128)} %get-tuple-element.8.count_ref, s32[424]{0:T(512)} %get-tuple-element.9.unit_ref, s32[424]{0:T(512)} %get-tuple-element.10.key_ref, bf16[8,2,4,256,128]{4,3,2,1,0:T(8,128)(2,1)} %all_to_all.10.refs_0_, ...), custom_call_target="tpu_custom_call" | custom-call | flops 3221225472 | bytes 8388608 | tf_op jit(solution)/shard_map/attend/pallas_call | solution.py:289
  111.0 11.9 %all-to-all-start.1 = ((bf16[32,256,128]{2,1,0:T(8,128)(2,1)}), bf16[32,256,128]{2,1,0:T(8,128)(2,1)S(1)}, u32[]{:S(2)}, u32[]{:S(2)}) async-start(bf16[32,256,128]{2,1,0:T(8,128)(2,1)} %attend.1), calls=%async_computation.1 | async-start | bytes 4194304 | tf_op jit(solution)/shard_map/all_to_all | solution.py:436
  122.9 1.3 constant_dynamic-slice_fusion
  124.4 1.4 collective-permute-start.12
  125.7 1.0 collective-permute-start.8
  126.7 108.8 %collective-permute-done.10.refs_2_ = bf16[256,2048]{1,0:T(8,128)(2,1)S(1)} collective-permute-done((bf16[256,2048]{1,0:T(8,128)(2,1)S(1)}, bf16[256,2048]{1,0:T(8,128)(2,1)S(1)}, u32[]{:S(2)}, u32[]{:S(2)}) %collective-permute-start.10) | collective-permute-done | bytes 1048608 | tf_op jit(solution)/shard_map/ppermute | solution.py:325
  235.5 1.5 collective-permute-start.11
  237.1 21.7 %collective-permute-done.12.refs_4_ = bf16[256,2048]{1,0:T(8,128)(2,1)S(1)} collective-permute-done((bf16[256,2048]{1,0:T(8,128)(2,1)S(1)}, bf16[256,2048]{1,0:T(8,128)(2,1)S(1)}, u32[]{:S(2)}, u32[]{:S(2)}) %collective-permute-start.12) | collective-permute-done | bytes 1048608 | tf_op jit(solution)/shard_map/ppermute | solution.py:325
  258.8 1.0 collective-permute-start.13
  259.8 2.2 collective-permute-done.13.refs_5_
  262.0 1.1 copy-done.9
  263.1 0.5 collective-permute-done.9.refs_1_
  263.7 1.3 copy-done.1
  265.0 9.6 %project.1 = bf16[512,2048]{1,0:T(8,128)(2,1)} custom-call(s32[3]{0:T(128)} %pad_add_fusion.spot_ref, bf16[4,2,4,256,128]{4,3,2,1,0:T(8,128)(2,1)} %bitcast.9, bf16[512,2048]{1,0:T(8,128)(2,1)} %w_ref.1, bf16[256,2048]{1,0:T(8,128)(2,1)} %copy-done.7, bf16[256,2048]{1,0:T(8,128)(2,1)} %collective-permute-done.9.refs_1_, bf16[256,2048]{1,0:T(8,128)(2,1)} %copy-done.5, ...), custom_call_target="tpu_custom_call" | custom-call | flops 4294967296 | bytes 8388608 | tf_op jit(solution)/shard_map/project/pallas_call | solution.py:389
  (40 shorter events, 2.6 us)
Async XLA Ops:
  0.0 63.2 %copy-start = (s32[64,16]{0,1:T(8,128)S(1)}, s32[64,16]{0,1:T(8,128)}, u32[]{:S(2)}) copy-start(s32[64,16]{0,1:T(8,128)} %param.9) | copy-start | bytes 12292
  5.0 54.3 %copy-start.3 = (s32[1,8,3]{1,0,2:T(1,128)S(1)}, s32[1,8,3]{1,0,2:T(1,128)}, u32[]{:S(2)}) copy-start(s32[1,8,3]{1,0,2:T(1,128)} %param.10) | copy-start | bytes 292
  5.0 54.5 %copy-start.4 = (s32[1,8,3]{1,0,2:T(1,128)S(1)}, s32[1,8,3]{1,0,2:T(1,128)}, u32[]{:S(2)}) copy-start(s32[1,8,3]{1,0,2:T(1,128)} %param.11) | copy-start | bytes 292
  5.0 54.7 %copy-start.2 = (s32[1,8]{1,0:T(1,128)S(1)}, s32[1,8]{1,0:T(1,128)}, u32[]{:S(2)}) copy-start(s32[1,8]{1,0:T(1,128)} %param.12) | copy-start | bytes 100
  58.1 23.3 %collective-permute-start.7 = (bf16[8,2,4,256,128]{4,3,2,1,0:T(8,128)(2,1)}, bf16[8,2,4,256,128]{4,3,2,1,0:T(8,128)(2,1)}, u32[]{:S(2)}, u32[]{:S(2)}) collective-permute-start(bf16[8,2,4,256,128]{4,3,2,1,0:T(8,128)(2,1)} %all_to_all.10.refs_0_), channel_id=1, source_target_pairs={{4,0},{0,4},{12,8},{8,12},{20,16},{16,20},{28,24},{24,28},{5,1},{1... | collective-permute-start | bytes 12582920 | tf_op jit(solution)/shard_map/ppermute | solution.py:317
  59.7 6.7 %collective-permute-start = (s32[56]{0:T(128)S(1)}, s32[56]{0:T(128)S(1)}, u32[]{:S(2)}, u32[]{:S(2)}) collective-permute-start(s32[56]{0:T(128)S(1)} %pad_add_fusion.1), channel_id=1, source_target_pairs={{4,0},{8,4},{12,8},{16,12},{20,16},{24,20},{28,24},{0,28},{5,1},{9... | collective-permute-start | bytes 680 | tf_op jit(solution)/shard_map/ppermute | solution.py:57
  59.7 7.2 %collective-permute-start.1 = (s32[56]{0:T(128)S(1)}, s32[56]{0:T(128)S(1)}, u32[]{:S(2)}, u32[]{:S(2)}) collective-permute-start(s32[56]{0:T(128)S(1)} %pad_add_fusion.1), channel_id=1, source_target_pairs={{8,0},{12,4},{16,8},{20,12},{24,16},{28,20},{0,24},{4,28},{9,1},{1... | collective-permute-start | bytes 680 | tf_op jit(solution)/shard_map/ppermute | solution.py:57
  60.0 7.2 %collective-permute-start.2 = (s32[56]{0:T(128)S(1)}, s32[56]{0:T(128)S(1)}, u32[]{:S(2)}, u32[]{:S(2)}) collective-permute-start(s32[56]{0:T(128)S(1)} %pad_add_fusion.1), channel_id=1, source_target_pairs={{12,0},{16,4},{20,8},{24,12},{28,16},{0,20},{4,24},{8,28},{13,1},{... | collective-permute-start | bytes 680 | tf_op jit(solution)/shard_map/ppermute | solution.py:57
  62.9 6.4 %collective-permute-start.3 = (s32[56]{0:T(128)S(1)}, s32[56]{0:T(128)S(1)}, u32[]{:S(2)}, u32[]{:S(2)}) collective-permute-start(s32[56]{0:T(128)S(1)} %pad_add_fusion.1), channel_id=1, source_target_pairs={{16,0},{20,4},{24,8},{28,12},{0,16},{4,20},{8,24},{12,28},{17,1},{... | collective-permute-start | bytes 680 | tf_op jit(solution)/shard_map/ppermute | solution.py:57
  66.4 3.9 %collective-permute-start.4 = (s32[56]{0:T(128)S(1)}, s32[56]{0:T(128)S(1)}, u32[]{:S(2)}, u32[]{:S(2)}) collective-permute-start(s32[56]{0:T(128)S(1)} %pad_add_fusion.1), channel_id=1, source_target_pairs={{20,0},{24,4},{28,8},{0,12},{4,16},{8,20},{12,24},{16,28},{21,1},{... | collective-permute-start | bytes 680 | tf_op jit(solution)/shard_map/ppermute | solution.py:57
  67.0 3.4 %collective-permute-start.5 = (s32[56]{0:T(128)S(1)}, s32[56]{0:T(128)S(1)}, u32[]{:S(2)}, u32[]{:S(2)}) collective-permute-start(s32[56]{0:T(128)S(1)} %pad_add_fusion.1), channel_id=1, source_target_pairs={{24,0},{28,4},{0,8},{4,12},{8,16},{12,20},{16,24},{20,28},{25,1},{... | collective-permute-start | bytes 680 | tf_op jit(solution)/shard_map/ppermute | solution.py:57
  67.2 3.1 %collective-permute-start.6 = (s32[56]{0:T(128)S(1)}, s32[56]{0:T(128)S(1)}, u32[]{:S(2)}, u32[]{:S(2)}) collective-permute-start(s32[56]{0:T(128)S(1)} %pad_add_fusion.1), channel_id=1, source_target_pairs={{28,0},{0,4},{4,8},{8,12},{12,16},{16,20},{20,24},{24,28},{29,1},{... | collective-permute-start | bytes 680 | tf_op jit(solution)/shard_map/ppermute | solution.py:57
  111.0 152.6 %all-to-all-start.1 = ((bf16[32,256,128]{2,1,0:T(8,128)(2,1)}), bf16[32,256,128]{2,1,0:T(8,128)(2,1)S(1)}, u32[]{:S(2)}, u32[]{:S(2)}) async-start(bf16[32,256,128]{2,1,0:T(8,128)(2,1)} %attend.1), calls=%async_computation.1 | async-start | bytes 4194304 | tf_op jit(solution)/shard_map/all_to_all | solution.py:436
  124.2 111.3 %collective-permute-start.10 = (bf16[256,2048]{1,0:T(8,128)(2,1)S(1)}, bf16[256,2048]{1,0:T(8,128)(2,1)S(1)}, u32[]{:S(2)}, u32[]{:S(2)}) collective-permute-start(bf16[256,2048]{1,0:T(8,128)(2,1)S(1)} %constant_dynamic-slice_fusion), channel_id=1, source_target_pairs={{2,0},{3,1},{0,2},{1,3},{6,4},{7,5},{4,6},{5,7},{10,8},{11,9},{8,1... | collective-permute-start | bytes 3145736 | tf_op jit(solution)/shard_map/ppermute | solution.py:325
  124.4 134.4 %collective-permute-start.12 = (bf16[256,2048]{1,0:T(8,128)(2,1)S(1)}, bf16[256,2048]{1,0:T(8,128)(2,1)S(1)}, u32[]{:S(2)}, u32[]{:S(2)}) collective-permute-start(bf16[256,2048]{1,0:T(8,128)(2,1)S(1)} %constant_dynamic-slice_fusion), channel_id=1, source_target_pairs={{3,0},{0,1},{1,2},{2,3},{7,4},{4,5},{5,6},{6,7},{11,8},{8,9},{9,10... | collective-permute-start | bytes 3145736 | tf_op jit(solution)/shard_map/ppermute | solution.py:325
  125.7 134.0 %collective-permute-start.8 = (bf16[256,2048]{1,0:T(8,128)(2,1)S(1)}, bf16[256,2048]{1,0:T(8,128)(2,1)S(1)}, u32[]{:S(2)}, u32[]{:S(2)}) collective-permute-start(bf16[256,2048]{1,0:T(8,128)(2,1)S(1)} %constant_dynamic-slice_fusion), channel_id=1, source_target_pairs={{1,0},{2,1},{3,2},{0,3},{5,4},{6,5},{7,6},{4,7},{9,8},{10,9},{11,1... | collective-permute-start | bytes 3145736 | tf_op jit(solution)/shard_map/ppermute | solution.py:325
  235.5 28.1 %copy-start.5 = (bf16[256,2048]{1,0:T(8,128)(2,1)}, bf16[256,2048]{1,0:T(8,128)(2,1)S(1)}, u32[]{:S(2)}) copy-start(bf16[256,2048]{1,0:T(8,128)(2,1)S(1)} %collective-permute-done.10.refs_2_) | copy-start | bytes 3145732
  235.5 24.3 %collective-permute-start.11 = (bf16[256,2048]{1,0:T(8,128)(2,1)S(1)}, bf16[256,2048]{1,0:T(8,128)(2,1)S(1)}, u32[]{:S(2)}, u32[]{:S(2)}) collective-permute-start(bf16[256,2048]{1,0:T(8,128)(2,1)S(1)} %collective-permute-done.10.refs_2_), channel_id=1, source_target_pairs={{4,0},{0,4},{12,8},{8,12},{20,16},{16,20},{28,24},{24,28},{5,1},{1... | collective-permute-start | bytes 3145736 | tf_op jit(solution)/shard_map/ppermute | solution.py:317
  258.8 3.3 %copy-start.6 = (bf16[256,2048]{1,0:T(8,128)(2,1)}, bf16[256,2048]{1,0:T(8,128)(2,1)S(1)}, u32[]{:S(2)}) copy-start(bf16[256,2048]{1,0:T(8,128)(2,1)S(1)} %collective-permute-done.12.refs_4_) | copy-start | bytes 3145732
  258.8 3.3 %collective-permute-start.13 = (bf16[256,2048]{1,0:T(8,128)(2,1)S(1)}, bf16[256,2048]{1,0:T(8,128)(2,1)S(1)}, u32[]{:S(2)}, u32[]{:S(2)}) collective-permute-start(bf16[256,2048]{1,0:T(8,128)(2,1)S(1)} %collective-permute-done.12.refs_4_), channel_id=1, source_target_pairs={{4,0},{0,4},{12,8},{8,12},{20,16},{16,20},{28,24},{24,28},{5,1},{1... | collective-permute-start | bytes 3145736 | tf_op jit(solution)/shard_map/ppermute | solution.py:317
  259.7 2.3 copy-start.7
  259.7 3.9 %collective-permute-start.9 = (bf16[256,2048]{1,0:T(8,128)(2,1)S(1)}, bf16[256,2048]{1,0:T(8,128)(2,1)}, u32[]{:S(2)}, u32[]{:S(2)}) collective-permute-start(bf16[256,2048]{1,0:T(8,128)(2,1)S(1)} %collective-permute-done.8.refs_0_), channel_id=1, source_target_pairs={{4,0},{0,4},{12,8},{8,12},{20,16},{16,20},{28,24},{24,28},{5,1},{1... | collective-permute-start | bytes 3145736 | tf_op jit(solution)/shard_map/ppermute | solution.py:317
  259.8 2.2 copy-start.8
  263.7 1.3 copy-start.1
  (1 other events, 1.1 us)

commit v3 on v2

--- a/solution.py
+++ b/solution.py
@@ -12,41 +12,42 @@
 HD = 128
 BLOCK = 256
 NEG = -1e30
-LEAD, TAIL = 2, 6
+LEAD, TAIL = 2, 14
 PREP_STEP = 4
+CHUNK = 8
+VALUE_STEP = 4
+FINISH_STEP = 4
 BF16 = jnp.bfloat16
 F32 = jnp.float32
 SMEM = pl.BlockSpec(memory_space=pltpu.SMEM)
 HBM = pl.BlockSpec(memory_space=pl.ANY)
 
 
-def pack_kernel(q_ref, v_ref, o_ref):
-    heads, groups, _, _, rows, _ = o_ref.shape
+def pack_kernel(turned, x_ref, o_ref):
+    heads, groups = o_ref.shape[:2]
+    rows = x_ref.shape[0] // groups
     for h in range(heads):
         for g in range(groups):
-            at = (pl.ds(g * rows, rows), pl.ds(h * HD, HD))
-            o_ref[h, g, 0, 0] = q_ref[at]
-            o_ref[h, g, 1, 0] = v_ref[at]
-
-
-def pack(qk, values, spans, groups):
-    tokens, width = qk.shape
+            part = x_ref[g * rows : (g + 1) * rows, h * HD : (h + 1) * HD]
+            o_ref[h, g, 0] = part.T if turned else part
+
+
+def pack(x, spans, groups, turned=False):
+    tokens, width = x.shape
     heads, span = width // HD, tokens // spans
     rows = span // groups
-    block = pl.BlockSpec((span, width), lambda i: (i, 0))
+    tail = (HD, rows) if turned else (rows, HD)
     return pl.pallas_call(
-        pack_kernel,
+        functools.partial(pack_kernel, turned),
         grid=(spans,),
-        in_specs=[block, block],
-        out_specs=pl.BlockSpec(
-            (heads, groups, 2, 1, rows, HD), lambda i: (0, 0, 0, i, 0, 0)
-        ),
-        out_shape=jax.ShapeDtypeStruct((heads, groups, 2, spans, rows, HD), BF16),
+        in_specs=[pl.BlockSpec((span, width), lambda i: (i, 0))],
+        out_specs=pl.BlockSpec((heads, groups, 1, *tail), lambda i: (0, 0, i, 0, 0)),
+        out_shape=jax.ShapeDtypeStruct((heads, groups, spans, *tail), BF16),
         cost_estimate=pl.CostEstimate(
-            flops=0, bytes_accessed=8 * tokens * width, transcendentals=0
+            flops=0, bytes_accessed=4 * tokens * width, transcendentals=0
         ),
         name="pack",
-    )(qk, values)
+    )(x)
 
 
 def gather_tables(pair_row, pair_col, pair_count, shards):
@@ -145,14 +146,15 @@
 
 
 def attend_kernel(groups, spot_ref, count_ref, unit_ref, key_ref, *refs):
-    pieces = refs[:groups]
+    pieces = refs[:groups], refs[groups : 2 * groups]
+    refs = refs[groups:]
     o_ref, q_ref, v_ref, vt_ref, inv_ref, s0, s1, x0, x1, p0, p1, a0, a1 = refs[
         groups : groups + 13
     ]
     top_ref, sum_ref, acc_ref, q_sem, v_sem = refs[groups + 13 :]
     units, span, _ = q_ref.shape
     rows = span // groups
-    spans = pieces[0].shape[2]
+    spans = pieces[0][0].shape[1]
     shards = units // spans
     blocks_per = span // BLOCK
     me = spot_ref[0]
@@ -165,7 +167,7 @@
             for s in range(shards):
                 copies[part].append(
                     pltpu.make_async_copy(
-                        pieces[r].at[s, part],
+                        pieces[part][r].at[s],
                         ref.at[pl.ds(s * spans, spans), pl.ds(piece * rows, rows), :],
                         sem,
                     )
@@ -277,9 +279,9 @@
     lax.fori_loop(0, units, finish, 0)
 
 
-def attend(spot, jobs, pieces):
-    groups = len(pieces)
-    shards, _, spans, rows, _ = pieces[0].shape
+def attend(spot, jobs, q_pieces, v_pieces):
+    groups = len(q_pieces)
+    shards, spans, rows, _ = q_pieces[0].shape
     units, span = shards * spans, rows * groups
     nblk = units * span // BLOCK
     work = 3 * units
@@ -288,7 +290,7 @@
     line = pltpu.VMEM((8, rows), F32)
     return pl.pallas_call(
         functools.partial(attend_kernel, groups),
-        in_specs=[SMEM] * 4 + [HBM] * groups,
+        in_specs=[SMEM] * 4 + [HBM] * (2 * groups),
         out_specs=pl.BlockSpec(memory_space=pltpu.VMEM),
         out_shape=jax.ShapeDtypeStruct((units, rows, HD), BF16),
         scratch_shapes=[
@@ -309,7 +311,266 @@
             transcendentals=work * rows * BLOCK,
         ),
         name="attend",
+    )(spot, *jobs, *q_pieces, *v_pieces)
+
+
+def scores_kernel(groups, spot_ref, count_ref, unit_ref, key_ref, *refs):
+    pieces = refs[:groups]
+    p_out, scale_ref, sum_ref, q_ref, inv_ref, s0, s1, x0, x1, top_ref, p_buf, q_sem, p_sem = refs[
+        groups:
+    ]
+    shards, spans, rows, _ = pieces[0].shape
+    units = shards * spans
+    me = spot_ref[0]
+    lanes = [slice(k, k + HD) for k in range(0, rows, HD)]
+
+    copies = []
+    for r in range(groups):
+        piece = lax.rem(me + r, groups)
+        for s in range(shards):
+            copies.append(
+                pltpu.make_async_copy(
+                    pieces[r].at[s], q_ref.at[pl.ds(s * spans, spans), piece], q_sem
+                )
+            )
+    for copy in copies:
+        copy.start()
+    sum_ref[...] = jnp.zeros(sum_ref.shape, F32)
+    for copy in copies:
+        copy.wait()
+
+    ones = jnp.ones((HD, HD), BF16)
+    contract = (((1,), (1,)), ((), ()))
+
+    def prepare(i, _):
+        for k in range(PREP_STEP):
+            b = i * PREP_STEP + k
+            wide = q_ref[b // groups, lax.rem(b, groups)].astype(F32)
+            square = wide * wide
+            high = square.astype(BF16)
+            low = (square - high.astype(F32)).astype(BF16)
+            total = jnp.dot(high, ones, preferred_element_type=F32)
+            total += jnp.dot(low, ones, preferred_element_type=F32)
+            scale = math.log2(math.e) / math.sqrt(HD)
+            inv_ref[b] = lax.rsqrt(total * (1.0 / HD) + 1e-06) * scale
+        return 0
+
+    lax.fori_loop(0, units * groups // PREP_STEP, prepare, 0)
+
+    def tiles(x):
+        return x.reshape(x.shape[0] // 8, 8, x.shape[1])
+
+    def score(j, s_ref, x_ref):
+        t = LEAD + j
+        unit, key = jnp.minimum(unit_ref[t], units - 1), key_ref[t]
+        first = unit_ref[t - 1] != unit_ref[t]
+        gram = lax.dot_general(
+            q_ref[key // groups, lax.rem(key, groups)],
+            q_ref[unit, me],
+            contract,
+            preferred_element_type=F32,
+        )
+        shift = jnp.where(first, 0, 2 * BLOCK)
+        for lane in lanes:
+            part = gram[:, lane] * inv_ref[key]
+            band = part[lane]
+            row = lax.broadcasted_iota(jnp.int32, band.shape, 0)
+            col = lax.broadcasted_iota(jnp.int32, band.shape, 1)
+            band = jnp.where(row - col == shift, NEG, band)
+            above = [part[: lane.start]] if lane.start else []
+            below = [part[lane.stop :]] if lane.stop < BLOCK else []
+            part = jnp.concatenate(above + [band] + below, axis=0)
+            s_ref[:, lane] = part
+            most = jnp.max(jnp.max(tiles(part), axis=0), axis=0, keepdims=True)
+            x_ref[:, lane] = jnp.broadcast_to(most, (8, HD))
+
+    def weigh(j, s_ref, x_ref, slot, at):
+        unit = unit_ref[LEAD + j]
+        first = unit_ref[LEAD + j - 1] != unit
+        old = jnp.where(first, 2 * NEG, top_ref[...])
+        new = jnp.maximum(old, x_ref[...])
+        top_ref[...] = new
+        scale = jnp.exp2(old - new)
+        scale_ref[pl.ds(j, 1), :] = scale[0:1]
+        total = sum_ref[unit] * scale
+        for lane in lanes:
+            prob = jnp.exp2(tiles(s_ref[:, lane]) - new[None, :, lane])
+            sum_ref[unit, :, lane] = total[:, lane] + jnp.sum(prob, axis=0)
+            p_buf[slot, at, :, lane] = prob.reshape(BLOCK, HD).astype(BF16)
+
+    def out_copy(chunk):
+        slot = lax.rem(chunk, 2)
+        return pltpu.make_async_copy(
+            p_buf.at[slot], p_out.at[pl.ds(chunk * CHUNK, CHUNK)], p_sem.at[slot]
+        )
+
+    score(0, s0, x0)
+    score(1, s1, x1)
+    chunks = (count_ref[0] + CHUNK - 1) // CHUNK
+
+    def chunk_step(chunk, _):
+        slot = lax.rem(chunk, 2)
+
+        @pl.when(chunk >= 2)
+        def _():
+            out_copy(chunk - 2).wait()
+
+        def step(k, _):
+            j = chunk * CHUNK + 2 * k
+            weigh(j, s0, x0, slot, 2 * k)
+            weigh(j + 1, s1, x1, slot, 2 * k + 1)
+            score(j + 2, s0, x0)
+            score(j + 3, s1, x1)
+            return 0
+
+        lax.fori_loop(0, CHUNK // 2, step, 0)
+        out_copy(chunk).start()
+        return 0
+
+    lax.fori_loop(0, chunks, chunk_step, 0)
+    for back in (2, 1):
+
+        @pl.when(chunks >= back)
+        def _():
+            out_copy(chunks - back).wait()
+
+
+def attend_scores(spot, jobs, pieces):
+    groups = len(pieces)
+    shards, spans, rows, _ = pieces[0].shape
+    units = shards * spans
+    nblk = units * groups
+    room = jobs[1].shape[0] // CHUNK * CHUNK
+    work = 3 * units
+    vmem = pl.BlockSpec(memory_space=pltpu.VMEM)
+    return pl.pallas_call(
+        functools.partial(scores_kernel, groups),
+        in_specs=[SMEM] * 4 + [HBM] * groups,
+        out_specs=[HBM, vmem, vmem],
+        out_shape=[
+            jax.ShapeDtypeStruct((room, BLOCK, rows), BF16),
+            jax.ShapeDtypeStruct((room, rows), F32),
+            jax.ShapeDtypeStruct((units + 1, 8, rows), F32),
+        ],
+        scratch_shapes=[
+            pltpu.VMEM((units, groups, rows, HD), BF16),
+            pltpu.VMEM((nblk, BLOCK, HD), F32),
+            pltpu.VMEM((BLOCK, rows), F32),
+            pltpu.VMEM((BLOCK, rows), F32),
+            *[pltpu.VMEM((8, rows), F32)] * 3,
+            pltpu.VMEM((2, CHUNK, BLOCK, rows), BF16),
+            pltpu.SemaphoreType.DMA,
+            pltpu.SemaphoreType.DMA((2,)),
+        ],
+        cost_estimate=pl.CostEstimate(
+            flops=2 * work * rows * BLOCK * HD,
+            bytes_accessed=2 * units * groups * rows * HD + 2 * work * rows * BLOCK,
+            transcendentals=work * rows * BLOCK,
+        ),
+        name="attend_scores",
     )(spot, *jobs, *pieces)
+
+
+def values_kernel(groups, spot_ref, count_ref, unit_ref, key_ref, *refs):
+    pieces = refs[:groups]
+    p_in, scale_ref, sum_ref, o_ref, vt_ref, acc_ref, p_buf, v_sem, p_sem = refs[groups:]
+    shards, spans, _, _ = pieces[0].shape
+    units = shards * spans
+    me = spot_ref[0]
+
+    copies = []
+    for r in range(groups):
+        piece = lax.rem(me + r, groups)
+        for s in range(shards):
+            copies.append(
+                pltpu.make_async_copy(
+                    pieces[r].at[s], vt_ref.at[pl.ds(s * spans, spans), piece], v_sem
+                )
+            )
+    for copy in copies:
+        copy.start()
+
+    def in_copy(chunk):
+        slot = lax.rem(chunk, 2)
+        return pltpu.make_async_copy(
+            p_in.at[pl.ds(chunk * CHUNK, CHUNK)], p_buf.at[slot], p_sem.at[slot]
+        )
+
+    in_copy(0).start()
+
+    def clear(unit, _):
+        acc_ref[unit] = jnp.zeros(acc_ref.shape[1:], F32)
+        return 0
+
+    lax.fori_loop(0, units + 1, clear, 0)
+    for copy in copies:
+        copy.wait()
+
+    def gather(j, slot, at):
+        unit, key = unit_ref[LEAD + j], key_ref[LEAD + j]
+        part = jnp.dot(
+            vt_ref[key // groups, lax.rem(key, groups)],
+            p_buf[slot, at],
+            preferred_element_type=F32,
+        )
+        acc_ref[unit] = acc_ref[unit] * scale_ref[pl.ds(j, 1), :] + part
+
+    chunks = (count_ref[0] + CHUNK - 1) // CHUNK
+
+    def chunk_step(chunk, _):
+        slot = lax.rem(chunk, 2)
+
+        @pl.when(chunk + 1 < chunks)
+        def _():
+            in_copy(chunk + 1).start()
+
+        in_copy(chunk).wait()
+
+        def step(k, _):
+            for i in range(VALUE_STEP):
+                gather(chunk * CHUNK + VALUE_STEP * k + i, slot, VALUE_STEP * k + i)
+            return 0
+
+        lax.fori_loop(0, CHUNK // VALUE_STEP, step, 0)
+        return 0
+
+    lax.fori_loop(0, chunks, chunk_step, 0)
+
+    def finish(i, _):
+        for k in range(FINISH_STEP):
+            unit = i * FINISH_STEP + k
+            total = 1.0 / jnp.sum(sum_ref[unit], axis=0, keepdims=True)
+            o_ref[unit] = (acc_ref[unit] * total).astype(BF16).T
+        return 0
+
+    lax.fori_loop(0, units // FINISH_STEP, finish, 0)
+
+
+def attend_values(spot, jobs, pieces, probs, scales, sums):
+    groups = len(pieces)
+    shards, spans, _, rows = pieces[0].shape
+    units = shards * spans
+    work = 3 * units
+    vmem = pl.BlockSpec(memory_space=pltpu.VMEM)
+    return pl.pallas_call(
+        functools.partial(values_kernel, groups),
+        in_specs=[SMEM] * 4 + [HBM] * (groups + 1) + [vmem, vmem],
+        out_specs=vmem,
+        out_shape=jax.ShapeDtypeStruct((units, rows, HD), BF16),
+        scratch_shapes=[
+            pltpu.VMEM((units, groups, HD, rows), BF16),
+            pltpu.VMEM((units + 1, HD, rows), F32),
+            pltpu.VMEM((2, CHUNK, BLOCK, rows), BF16),
+            pltpu.SemaphoreType.DMA,
+            pltpu.SemaphoreType.DMA((2,)),
+        ],
+        cost_estimate=pl.CostEstimate(
+            flops=2 * work * rows * BLOCK * HD,
+            bytes_accessed=2 * units * groups * rows * HD + 2 * work * rows * BLOCK,
+            transcendentals=0,
+        ),
+        name="attend_values",
+    )(spot, *jobs, *pieces, probs, scales, sums)
 
 
 def group_shift(x, shards, groups, r):
@@ -419,20 +680,28 @@
     spot = jnp.stack([member, z, here]).astype(jnp.int32)
 
     shares = gather_weights(w_out, groups, member)
-    sent = pack(qk, values, spans, groups)
-    rows = sent.shape[4]
-    got = lax.all_to_all(
-        sent.reshape(shards, 2, spans, rows, HD), "seq", 0, 0, tiled=True
-    )
-    pieces = [got] + [group_shift(got, shards, groups, r) for r in range(1, groups)]
-
+    units = shards * spans
+    rows = tokens // spans // groups
+    turned = rows == BLOCK
+
+    def send(x, turn):
+        sent = pack(x, spans, groups, turn)
+        sent = sent.reshape(shards, spans, *sent.shape[3:])
+        got = lax.all_to_all(sent, "seq", 0, 0, tiled=True)
+        return [got] + [group_shift(got, shards, groups, r) for r in range(1, groups)]
+
+    q_pieces = send(qk, False)
+    v_pieces = send(values, turned)
     tables = gather_tables(pair_row, pair_col, pair_count, shards)
     buckets = lax.dynamic_slice_in_dim(bucket, z * heads + head, 1, 1).reshape(-1)
-    units = shards * spans
     jobs = job_lists(
         tables, buckets, spot, shards, slots, blocks, units, tokens // spans, rows
     )
-    attn = attend(spot, jobs, pieces)
+    if turned:
+        weights = attend_scores(spot, jobs, q_pieces)
+        attn = attend_values(spot, jobs, v_pieces, *weights)
+    else:
+        attn = attend(spot, jobs, q_pieces, v_pieces)
     mixed = lax.all_to_all(attn, ("seq", "head"), 0, 0, tiled=True)
     mixed = mixed.reshape(heads, groups, spans, rows, HD)
     weights = []

time: 275 us -> 295 us (1.073)
  the two profiles are of different devices: /device:TPU:17 before, /device:TPU:2 now
where the time goes in v3:
time: 295 us; the launch traced here: 292 us
  waiting for transfers between devices  186 us (63%)
  Pallas kernels  67.6 us (23%)
  starting transfers between devices  30.5 us (10%)
  local copies, waits for them, and re-layouts  6.54 us (2%)
    ppermute x3, waiting for transfers between devices, gather_weights(): lax.ppermute(mine, 'head', [((i + r) % count, i) for i in range(count)])  133 us
    all_to_all x2, waiting for transfers between devices, send(): got = lax.all_to_all(sent, 'seq', 0, 0, tiled=True)  46 us
    pallas_call x1, Pallas kernels, attend_scores(): pl.pallas_call(functools.partial(scores_kernel, groups), in_specs=[SMEM]...  22.5 us
    pallas_call x1, Pallas kernels, attend_values(): pl.pallas_call(functools.partial(values_kernel, groups), in_specs=[SMEM]...  17.1 us
    all_to_all x1, starting transfers between devices, body(): mixed = lax.all_to_all(attn, ('seq', 'head'), 0, 0, tiled=True)  11.8 us
    pallas_call x1, Pallas kernels, job_lists(): pl.pallas_call(kernel, in_specs=[SMEM, SMEM, SMEM], out_specs=[SMEM, SMEM...  10.4 us
    pallas_call x1, Pallas kernels, project(): pl.pallas_call(project_kernel, grid=(width // tile,), in_specs=[SMEM, pl....  9.58 us
    all_to_all x2, starting transfers between devices, send(): got = lax.all_to_all(sent, 'seq', 0, 0, tiled=True)  9.28 us
  transfers between devices with their start and end apart: 18, of which 11 were waited for; matrix products, arithmetic and copies ran while one was open for 1% of the time, Pallas kernels for 13%

profile of v3, /device:TPU:2, one launch (start us, length us, event | category | flops | bytes accessed | tf_op | source)
XLA Modules:
  0.0 291.9 jit_solution(13616887646273640462)
XLA Ops:
  0.0 3.9 %pack.3 = bf16[4,2,4,256,128]{4,3,2,1,0:T(8,128)(2,1)} custom-call(bf16[2048,512]{1,0:T(8,128)(2,1)} %x_ref.3), custom_call_target="tpu_custom_call" | custom-call | bytes 4194304 | tf_op jit(solution)/shard_map/pack/pallas_call | solution.py:40
  3.9 4.3 %all-to-all-start.1 = ((bf16[8,4,256,128]{3,2,1,0:T(8,128)(2,1)}), bf16[8,4,256,128]{3,2,1,0:T(8,128)(2,1)S(1)}, u32[]{:S(2)}, u32[]{:S(2)}) async-start(bf16[8,4,256,128]{3,2,1,0:T(8,128)(2,1)} %bitcast.10), calls=%async_computation.1 | async-start | bytes 4194304 | tf_op jit(solution)/shard_map/all_to_all | solution.py:690
  8.2 4.1 %pack.2 = bf16[4,2,4,128,256]{4,3,2,1,0:T(8,128)(2,1)} custom-call(bf16[2048,512]{1,0:T(8,128)(2,1)} %x_ref.2), custom_call_target="tpu_custom_call" | custom-call | bytes 4194304 | tf_op jit(solution)/shard_map/pack/pallas_call | solution.py:40
  12.3 21.0 %all-to-all-done.1.refs_0_ = bf16[8,4,256,128]{3,2,1,0:T(8,128)(2,1)S(1)} async-done(((bf16[8,4,256,128]{3,2,1,0:T(8,128)(2,1)}), bf16[8,4,256,128]{3,2,1,0:T(8,128)(2,1)S(1)}, u32[]{:S(2)}, u32[]{:S(2)}) %all-to-all-start.1) | async-done | bytes 2097184 | tf_op jit(solution)/shard_map/all_to_all | solution.py:690
  33.3 1.3 copy-done.3
  34.6 5.0 %all-to-all-start = ((bf16[8,4,128,256]{3,2,1,0:T(8,128)(2,1)}), bf16[8,4,128,256]{3,2,1,0:T(8,128)(2,1)S(1)}, u32[]{:S(2)}, u32[]{:S(2)}) async-start(bf16[8,4,128,256]{3,2,1,0:T(8,128)(2,1)} %bitcast.9), calls=%async_computation | async-start | bytes 4194304 | tf_op jit(solution)/shard_map/all_to_all | solution.py:690
  39.8 25.0 %all-to-all-done.refs_0_ = bf16[8,4,128,256]{3,2,1,0:T(8,128)(2,1)S(1)} async-done(((bf16[8,4,128,256]{3,2,1,0:T(8,128)(2,1)}), bf16[8,4,128,256]{3,2,1,0:T(8,128)(2,1)S(1)}, u32[]{:S(2)}, u32[]{:S(2)}) %all-to-all-start) | async-done | bytes 2097184 | tf_op jit(solution)/shard_map/all_to_all | solution.py:690
  65.3 1.6 collective-permute-start
  68.0 1.1 collective-permute-done
  69.7 1.6 collective-permute-done.1
  71.7 1.0 collective-permute-start.5
  76.5 10.4 %job_lists.1 = (s32[1]{0:T(128)}, s32[432]{0:T(512)}, s32[432]{0:T(512)}) custom-call(s32[448]{0:T(512)} %concatenate.8.tab_ref, s32[64]{0:T(128)} %dynamic-slice_bitcast_fusion.bucket_ref, s32[3]{0:T(128)} %pad_add_fusion.spot_ref), custom_call_target="tpu_custom_call" | custom-call | bytes 33554432 | tf_op jit(solution)/shard_map/job_lists/pallas_call | solution.py:124
  86.9 22.5 %attend_scores.1 = (bf16[432,256,256]{2,1,0:T(8,128)(2,1)}, f32[432,256]{1,0:T(8,128)}, f32[33,8,256]{2,1,0:T(8,128)}) custom-call(s32[3]{0:T(128)} %pad_add_fusion.spot_ref, s32[1]{0:T(128)} %get-tuple-element.11.count_ref, s32[432]{0:T(512)} %get-tuple-element.12.unit_ref, s32[432]{0:T(512)} %get-tuple-element.13.key_ref, ...), custom_call_target="tpu_custom_call" | custom-call | flops 1610612736 | bytes 16777216 | tf_op jit(solution)/shard_map/attend_scores/pallas_call | solution.py:446
  109.4 17.1 %attend_values.1 = bf16[32,256,128]{2,1,0:T(8,128)(2,1)} custom-call(s32[3]{0:T(128)} %pad_add_fusion.spot_ref, s32[1]{0:T(128)} %get-tuple-element.11.count_ref, s32[432]{0:T(512)} %get-tuple-element.12.unit_ref, s32[432]{0:T(512)} %get-tuple-element.13.key_ref, bf16[8,4,128,256]{3,2,1,0:T(8,128)(2,1)} %copy-done.2, ...), custom_call_target="tpu_custom_call" | custom-call | flops 1610612736 | bytes 16777216 | tf_op jit(solution)/shard_map/attend_values/pallas_call | solution.py:555
  126.6 11.8 %all-to-all-start.2 = ((bf16[32,256,128]{2,1,0:T(8,128)(2,1)}), bf16[32,256,128]{2,1,0:T(8,128)(2,1)S(1)}, u32[]{:S(2)}, u32[]{:S(2)}) async-start(bf16[32,256,128]{2,1,0:T(8,128)(2,1)} %attend_values.1), calls=%async_computation.2 | async-start | bytes 4194304 | tf_op jit(solution)/shard_map/all_to_all | solution.py:705
  138.4 1.3 constant_dynamic-slice_fusion
  139.7 3.4 %collective-permute-start.9 = (bf16[256,2048]{1,0:T(8,128)(2,1)S(1)}, bf16[256,2048]{1,0:T(8,128)(2,1)S(1)}, u32[]{:S(2)}, u32[]{:S(2)}) collective-permute-start(bf16[256,2048]{1,0:T(8,128)(2,1)S(1)} %constant_dynamic-slice_fusion), channel_id=1, source_target_pairs={{1,0},{2,1},{3,2},{0,3},{5,4},{6,5},{7,6},{4,7},{9,8},{10,9},{11,1... | collective-permute-start | bytes 3145736 | tf_op jit(solution)/shard_map/ppermute | solution.py:586
  143.0 1.1 collective-permute-start.13
  144.1 53.0 %collective-permute-done.9.refs_0_ = bf16[256,2048]{1,0:T(8,128)(2,1)S(1)} collective-permute-done((bf16[256,2048]{1,0:T(8,128)(2,1)S(1)}, bf16[256,2048]{1,0:T(8,128)(2,1)S(1)}, u32[]{:S(2)}, u32[]{:S(2)}) %collective-permute-start.9) | collective-permute-done | bytes 1048608 | tf_op jit(solution)/shard_map/ppermute | solution.py:586
  197.1 79.5 %collective-permute-done.11.refs_2_ = bf16[256,2048]{1,0:T(8,128)(2,1)S(1)} collective-permute-done((bf16[256,2048]{1,0:T(8,128)(2,1)S(1)}, bf16[256,2048]{1,0:T(8,128)(2,1)S(1)}, u32[]{:S(2)}, u32[]{:S(2)}) %collective-permute-start.11) | collective-permute-done | bytes 1048608 | tf_op jit(solution)/shard_map/ppermute | solution.py:586
  277.2 2.1 collective-permute-done.12.refs_3_
  279.3 1.0 copy-done.12
  281.0 1.3 copy-done.4
  282.3 9.6 %project.1 = bf16[512,2048]{1,0:T(8,128)(2,1)} custom-call(s32[3]{0:T(128)} %pad_add_fusion.spot_ref, bf16[4,2,4,256,128]{4,3,2,1,0:T(8,128)(2,1)} %bitcast.11, bf16[512,2048]{1,0:T(8,128)(2,1)} %w_ref.1, bf16[256,2048]{1,0:T(8,128)(2,1)} %copy-done.8, bf16[256,2048]{1,0:T(8,128)(2,1)} %copy-done.11, bf16[256,2048]{1,0:T(8,128)(2,1)} %copy-done.9, ...), custom_call_target="tpu_custom_call" | custom-call | flops 4294967296 | bytes 8388608 | tf_op jit(solution)/shard_map/project/pallas_call | solution.py:650
  (53 shorter events, 7.6 us)
Async XLA Ops:
  0.0 67.4 %copy-start = (s32[64,16]{0,1:T(8,128)S(1)}, s32[64,16]{0,1:T(8,128)}, u32[]{:S(2)}) copy-start(s32[64,16]{0,1:T(8,128)} %param.9) | copy-start | bytes 12292
  3.9 29.4 %all-to-all-start.1 = ((bf16[8,4,256,128]{3,2,1,0:T(8,128)(2,1)}), bf16[8,4,256,128]{3,2,1,0:T(8,128)(2,1)S(1)}, u32[]{:S(2)}, u32[]{:S(2)}) async-start(bf16[8,4,256,128]{3,2,1,0:T(8,128)(2,1)} %bitcast.10), calls=%async_computation.1 | async-start | bytes 4194304 | tf_op jit(solution)/shard_map/all_to_all | solution.py:690
  33.3 31.6 %copy-start.6 = (s32[1,8,3]{1,0,2:T(1,128)S(1)}, s32[1,8,3]{1,0,2:T(1,128)}, u32[]{:S(2)}) copy-start(s32[1,8,3]{1,0,2:T(1,128)} %param.10) | copy-start | bytes 292
  33.3 31.7 %copy-start.7 = (s32[1,8,3]{1,0,2:T(1,128)S(1)}, s32[1,8,3]{1,0,2:T(1,128)}, u32[]{:S(2)}) copy-start(s32[1,8,3]{1,0,2:T(1,128)} %param.11) | copy-start | bytes 292
  33.3 31.9 %copy-start.5 = (s32[1,8]{1,0:T(1,128)S(1)}, s32[1,8]{1,0:T(1,128)}, u32[]{:S(2)}) copy-start(s32[1,8]{1,0:T(1,128)} %param.12) | copy-start | bytes 100
  34.6 30.1 %all-to-all-start = ((bf16[8,4,128,256]{3,2,1,0:T(8,128)(2,1)}), bf16[8,4,128,256]{3,2,1,0:T(8,128)(2,1)S(1)}, u32[]{:S(2)}, u32[]{:S(2)}) async-start(bf16[8,4,128,256]{3,2,1,0:T(8,128)(2,1)} %bitcast.9), calls=%async_computation | async-start | bytes 4194304 | tf_op jit(solution)/shard_map/all_to_all | solution.py:690
  39.7 47.2 %collective-permute-start.8 = (bf16[8,4,256,128]{3,2,1,0:T(8,128)(2,1)}, bf16[8,4,256,128]{3,2,1,0:T(8,128)(2,1)}, u32[]{:S(2)}, u32[]{:S(2)}) collective-permute-start(bf16[8,4,256,128]{3,2,1,0:T(8,128)(2,1)} %copy-done.3), channel_id=1, source_target_pairs={{4,0},{0,4},{12,8},{8,12},{20,16},{16,20},{28,24},{24,28},{5,1},{1... | collective-permute-start | bytes 6291464 | tf_op jit(solution)/shard_map/ppermute | solution.py:578
  64.8 44.6 %copy-start.2 = (bf16[8,4,128,256]{3,2,1,0:T(8,128)(2,1)}, bf16[8,4,128,256]{3,2,1,0:T(8,128)(2,1)S(1)}, u32[]{:S(2)}) copy-start(bf16[8,4,128,256]{3,2,1,0:T(8,128)(2,1)S(1)} %all-to-all-done.refs_0_) | copy-start | bytes 6291460
  64.8 44.6 %collective-permute-start.7 = (bf16[8,4,128,256]{3,2,1,0:T(8,128)(2,1)S(1)}, bf16[8,4,128,256]{3,2,1,0:T(8,128)(2,1)}, u32[]{:S(2)}, u32[]{:S(2)}) collective-permute-start(bf16[8,4,128,256]{3,2,1,0:T(8,128)(2,1)S(1)} %all-to-all-done.refs_0_), channel_id=1, source_target_pairs={{4,0},{0,4},{12,8},{8,12},{20,16},{16,20},{28,24},{24,28},{5,1},{1... | collective-permute-start | bytes 6291464 | tf_op jit(solution)/shard_map/ppermute | solution.py:578
  65.3 3.8 %collective-permute-start = (s32[56]{0:T(128)S(1)}, s32[56]{0:T(128)S(1)}, u32[]{:S(2)}, u32[]{:S(2)}) collective-permute-start(s32[56]{0:T(128)S(1)} %pad_add_fusion.1), channel_id=1, source_target_pairs={{4,0},{8,4},{12,8},{16,12},{20,16},{24,20},{28,24},{0,28},{5,1},{9... | collective-permute-start | bytes 680 | tf_op jit(solution)/shard_map/ppermute | solution.py:58
  66.9 4.5 %collective-permute-start.1 = (s32[56]{0:T(128)S(1)}, s32[56]{0:T(128)S(1)}, u32[]{:S(2)}, u32[]{:S(2)}) collective-permute-start(s32[56]{0:T(128)S(1)} %pad_add_fusion.1), channel_id=1, source_target_pairs={{8,0},{12,4},{16,8},{20,12},{24,16},{28,20},{0,24},{4,28},{9,1},{1... | collective-permute-start | bytes 680 | tf_op jit(solution)/shard_map/ppermute | solution.py:58
  67.4 4.3 %collective-permute-start.2 = (s32[56]{0:T(128)S(1)}, s32[56]{0:T(128)S(1)}, u32[]{:S(2)}, u32[]{:S(2)}) collective-permute-start(s32[56]{0:T(128)S(1)} %pad_add_fusion.1), channel_id=1, source_target_pairs={{12,0},{16,4},{20,8},{24,12},{28,16},{0,20},{4,24},{8,28},{13,1},{... | collective-permute-start | bytes 680 | tf_op jit(solution)/shard_map/ppermute | solution.py:58
  69.1 3.7 %collective-permute-start.3 = (s32[56]{0:T(128)S(1)}, s32[56]{0:T(128)S(1)}, u32[]{:S(2)}, u32[]{:S(2)}) collective-permute-start(s32[56]{0:T(128)S(1)} %pad_add_fusion.1), channel_id=1, source_target_pairs={{16,0},{20,4},{24,8},{28,12},{0,16},{4,20},{8,24},{12,28},{17,1},{... | collective-permute-start | bytes 680 | tf_op jit(solution)/shard_map/ppermute | solution.py:58
  71.3 3.0 %collective-permute-start.4 = (s32[56]{0:T(128)S(1)}, s32[56]{0:T(128)S(1)}, u32[]{:S(2)}, u32[]{:S(2)}) collective-permute-start(s32[56]{0:T(128)S(1)} %pad_add_fusion.1), channel_id=1, source_target_pairs={{20,0},{24,4},{28,8},{0,12},{4,16},{8,20},{12,24},{16,28},{21,1},{... | collective-permute-start | bytes 680 | tf_op jit(solution)/shard_map/ppermute | solution.py:58
  71.7 3.6 %collective-permute-start.5 = (s32[56]{0:T(128)S(1)}, s32[56]{0:T(128)S(1)}, u32[]{:S(2)}, u32[]{:S(2)}) collective-permute-start(s32[56]{0:T(128)S(1)} %pad_add_fusion.1), channel_id=1, source_target_pairs={{24,0},{28,4},{0,8},{4,12},{8,16},{12,20},{16,24},{20,28},{25,1},{... | collective-permute-start | bytes 680 | tf_op jit(solution)/shard_map/ppermute | solution.py:58
  72.8 3.0 %collective-permute-start.6 = (s32[56]{0:T(128)S(1)}, s32[56]{0:T(128)S(1)}, u32[]{:S(2)}, u32[]{:S(2)}) collective-permute-start(s32[56]{0:T(128)S(1)} %pad_add_fusion.1), channel_id=1, source_target_pairs={{28,0},{0,4},{4,8},{8,12},{12,16},{16,20},{20,24},{24,28},{29,1},{... | collective-permute-start | bytes 680 | tf_op jit(solution)/shard_map/ppermute | solution.py:58
  126.6 154.4 %all-to-all-start.2 = ((bf16[32,256,128]{2,1,0:T(8,128)(2,1)}), bf16[32,256,128]{2,1,0:T(8,128)(2,1)S(1)}, u32[]{:S(2)}, u32[]{:S(2)}) async-start(bf16[32,256,128]{2,1,0:T(8,128)(2,1)} %attend_values.1), calls=%async_computation.2 | async-start | bytes 4194304 | tf_op jit(solution)/shard_map/all_to_all | solution.py:705
  139.7 57.4 %collective-permute-start.9 = (bf16[256,2048]{1,0:T(8,128)(2,1)S(1)}, bf16[256,2048]{1,0:T(8,128)(2,1)S(1)}, u32[]{:S(2)}, u32[]{:S(2)}) collective-permute-start(bf16[256,2048]{1,0:T(8,128)(2,1)S(1)} %constant_dynamic-slice_fusion), channel_id=1, source_target_pairs={{1,0},{2,1},{3,2},{0,3},{5,4},{6,5},{7,6},{4,7},{9,8},{10,9},{11,1... | collective-permute-start | bytes 3145736 | tf_op jit(solution)/shard_map/ppermute | solution.py:586
  143.0 133.6 %collective-permute-start.11 = (bf16[256,2048]{1,0:T(8,128)(2,1)S(1)}, bf16[256,2048]{1,0:T(8,128)(2,1)S(1)}, u32[]{:S(2)}, u32[]{:S(2)}) collective-permute-start(bf16[256,2048]{1,0:T(8,128)(2,1)S(1)} %constant_dynamic-slice_fusion), channel_id=1, source_target_pairs={{2,0},{3,1},{0,2},{1,3},{6,4},{7,5},{4,6},{5,7},{10,8},{11,9},{8,1... | collective-permute-start | bytes 3145736 | tf_op jit(solution)/shard_map/ppermute | solution.py:586
  143.0 133.6 %collective-permute-start.13 = (bf16[256,2048]{1,0:T(8,128)(2,1)S(1)}, bf16[256,2048]{1,0:T(8,128)(2,1)S(1)}, u32[]{:S(2)}, u32[]{:S(2)}) collective-permute-start(bf16[256,2048]{1,0:T(8,128)(2,1)S(1)} %constant_dynamic-slice_fusion), channel_id=1, source_target_pairs={{3,0},{0,1},{1,2},{2,3},{7,4},{4,5},{5,6},{6,7},{11,8},{8,9},{9,10... | collective-permute-start | bytes 3145736 | tf_op jit(solution)/shard_map/ppermute | solution.py:586
  197.1 83.9 %copy-start.8 = (bf16[256,2048]{1,0:T(8,128)(2,1)}, bf16[256,2048]{1,0:T(8,128)(2,1)S(1)}, u32[]{:S(2)}) copy-start(bf16[256,2048]{1,0:T(8,128)(2,1)S(1)} %collective-permute-done.9.refs_0_) | copy-start | bytes 3145732
  197.1 80.1 %collective-permute-start.10 = (bf16[256,2048]{1,0:T(8,128)(2,1)S(1)}, bf16[256,2048]{1,0:T(8,128)(2,1)S(1)}, u32[]{:S(2)}, u32[]{:S(2)}) collective-permute-start(bf16[256,2048]{1,0:T(8,128)(2,1)S(1)} %collective-permute-done.9.refs_0_), channel_id=1, source_target_pairs={{4,0},{0,4},{12,8},{8,12},{20,16},{16,20},{28,24},{24,28},{5,1},{1... | collective-permute-start | bytes 3145736 | tf_op jit(solution)/shard_map/ppermute | solution.py:578
  276.6 2.7 collective-permute-start.12
  276.7 4.3 %collective-permute-start.14 = (bf16[256,2048]{1,0:T(8,128)(2,1)S(1)}, bf16[256,2048]{1,0:T(8,128)(2,1)}, u32[]{:S(2)}, u32[]{:S(2)}) collective-permute-start(bf16[256,2048]{1,0:T(8,128)(2,1)S(1)} %collective-permute-done.13.refs_4_), channel_id=1, source_target_pairs={{4,0},{0,4},{12,8},{8,12},{20,16},{16,20},{28,24},{24,28},{5,1},{1... | collective-permute-start | bytes 3145736 | tf_op jit(solution)/shard_map/ppermute | solution.py:578
  (7 other events, 20.8 us)

commit v4 on v3

--- a/solution.py
+++ b/solution.py
@@ -15,8 +15,10 @@
 LEAD, TAIL = 2, 14
 PREP_STEP = 4
 CHUNK = 8
+OUT_RING, IN_RING = 4, 8
 VALUE_STEP = 4
 FINISH_STEP = 4
+PROJECT_TILE = 512
 BF16 = jnp.bfloat16
 F32 = jnp.float32
 SMEM = pl.BlockSpec(memory_space=pltpu.SMEM)
@@ -74,28 +76,34 @@
         lax.fori_loop(0, nblk, clear, 0)
         per = shards * slots
 
-        def visit(pair, _):
-            shard = pair // per
-            rest = pair - shard * per
-            other = rest // slots
-            slot = rest - other * slots
+        def from_shard(shard, _):
             base = lax.rem(shard + shards - spot_ref[2], shards) * (2 * per + shards)
-            a = shard * blocks + tab_ref[base + rest]
-            b = other * blocks + tab_ref[base + per + rest]
-            live = slot < tab_ref[base + 2 * per + other]
-
-            @pl.when(live & (bucket_ref[a] == bucket_ref[b]))
-            def _():
-                at = fill[a]
-                lists[a * cap + at] = b
-                fill[a] = at + 1
-                bt = fill[b]
-                lists[b * cap + bt] = a
-                fill[b] = bt + 1
-
+
+            def to_shard(other, _):
+                at = base + other * slots
+
+                def visit(slot, _):
+                    a = shard * blocks + tab_ref[at + slot]
+                    b = other * blocks + tab_ref[at + per + slot]
+
+                    @pl.when(bucket_ref[a] == bucket_ref[b])
+                    def _():
+                        end_a, end_b = fill[a], fill[b]
+                        lists[a * cap + end_a] = b
+                        lists[b * cap + end_b] = a
+                        fill[a] = end_a + 1
+                        fill[b] = end_b + 1
+
+                    return 0
+
+                live = jnp.minimum(tab_ref[base + 2 * per + other], slots)
+                lax.fori_loop(0, live, visit, 0)
+                return 0
+
+            lax.fori_loop(0, shards, to_shard, 0)
             return 0
 
-        lax.fori_loop(0, shards * per, visit, 0)
+        lax.fori_loop(0, shards, from_shard, 0)
 
         for i in range(LEAD):
             unit_ref[i] = units
@@ -339,20 +347,16 @@
     for copy in copies:
         copy.wait()
 
-    ones = jnp.ones((HD, HD), BF16)
     contract = (((1,), (1,)), ((), ()))
+    fold = math.log2(math.e) ** -2
 
     def prepare(i, _):
         for k in range(PREP_STEP):
             b = i * PREP_STEP + k
             wide = q_ref[b // groups, lax.rem(b, groups)].astype(F32)
-            square = wide * wide
-            high = square.astype(BF16)
-            low = (square - high.astype(F32)).astype(BF16)
-            total = jnp.dot(high, ones, preferred_element_type=F32)
-            total += jnp.dot(low, ones, preferred_element_type=F32)
-            scale = math.log2(math.e) / math.sqrt(HD)
-            inv_ref[b] = lax.rsqrt(total * (1.0 / HD) + 1e-06) * scale
+            total = jnp.sum(wide * wide, axis=1, keepdims=True)
+            inv = lax.rsqrt(total * fold + 1e-06 * HD * fold)
+            inv_ref[b] = jnp.broadcast_to(inv, (BLOCK, HD))
         return 0
 
     lax.fori_loop(0, units * groups // PREP_STEP, prepare, 0)
@@ -398,8 +402,10 @@
             sum_ref[unit, :, lane] = total[:, lane] + jnp.sum(prob, axis=0)
             p_buf[slot, at, :, lane] = prob.reshape(BLOCK, HD).astype(BF16)
 
+    ring = p_buf.shape[0]
+
     def out_copy(chunk):
-        slot = lax.rem(chunk, 2)
+        slot = lax.rem(chunk, ring)
         return pltpu.make_async_copy(
             p_buf.at[slot], p_out.at[pl.ds(chunk * CHUNK, CHUNK)], p_sem.at[slot]
         )
@@ -409,11 +415,11 @@
     chunks = (count_ref[0] + CHUNK - 1) // CHUNK
 
     def chunk_step(chunk, _):
-        slot = lax.rem(chunk, 2)
-
-        @pl.when(chunk >= 2)
+        slot = lax.rem(chunk, ring)
+
+        @pl.when(chunk >= ring)
         def _():
-            out_copy(chunk - 2).wait()
+            out_copy(chunk - ring).wait()
 
         def step(k, _):
             j = chunk * CHUNK + 2 * k
@@ -428,7 +434,7 @@
         return 0
 
     lax.fori_loop(0, chunks, chunk_step, 0)
-    for back in (2, 1):
+    for back in range(ring, 0, -1):
 
         @pl.when(chunks >= back)
         def _():
@@ -458,9 +464,9 @@
             pltpu.VMEM((BLOCK, rows), F32),
             pltpu.VMEM((BLOCK, rows), F32),
             *[pltpu.VMEM((8, rows), F32)] * 3,
-            pltpu.VMEM((2, CHUNK, BLOCK, rows), BF16),
+            pltpu.VMEM((OUT_RING, CHUNK, BLOCK, rows), BF16),
             pltpu.SemaphoreType.DMA,
-            pltpu.SemaphoreType.DMA((2,)),
+            pltpu.SemaphoreType.DMA((OUT_RING,)),
         ],
         cost_estimate=pl.CostEstimate(
             flops=2 * work * rows * BLOCK * HD,
@@ -490,13 +496,20 @@
     for copy in copies:
         copy.start()
 
+    ring = p_buf.shape[0]
+    chunks = (count_ref[0] + CHUNK - 1) // CHUNK
+
     def in_copy(chunk):
-        slot = lax.rem(chunk, 2)
+        slot = lax.rem(chunk, ring)
         return pltpu.make_async_copy(
             p_in.at[pl.ds(chunk * CHUNK, CHUNK)], p_buf.at[slot], p_sem.at[slot]
         )
 
-    in_copy(0).start()
+    for ahead in range(ring - 1):
+
+        @pl.when(ahead < chunks)
+        def _():
+            in_copy(ahead).start()
 
     def clear(unit, _):
         acc_ref[unit] = jnp.zeros(acc_ref.shape[1:], F32)
@@ -515,14 +528,12 @@
         )
         acc_ref[unit] = acc_ref[unit] * scale_ref[pl.ds(j, 1), :] + part
 
-    chunks = (count_ref[0] + CHUNK - 1) // CHUNK
-
     def chunk_step(chunk, _):
-        slot = lax.rem(chunk, 2)
-
-        @pl.when(chunk + 1 < chunks)
+        slot = lax.rem(chunk, ring)
+
+        @pl.when(chunk + ring - 1 < chunks)
         def _():
-            in_copy(chunk + 1).start()
+            in_copy(chunk + ring - 1).start()
 
         in_copy(chunk).wait()
 
@@ -560,9 +571,9 @@
         scratch_shapes=[
             pltpu.VMEM((units, groups, HD, rows), BF16),
             pltpu.VMEM((units + 1, HD, rows), F32),
-            pltpu.VMEM((2, CHUNK, BLOCK, rows), BF16),
+            pltpu.VMEM((IN_RING, CHUNK, BLOCK, rows), BF16),
             pltpu.SemaphoreType.DMA,
-            pltpu.SemaphoreType.DMA((2,)),
+            pltpu.SemaphoreType.DMA((IN_RING,)),
         ],
         cost_estimate=pl.CostEstimate(
             flops=2 * work * rows * BLOCK * HD,
@@ -578,13 +589,18 @@
     return lax.ppermute(x, "seq", pairs)
 
 
-def gather_weights(w_out, groups, member):
+def ring_weights(w_out, groups, member):
     count = lax.axis_size("head")
+    here = lax.axis_index("head")
     share = w_out.shape[0] // groups
-    mine = lax.dynamic_slice_in_dim(w_out, member * share, share, 0)
+    up = down = lax.dynamic_slice_in_dim(w_out, member * share, share, 0)
+    ups, downs = {}, {}
+    for k in range(1, count):
+        up = lax.ppermute(up, "head", [(i, i + 1) for i in range(k - 1, count - 1)])
+        down = lax.ppermute(down, "head", [(i, i - 1) for i in range(1, count - k + 1)])
+        ups[k], downs[k] = up, down
     return [
-        lax.ppermute(mine, "head", [((i + r) % count, i) for i in range(count)])
-        for r in range(1, count)
+        jnp.where(here + r < count, downs[r], ups[count - r]) for r in range(1, count)
     ]
 
 
@@ -596,11 +612,12 @@
     tile = w_buf.shape[2]
     share = pieces[0].shape[0]
     depth = heads * HD
-    step, steps = pl.program_id(0), pl.num_programs(0)
-
-    def copies(i):
-        slot = lax.rem(i, 2)
-        cols = pl.ds(pl.multiple_of(i * tile, tile), tile)
+    step = pl.program_id(0)
+
+    def copies(slot):
+        cols = pl.ds(slot * tile, tile)
+        if not isinstance(slot, int):
+            cols = pl.ds(pl.multiple_of(slot * tile, tile), tile)
         out = [
             pltpu.make_async_copy(
                 w_ref.at[:, cols],
@@ -622,30 +639,24 @@
 
     @pl.when(step == 0)
     def _():
-        for copy in copies(step):
-            copy.start()
+        for i in range(w_buf.shape[0]):
+            for copy in copies(i):
+                copy.start()
         for z_at in range(spans):
             for h in range(heads):
                 at = (z_at * heads + h) * HD
                 for g in range(groups):
                     wide_ref[g * rows : (g + 1) * rows, at : at + HD] = x_ref[h, g, z_at]
 
-    @pl.when(step + 1 < steps)
-    def _():
-        for copy in copies(step + 1):
-            copy.start()
-
     for copy in copies(step):
         copy.wait()
-    o_ref[...] = jnp.dot(
-        wide_ref[...], w_buf[lax.rem(step, 2)], preferred_element_type=F32
-    ).astype(BF16)
+    o_ref[...] = jnp.dot(wide_ref[...], w_buf[step], preferred_element_type=F32).astype(BF16)
 
 
 def project(spot, mixed, w_out, pieces):
     _, groups, spans, rows, _ = mixed.shape
     depth, width = w_out.shape
-    tile = min(512, width)
+    tile = min(PROJECT_TILE, width)
     out_rows = groups * rows
     return pl.pallas_call(
         project_kernel,
@@ -655,8 +666,8 @@
         out_shape=jax.ShapeDtypeStruct((out_rows, width), BF16),
         scratch_shapes=[
             pltpu.VMEM((out_rows, spans * depth), BF16),
-            pltpu.VMEM((2, spans * depth, tile), BF16),
-            pltpu.SemaphoreType.DMA((2,)),
+            pltpu.VMEM((width // tile, spans * depth, tile), BF16),
+            pltpu.SemaphoreType.DMA((width // tile,)),
         ],
         cost_estimate=pl.CostEstimate(
             flops=2 * out_rows * spans * depth * width,
@@ -664,7 +675,7 @@
             transcendentals=0,
         ),
         name="project",
-    )(spot, mixed, w_out, *pieces)
+    )(spot, pltpu.with_memory_space_constraint(mixed, pltpu.VMEM), w_out, *pieces)
 
 
 def body(qk, values, bucket, pair_row, pair_col, pair_count, w_out):
@@ -679,7 +690,7 @@
     head, member = here // groups, lax.rem(here, groups)
     spot = jnp.stack([member, z, here]).astype(jnp.int32)
 
-    shares = gather_weights(w_out, groups, member)
+    shares = ring_weights(w_out, groups, member)
     units = shards * spans
     rows = tokens // spans // groups
     turned = rows == BLOCK
@@ -699,16 +710,19 @@
     )
     if turned:
         weights = attend_scores(spot, jobs, q_pieces)
+        v_pieces = [pltpu.with_memory_space_constraint(x, pltpu.HBM) for x in v_pieces]
         attn = attend_values(spot, jobs, v_pieces, *weights)
     else:
         attn = attend(spot, jobs, q_pieces, v_pieces)
     mixed = lax.all_to_all(attn, ("seq", "head"), 0, 0, tiled=True)
     mixed = mixed.reshape(heads, groups, spans, rows, HD)
     weights = []
+    shares = [pltpu.with_memory_space_constraint(x, pltpu.HBM) for x in shares]
     for piece in shares:
         weights += [piece] + [
             group_shift(piece, shards, groups, k) for k in range(1, groups)
         ]
+    weights = [pltpu.with_memory_space_constraint(x, pltpu.HBM) for x in weights]
     return project(spot, mixed, w_out, weights)
 
 

time: 295 us -> 260 us (0.88)
  waiting for transfers between devices: 186 us -> 155 us
  Pallas kernels: 67.6 us -> 57.6 us
  starting transfers between devices: 30.5 us -> 34.8 us
    ppermute x3 -> x6, waiting for transfers between devices: 133 us -> 89.1 us  [the longest x3 89.1 us: ring_weights(): lax.ppermute(down, 'head', [(i, i - 1) for i in range(1, count - k + 1)])]
    ppermute x7, waiting for transfers between devices: 5.09 us -> 19.3 us  [gather_tables(): lax.ppermute(mine, 'seq', [((i + r) % shards, i) for i in range(shards)])]
    ppermute x3 -> x6, starting transfers between devices: 4.45 us -> 11.7 us  [the longest x3 7.8 us: ring_weights(): up = lax.ppermute(up, 'head', [(i, i + 1) for i in range(k - 1, count - 1)])]
    pallas_call x1, Pallas kernels: 10.4 us -> 5.89 us  [job_lists(): pl.pallas_call(kernel, in_specs=[SMEM, SMEM, SMEM], out_specs=[SMEM, SMEM...]
  transfers between devices with their start and end apart: 18 -> 21, of which waited for: 11 -> 12; matrix products, arithmetic and copies ran while one was open for 1% -> 2% of each run, Pallas kernels for 13% -> 18%
where the time goes in v4:
time: 260 us; the launch traced here: 257 us
  waiting for transfers between devices  155 us (60%)
  Pallas kernels  57.6 us (22%)
  starting transfers between devices  34.8 us (13%)
  local copies, waits for them, and re-layouts  6.9 us (3%)
  other arithmetic  2.67 us (1%)
    ppermute x3, waiting for transfers between devices, ring_weights(): lax.ppermute(down, 'head', [(i, i - 1) for i in range(1, count - k + 1)])  89.1 us
    all_to_all x2, waiting for transfers between devices, send(): got = lax.all_to_all(sent, 'seq', 0, 0, tiled=True)  45.9 us
    pallas_call x1, Pallas kernels, attend_scores(): pl.pallas_call(functools.partial(scores_kernel, groups), in_specs=[SMEM]...  21.2 us
    ppermute x7, waiting for transfers between devices, gather_tables(): lax.ppermute(mine, 'seq', [((i + r) % shards, i) for i in range(shards)])  19.3 us
    pallas_call x1, Pallas kernels, attend_values(): pl.pallas_call(functools.partial(values_kernel, groups), in_specs=[SMEM]...  14.3 us
    all_to_all x1, starting transfers between devices, body(): mixed = lax.all_to_all(attn, ('seq', 'head'), 0, 0, tiled=True)  10.3 us
    all_to_all x2, starting transfers between devices, send(): got = lax.all_to_all(sent, 'seq', 0, 0, tiled=True)  9.28 us
    pallas_call x1, Pallas kernels, project(): pl.pallas_call(project_kernel, grid=(width // tile,), in_specs=[SMEM, pl....  8.17 us
  transfers between devices with their start and end apart: 21, of which 12 were waited for; matrix products, arithmetic and copies ran while one was open for 2% of the time, Pallas kernels for 18%

profile of v4, /device:TPU:2, one launch (start us, length us, event | category | flops | bytes accessed | tf_op | source)
XLA Modules:
  0.0 257.3 jit_solution(7775719607958241241)
XLA Ops:
  0.0 3.9 %pack.3 = bf16[4,2,4,256,128]{4,3,2,1,0:T(8,128)(2,1)} custom-call(bf16[2048,512]{1,0:T(8,128)(2,1)} %x_ref.3), custom_call_target="tpu_custom_call" | custom-call | bytes 4194304 | tf_op jit(solution)/shard_map/pack/pallas_call | solution.py:42
  3.9 4.3 %all-to-all-start.1 = ((bf16[8,4,256,128]{3,2,1,0:T(8,128)(2,1)}), bf16[8,4,256,128]{3,2,1,0:T(8,128)(2,1)S(1)}, u32[]{:S(2)}, u32[]{:S(2)}) async-start(bf16[8,4,256,128]{3,2,1,0:T(8,128)(2,1)} %bitcast.11), calls=%async_computation.1 | async-start | bytes 4194304 | tf_op jit(solution)/shard_map/all_to_all | solution.py:701
  8.2 4.1 %pack.2 = bf16[4,2,4,128,256]{4,3,2,1,0:T(8,128)(2,1)} custom-call(bf16[2048,512]{1,0:T(8,128)(2,1)} %x_ref.2), custom_call_target="tpu_custom_call" | custom-call | bytes 4194304 | tf_op jit(solution)/shard_map/pack/pallas_call | solution.py:42
  12.3 21.0 %all-to-all-done.1.refs_0_ = bf16[8,4,256,128]{3,2,1,0:T(8,128)(2,1)S(1)} async-done(((bf16[8,4,256,128]{3,2,1,0:T(8,128)(2,1)}), bf16[8,4,256,128]{3,2,1,0:T(8,128)(2,1)S(1)}, u32[]{:S(2)}, u32[]{:S(2)}) %all-to-all-start.1) | async-done | bytes 2097184 | tf_op jit(solution)/shard_map/all_to_all | solution.py:701
  34.6 5.0 %all-to-all-start = ((bf16[8,4,128,256]{3,2,1,0:T(8,128)(2,1)}), bf16[8,4,128,256]{3,2,1,0:T(8,128)(2,1)S(1)}, u32[]{:S(2)}, u32[]{:S(2)}) async-start(bf16[8,4,128,256]{3,2,1,0:T(8,128)(2,1)} %bitcast.10), calls=%async_computation | async-start | bytes 4194304 | tf_op jit(solution)/shard_map/all_to_all | solution.py:701
  39.9 24.9 %all-to-all-done.refs_0_ = bf16[8,4,128,256]{3,2,1,0:T(8,128)(2,1)S(1)} async-done(((bf16[8,4,128,256]{3,2,1,0:T(8,128)(2,1)}), bf16[8,4,128,256]{3,2,1,0:T(8,128)(2,1)S(1)}, u32[]{:S(2)}, u32[]{:S(2)}) %all-to-all-start) | async-done | bytes 2097184 | tf_op jit(solution)/shard_map/all_to_all | solution.py:701
  64.9 2.0 constant_dynamic-slice_fusion
  66.9 4.5 %collective-permute-start.10 = (bf16[256,2048]{1,0:T(8,128)(2,1)S(1)}, bf16[256,2048]{1,0:T(8,128)(2,1)}, u32[]{:S(2)}, u32[]{:S(2)}) collective-permute-start(bf16[256,2048]{1,0:T(8,128)(2,1)S(1)} %constant_dynamic-slice_fusion), channel_id=1, source_target_pairs={{0,1},{1,2},{2,3},{4,5},{5,6},{6,7},{8,9},{9,10},{10,11},{12,13},{... | collective-permute-start | bytes 3145736 | tf_op jit(solution)/shard_map/ppermute | solution.py:599
  75.9 3.5 %collective-permute-done.1 = s32[56]{0:T(128)S(1)} collective-permute-done((s32[56]{0:T(128)S(1)}, s32[56]{0:T(128)S(1)}, u32[]{:S(2)}, u32[]{:S(2)}) %collective-permute-start.1) | collective-permute-done | bytes 256 | tf_op jit(solution)/shard_map/ppermute | solution.py:60
  80.3 3.0 %collective-permute-done.2 = s32[56]{0:T(128)S(1)} collective-permute-done((s32[56]{0:T(128)S(1)}, s32[56]{0:T(128)S(1)}, u32[]{:S(2)}, u32[]{:S(2)}) %collective-permute-start.2) | collective-permute-done | bytes 256 | tf_op jit(solution)/shard_map/ppermute | solution.py:60
  83.9 3.0 %collective-permute-done.3 = s32[56]{0:T(128)S(1)} collective-permute-done((s32[56]{0:T(128)S(1)}, s32[56]{0:T(128)S(1)}, u32[]{:S(2)}, u32[]{:S(2)}) %collective-permute-start.3) | collective-permute-done | bytes 256 | tf_op jit(solution)/shard_map/ppermute | solution.py:60
  86.9 3.0 %collective-permute-done.4 = s32[56]{0:T(128)S(1)} collective-permute-done((s32[56]{0:T(128)S(1)}, s32[56]{0:T(128)S(1)}, u32[]{:S(2)}, u32[]{:S(2)}) %collective-permute-start.4) | collective-permute-done | bytes 256 | tf_op jit(solution)/shard_map/ppermute | solution.py:60
  90.4 3.1 %collective-permute-done.5 = s32[56]{0:T(128)S(1)} collective-permute-done((s32[56]{0:T(128)S(1)}, s32[56]{0:T(128)S(1)}, u32[]{:S(2)}, u32[]{:S(2)}) %collective-permute-start.5) | collective-permute-done | bytes 256 | tf_op jit(solution)/shard_map/ppermute | solution.py:60
  94.0 2.4 collective-permute-done.6
  97.1 5.9 %job_lists.1 = (s32[1]{0:T(128)}, s32[432]{0:T(512)}, s32[432]{0:T(512)}) custom-call(s32[448]{0:T(512)} %concatenate.8.tab_ref, s32[64]{0:T(128)} %dynamic-slice_bitcast_fusion.bucket_ref, s32[3]{0:T(128)} %pad_add_fusion.spot_ref), custom_call_target="tpu_custom_call" | custom-call | bytes 33554432 | tf_op jit(solution)/shard_map/job_lists/pallas_call | solution.py:132
  103.0 1.6 collective-permute-start.11
  104.7 21.2 %attend_scores.1 = (bf16[432,256,256]{2,1,0:T(8,128)(2,1)}, f32[432,256]{1,0:T(8,128)}, f32[33,8,256]{2,1,0:T(8,128)}) custom-call(s32[3]{0:T(128)} %pad_add_fusion.spot_ref, s32[1]{0:T(128)} %get-tuple-element.11.count_ref, s32[432]{0:T(512)} %get-tuple-element.12.unit_ref, s32[432]{0:T(512)} %get-tuple-element.13.key_ref, ...), custom_call_target="tpu_custom_call" | custom-call | flops 1610612736 | bytes 16777216 | tf_op jit(solution)/shard_map/attend_scores/pallas_call | solution.py:452
  125.9 14.3 %attend_values.1 = bf16[32,256,128]{2,1,0:T(8,128)(2,1)} custom-call(s32[3]{0:T(128)} %pad_add_fusion.spot_ref, s32[1]{0:T(128)} %get-tuple-element.11.count_ref, s32[432]{0:T(512)} %get-tuple-element.12.unit_ref, s32[432]{0:T(512)} %get-tuple-element.13.key_ref, bf16[8,4,128,256]{3,2,1,0:T(8,128)(2,1)} %copy-done.2, ...), custom_call_target="tpu_custom_call" | custom-call | flops 1610612736 | bytes 16777216 | tf_op jit(solution)/shard_map/attend_values/pallas_call | solution.py:566
  140.2 10.3 %all-to-all-start.2 = ((bf16[32,256,128]{2,1,0:T(8,128)(2,1)}), bf16[32,256,128]{2,1,0:T(8,128)(2,1)S(1)}, u32[]{:S(2)}, u32[]{:S(2)}) async-start(bf16[32,256,128]{2,1,0:T(8,128)(2,1)} %attend_values.1), calls=%async_computation.2 | async-start | bytes 4194304 | tf_op jit(solution)/shard_map/all_to_all | solution.py:717
  151.8 1.7 collective-permute-start.12
  153.5 55.8 %collective-permute-done.14 = bf16[256,2048]{1,0:T(8,128)(2,1)S(1)} collective-permute-done((bf16[256,2048]{1,0:T(8,128)(2,1)}, bf16[256,2048]{1,0:T(8,128)(2,1)S(1)}, u32[]{:S(2)}, u32[]{:S(2)}) %collective-permute-start.14) | collective-permute-done | bytes 1048608 | tf_op jit(solution)/shard_map/ppermute | solution.py:600
  210.8 1.6 broadcast_select_fusion.2.refs_0_
  212.7 33.4 %collective-permute-done.16 = bf16[256,2048]{1,0:T(8,128)(2,1)S(1)} collective-permute-done((bf16[256,2048]{1,0:T(8,128)(2,1)S(1)}, bf16[256,2048]{1,0:T(8,128)(2,1)S(1)}, u32[]{:S(2)}, u32[]{:S(2)}) %collective-permute-start.16) | collective-permute-done | bytes 1048608 | tf_op jit(solution)/shard_map/ppermute | solution.py:600
  249.2 8.2 %project.1 = bf16[512,2048]{1,0:T(8,128)(2,1)} custom-call(s32[3]{0:T(128)} %pad_add_fusion.spot_ref, bf16[4,2,4,256,128]{4,3,2,1,0:T(8,128)(2,1)S(1)} %bitcast.9, bf16[512,2048]{1,0:T(8,128)(2,1)} %w_ref.1, bf16[256,2048]{1,0:T(8,128)(2,1)} %copy-done.5, bf16[256,2048]{1,0:T(8,128)(2,1)} %copy-done.11, bf16[256,2048]{1,0:T(8,128)(2,1)} %copy-done.4, ...), custom_call_target="tpu_custom_call" | custom-call | flops 4294967296 | bytes 8388608 | tf_op jit(solution)/shard_map/project/pallas_call | solution.py:661
  (60 shorter events, 15.5 us)
Async XLA Ops:
  0.0 89.9 %copy-start = (s32[64,16]{0,1:T(8,128)S(1)}, s32[64,16]{0,1:T(8,128)}, u32[]{:S(2)}) copy-start(s32[64,16]{0,1:T(8,128)} %param.9) | copy-start | bytes 12292
  3.9 29.4 %all-to-all-start.1 = ((bf16[8,4,256,128]{3,2,1,0:T(8,128)(2,1)}), bf16[8,4,256,128]{3,2,1,0:T(8,128)(2,1)S(1)}, u32[]{:S(2)}, u32[]{:S(2)}) async-start(bf16[8,4,256,128]{3,2,1,0:T(8,128)(2,1)} %bitcast.11), calls=%async_computation.1 | async-start | bytes 4194304 | tf_op jit(solution)/shard_map/all_to_all | solution.py:701
  34.6 30.1 %all-to-all-start = ((bf16[8,4,128,256]{3,2,1,0:T(8,128)(2,1)}), bf16[8,4,128,256]{3,2,1,0:T(8,128)(2,1)S(1)}, u32[]{:S(2)}, u32[]{:S(2)}) async-start(bf16[8,4,128,256]{3,2,1,0:T(8,128)(2,1)} %bitcast.10), calls=%async_computation | async-start | bytes 4194304 | tf_op jit(solution)/shard_map/all_to_all | solution.py:701
  39.7 65.0 %collective-permute-start.8 = (bf16[8,4,256,128]{3,2,1,0:T(8,128)(2,1)}, bf16[8,4,256,128]{3,2,1,0:T(8,128)(2,1)}, u32[]{:S(2)}, u32[]{:S(2)}) collective-permute-start(bf16[8,4,256,128]{3,2,1,0:T(8,128)(2,1)} %copy-done.3), channel_id=1, source_target_pairs={{4,0},{0,4},{12,8},{8,12},{20,16},{16,20},{28,24},{24,28},{5,1},{1... | collective-permute-start | bytes 6291464 | tf_op jit(solution)/shard_map/ppermute | solution.py:589
  64.8 61.1 %copy-start.2 = (bf16[8,4,128,256]{3,2,1,0:T(8,128)(2,1)}, bf16[8,4,128,256]{3,2,1,0:T(8,128)(2,1)S(1)}, u32[]{:S(2)}) copy-start(bf16[8,4,128,256]{3,2,1,0:T(8,128)(2,1)S(1)} %all-to-all-done.refs_0_) | copy-start | bytes 6291460
  64.8 61.1 %collective-permute-start.7 = (bf16[8,4,128,256]{3,2,1,0:T(8,128)(2,1)S(1)}, bf16[8,4,128,256]{3,2,1,0:T(8,128)(2,1)}, u32[]{:S(2)}, u32[]{:S(2)}) collective-permute-start(bf16[8,4,128,256]{3,2,1,0:T(8,128)(2,1)S(1)} %all-to-all-done.refs_0_), channel_id=1, source_target_pairs={{4,0},{0,4},{12,8},{8,12},{20,16},{16,20},{28,24},{24,28},{5,1},{1... | collective-permute-start | bytes 6291464 | tf_op jit(solution)/shard_map/ppermute | solution.py:589
  66.9 36.2 %collective-permute-start.10 = (bf16[256,2048]{1,0:T(8,128)(2,1)S(1)}, bf16[256,2048]{1,0:T(8,128)(2,1)}, u32[]{:S(2)}, u32[]{:S(2)}) collective-permute-start(bf16[256,2048]{1,0:T(8,128)(2,1)S(1)} %constant_dynamic-slice_fusion), channel_id=1, source_target_pairs={{0,1},{1,2},{2,3},{4,5},{5,6},{6,7},{8,9},{9,10},{10,11},{12,13},{... | collective-permute-start | bytes 3145736 | tf_op jit(solution)/shard_map/ppermute | solution.py:599
  71.4 79.1 %collective-permute-start.9 = (bf16[256,2048]{1,0:T(8,128)(2,1)S(1)}, bf16[256,2048]{1,0:T(8,128)(2,1)}, u32[]{:S(2)}, u32[]{:S(2)}) collective-permute-start(bf16[256,2048]{1,0:T(8,128)(2,1)S(1)} %constant_dynamic-slice_fusion), channel_id=1, source_target_pairs={{1,0},{2,1},{3,2},{5,4},{6,5},{7,6},{9,8},{10,9},{11,10},{13,12},{... | collective-permute-start | bytes 3145736 | tf_op jit(solution)/shard_map/ppermute | solution.py:600
  73.1 1.9 collective-permute-start
  75.0 4.5 %collective-permute-start.1 = (s32[56]{0:T(128)S(1)}, s32[56]{0:T(128)S(1)}, u32[]{:S(2)}, u32[]{:S(2)}) collective-permute-start(s32[56]{0:T(128)S(1)} %pad_add_fusion.1), channel_id=1, source_target_pairs={{8,0},{12,4},{16,8},{20,12},{24,16},{28,20},{0,24},{4,28},{9,1},{1... | collective-permute-start | bytes 680 | tf_op jit(solution)/shard_map/ppermute | solution.py:60
  79.4 3.9 %collective-permute-start.2 = (s32[56]{0:T(128)S(1)}, s32[56]{0:T(128)S(1)}, u32[]{:S(2)}, u32[]{:S(2)}) collective-permute-start(s32[56]{0:T(128)S(1)} %pad_add_fusion.1), channel_id=1, source_target_pairs={{12,0},{16,4},{20,8},{24,12},{28,16},{0,20},{4,24},{8,28},{13,1},{... | collective-permute-start | bytes 680 | tf_op jit(solution)/shard_map/ppermute | solution.py:60
  83.3 3.6 %collective-permute-start.3 = (s32[56]{0:T(128)S(1)}, s32[56]{0:T(128)S(1)}, u32[]{:S(2)}, u32[]{:S(2)}) collective-permute-start(s32[56]{0:T(128)S(1)} %pad_add_fusion.1), channel_id=1, source_target_pairs={{16,0},{20,4},{24,8},{28,12},{0,16},{4,20},{8,24},{12,28},{17,1},{... | collective-permute-start | bytes 680 | tf_op jit(solution)/shard_map/ppermute | solution.py:60
  86.9 3.0 %collective-permute-start.4 = (s32[56]{0:T(128)S(1)}, s32[56]{0:T(128)S(1)}, u32[]{:S(2)}, u32[]{:S(2)}) collective-permute-start(s32[56]{0:T(128)S(1)} %pad_add_fusion.1), channel_id=1, source_target_pairs={{20,0},{24,4},{28,8},{0,12},{4,16},{8,20},{12,24},{16,28},{21,1},{... | collective-permute-start | bytes 680 | tf_op jit(solution)/shard_map/ppermute | solution.py:60
  89.9 3.6 %collective-permute-start.5 = (s32[56]{0:T(128)S(1)}, s32[56]{0:T(128)S(1)}, u32[]{:S(2)}, u32[]{:S(2)}) collective-permute-start(s32[56]{0:T(128)S(1)} %pad_add_fusion.1), channel_id=1, source_target_pairs={{24,0},{28,4},{0,8},{4,12},{8,16},{12,20},{16,24},{20,28},{25,1},{... | collective-permute-start | bytes 680 | tf_op jit(solution)/shard_map/ppermute | solution.py:60
  93.5 3.0 %collective-permute-start.6 = (s32[56]{0:T(128)S(1)}, s32[56]{0:T(128)S(1)}, u32[]{:S(2)}, u32[]{:S(2)}) collective-permute-start(s32[56]{0:T(128)S(1)} %pad_add_fusion.1), channel_id=1, source_target_pairs={{28,0},{0,4},{4,8},{8,12},{12,16},{16,20},{20,24},{24,28},{29,1},{... | collective-permute-start | bytes 680 | tf_op jit(solution)/shard_map/ppermute | solution.py:60
  103.0 48.8 %collective-permute-start.11 = (bf16[256,2048]{1,0:T(8,128)(2,1)}, bf16[256,2048]{1,0:T(8,128)(2,1)}, u32[]{:S(2)}, u32[]{:S(2)}) collective-permute-start(bf16[256,2048]{1,0:T(8,128)(2,1)} %collective-permute-done.10), channel_id=1, source_target_pairs={{1,2},{2,3},{5,6},{6,7},{9,10},{10,11},{13,14},{14,15},{17,18},{18... | collective-permute-start | bytes 3145736 | tf_op jit(solution)/shard_map/ppermute | solution.py:599
  140.2 108.9 %all-to-all-start.2 = ((bf16[32,256,128]{2,1,0:T(8,128)(2,1)}), bf16[32,256,128]{2,1,0:T(8,128)(2,1)S(1)}, u32[]{:S(2)}, u32[]{:S(2)}) async-start(bf16[32,256,128]{2,1,0:T(8,128)(2,1)} %attend_values.1), calls=%async_computation.2 | async-start | bytes 4194304 | tf_op jit(solution)/shard_map/all_to_all | solution.py:717
  150.5 58.7 %collective-permute-start.14 = (bf16[256,2048]{1,0:T(8,128)(2,1)}, bf16[256,2048]{1,0:T(8,128)(2,1)S(1)}, u32[]{:S(2)}, u32[]{:S(2)}) collective-permute-start(bf16[256,2048]{1,0:T(8,128)(2,1)} %collective-permute-done.9), channel_id=1, source_target_pairs={{1,0},{2,1},{5,4},{6,5},{9,8},{10,9},{13,12},{14,13},{17,16},{18,1... | collective-permute-start | bytes 3145736 | tf_op jit(solution)/shard_map/ppermute | solution.py:600
  151.8 59.0 %collective-permute-start.12 = (bf16[256,2048]{1,0:T(8,128)(2,1)}, bf16[256,2048]{1,0:T(8,128)(2,1)}, u32[]{:S(2)}, u32[]{:S(2)}) collective-permute-start(bf16[256,2048]{1,0:T(8,128)(2,1)} %collective-permute-done.11), channel_id=1, source_target_pairs={{2,3},{6,7},{10,11},{14,15},{18,19},{22,23},{26,27},{30,31}} | collective-permute-start | bytes 3145736 | tf_op jit(solution)/shard_map/ppermute | solution.py:599
  209.2 36.8 %collective-permute-start.16 = (bf16[256,2048]{1,0:T(8,128)(2,1)S(1)}, bf16[256,2048]{1,0:T(8,128)(2,1)S(1)}, u32[]{:S(2)}, u32[]{:S(2)}) collective-permute-start(bf16[256,2048]{1,0:T(8,128)(2,1)S(1)} %collective-permute-done.14), channel_id=1, source_target_pairs={{1,0},{5,4},{9,8},{13,12},{17,16},{21,20},{25,24},{29,28}} | collective-permute-start | bytes 3145736 | tf_op jit(solution)/shard_map/ppermute | solution.py:600
  210.7 35.6 %copy-start.4 = (bf16[256,2048]{1,0:T(8,128)(2,1)}, bf16[256,2048]{1,0:T(8,128)(2,1)S(1)}, u32[]{:S(2)}) copy-start(bf16[256,2048]{1,0:T(8,128)(2,1)S(1)} %broadcast_select_fusion.1.refs_2_) | copy-start | bytes 3145732
  210.7 35.7 %collective-permute-start.15 = (bf16[256,2048]{1,0:T(8,128)(2,1)S(1)}, bf16[256,2048]{1,0:T(8,128)(2,1)S(1)}, u32[]{:S(2)}, u32[]{:S(2)}) collective-permute-start(bf16[256,2048]{1,0:T(8,128)(2,1)S(1)} %broadcast_select_fusion.1.refs_2_), channel_id=1, source_target_pairs={{4,0},{0,4},{12,8},{8,12},{20,16},{16,20},{28,24},{24,28},{5,1},{1... | collective-permute-start | bytes 3145736 | tf_op jit(solution)/shard_map/ppermute | solution.py:589
  212.4 33.9 %collective-permute-start.13 = (bf16[256,2048]{1,0:T(8,128)(2,1)S(1)}, bf16[256,2048]{1,0:T(8,128)(2,1)S(1)}, u32[]{:S(2)}, u32[]{:S(2)}) collective-permute-start(bf16[256,2048]{1,0:T(8,128)(2,1)S(1)} %broadcast_select_fusion.2.refs_0_), channel_id=1, source_target_pairs={{4,0},{0,4},{12,8},{8,12},{20,16},{16,20},{28,24},{24,28},{5,1},{1... | collective-permute-start | bytes 3145736 | tf_op jit(solution)/shard_map/ppermute | solution.py:589
  246.3 2.9 %collective-permute-start.17 = (bf16[256,2048]{1,0:T(8,128)(2,1)S(1)}, bf16[256,2048]{1,0:T(8,128)(2,1)}, u32[]{:S(2)}, u32[]{:S(2)}) collective-permute-start(bf16[256,2048]{1,0:T(8,128)(2,1)S(1)} %broadcast_select_fusion.refs_4_), channel_id=1, source_target_pairs={{4,0},{0,4},{12,8},{8,12},{20,16},{16,20},{28,24},{24,28},{5,1},{1... | collective-permute-start | bytes 3145736 | tf_op jit(solution)/shard_map/ppermute | solution.py:589
  (9 other events, 147.9 us)

commit v5 on v4

--- a/solution.py
+++ b/solution.py
@@ -12,11 +12,14 @@
 HD = 128
 BLOCK = 256
 NEG = -1e30
+MIB = 1024 * 1024
 LEAD, TAIL = 2, 14
 PREP_STEP = 4
 CHUNK = 8
 OUT_RING, IN_RING = 4, 8
-VALUE_STEP = 4
+SCORE_STEP = 4
+VALUE_STEP = 8
+ONES = 16
 FINISH_STEP = 4
 PROJECT_TILE = 512
 BF16 = jnp.bfloat16
@@ -25,29 +28,67 @@
 HBM = pl.BlockSpec(memory_space=pl.ANY)
 
 
-def pack_kernel(turned, x_ref, o_ref):
+def turn_kernel(x_ref, o_ref):
     heads, groups = o_ref.shape[:2]
     rows = x_ref.shape[0] // groups
     for h in range(heads):
         for g in range(groups):
-            part = x_ref[g * rows : (g + 1) * rows, h * HD : (h + 1) * HD]
-            o_ref[h, g, 0] = part.T if turned else part
+            o_ref[h, g, 0] = x_ref[g * rows : (g + 1) * rows, h * HD : (h + 1) * HD].T
+
+
+def pack_kernel(x_ref, o_ref, held_ref, in_sem, out_sem):
+    heads, groups, spans, rows, _ = o_ref.shape
+    steps = [(z, g) for z in range(spans) for g in range(groups)]
+
+    def arrive(i):
+        some = pl.ds(i * rows, rows)
+        return pltpu.make_async_copy(x_ref.at[some], held_ref.at[some], in_sem.at[i])
+
+    def leave(i, h):
+        z, g = steps[i]
+        return pltpu.make_async_copy(
+            held_ref.at[pl.ds(i * rows, rows), pl.ds(h * HD, HD)],
+            o_ref.at[h, g, z],
+            out_sem.at[i, h],
+        )
+
+    for i in range(len(steps)):
+        arrive(i).start()
+    for i in range(len(steps)):
+        arrive(i).wait()
+        for h in range(heads):
+            leave(i, h).start()
+    for i in range(len(steps)):
+        for h in range(heads):
+            leave(i, h).wait()
 
 
 def pack(x, spans, groups, turned=False):
     tokens, width = x.shape
     heads, span = width // HD, tokens // spans
     rows = span // groups
-    tail = (HD, rows) if turned else (rows, HD)
+    cost = pl.CostEstimate(flops=0, bytes_accessed=4 * tokens * width, transcendentals=0)
+    if turned:
+        return pl.pallas_call(
+            turn_kernel,
+            grid=(spans,),
+            in_specs=[pl.BlockSpec((span, width), lambda i: (i, 0))],
+            out_specs=pl.BlockSpec((heads, groups, 1, HD, rows), lambda i: (0, 0, i, 0, 0)),
+            out_shape=jax.ShapeDtypeStruct((heads, groups, spans, HD, rows), BF16),
+            cost_estimate=cost,
+            name="turn",
+        )(x)
     return pl.pallas_call(
-        functools.partial(pack_kernel, turned),
-        grid=(spans,),
-        in_specs=[pl.BlockSpec((span, width), lambda i: (i, 0))],
-        out_specs=pl.BlockSpec((heads, groups, 1, *tail), lambda i: (0, 0, i, 0, 0)),
-        out_shape=jax.ShapeDtypeStruct((heads, groups, spans, *tail), BF16),
-        cost_estimate=pl.CostEstimate(
-            flops=0, bytes_accessed=4 * tokens * width, transcendentals=0
-        ),
+        pack_kernel,
+        in_specs=[HBM],
+        out_specs=HBM,
+        out_shape=jax.ShapeDtypeStruct((heads, groups, spans, rows, HD), BF16),
+        scratch_shapes=[
+            pltpu.VMEM((tokens, width), BF16),
+            pltpu.SemaphoreType.DMA((spans * groups,)),
+            pltpu.SemaphoreType.DMA((spans * groups, heads)),
+        ],
+        cost_estimate=cost,
         name="pack",
     )(x)
 
@@ -63,12 +104,14 @@
     return jnp.concatenate([mine] + rest)
 
 
-def job_lists(tables, buckets, spot, shards, slots, blocks, units, span, rows):
+def job_lists(tables, bucket, spot, shards, slots, blocks, units, span, rows):
     nblk = shards * blocks
     cap = 2 * shards * slots
     limit = job_limit(units, shards, slots)
 
     def kernel(tab_ref, bucket_ref, spot_ref, count_ref, unit_ref, key_ref, fill, lists):
+        head = spot_ref[3]
+
         def clear(b, _):
             fill[b] = 0
             return 0
@@ -76,8 +119,9 @@
         lax.fori_loop(0, nblk, clear, 0)
         per = shards * slots
 
-        def from_shard(shard, _):
-            base = lax.rem(shard + shards - spot_ref[2], shards) * (2 * per + shards)
+        for r in range(shards):
+            shard = lax.rem(spot_ref[2] + r, shards)
+            base = r * (2 * per + shards)
 
             def to_shard(other, _):
                 at = base + other * slots
@@ -86,7 +130,7 @@
                     a = shard * blocks + tab_ref[at + slot]
                     b = other * blocks + tab_ref[at + per + slot]
 
-                    @pl.when(bucket_ref[a] == bucket_ref[b])
+                    @pl.when(bucket_ref[head, a] == bucket_ref[head, b])
                     def _():
                         end_a, end_b = fill[a], fill[b]
                         lists[a * cap + end_a] = b
@@ -101,9 +145,6 @@
                 return 0
 
             lax.fori_loop(0, shards, to_shard, 0)
-            return 0
-
-        lax.fori_loop(0, shards, from_shard, 0)
 
         for i in range(LEAD):
             unit_ref[i] = units
@@ -131,7 +172,7 @@
 
     return pl.pallas_call(
         kernel,
-        in_specs=[SMEM, SMEM, SMEM],
+        in_specs=[SMEM] * 3,
         out_specs=[SMEM, SMEM, SMEM],
         out_shape=[
             jax.ShapeDtypeStruct((1,), jnp.int32),
@@ -146,7 +187,7 @@
             flops=0, bytes_accessed=32 * 1024 * 1024, transcendentals=0
         ),
         name="job_lists",
-    )(tables, buckets, spot)
+    )(tables, bucket.T, spot)
 
 
 def job_limit(units, shards, slots):
@@ -324,42 +365,41 @@
 
 def scores_kernel(groups, spot_ref, count_ref, unit_ref, key_ref, *refs):
     pieces = refs[:groups]
-    p_out, scale_ref, sum_ref, q_ref, inv_ref, s0, s1, x0, x1, top_ref, p_buf, q_sem, p_sem = refs[
-        groups:
-    ]
+    p_out, scale_ref, q_ref, inv_ref, top_ref, p_buf, q_sem, p_sem = refs[groups : groups + 8]
+    held = refs[groups + 8 :]
+    s_refs, x_refs = held[:SCORE_STEP], held[SCORE_STEP:]
     shards, spans, rows, _ = pieces[0].shape
     units = shards * spans
     me = spot_ref[0]
     lanes = [slice(k, k + HD) for k in range(0, rows, HD)]
 
-    copies = []
-    for r in range(groups):
-        piece = lax.rem(me + r, groups)
-        for s in range(shards):
-            copies.append(
-                pltpu.make_async_copy(
-                    pieces[r].at[s], q_ref.at[pl.ds(s * spans, spans), piece], q_sem
-                )
+    def arrivals(s):
+        some = pl.ds(s * spans, spans)
+        return [
+            pltpu.make_async_copy(
+                pieces[r].at[s], q_ref.at[some, lax.rem(me + r, groups)], q_sem.at[s]
             )
-    for copy in copies:
-        copy.start()
-    sum_ref[...] = jnp.zeros(sum_ref.shape, F32)
-    for copy in copies:
-        copy.wait()
-
-    contract = (((1,), (1,)), ((), ()))
+            for r in range(groups)
+        ]
+
+    for s in range(shards):
+        for copy in arrivals(s):
+            copy.start()
+
     fold = math.log2(math.e) ** -2
 
-    def prepare(i, _):
-        for k in range(PREP_STEP):
-            b = i * PREP_STEP + k
-            wide = q_ref[b // groups, lax.rem(b, groups)].astype(F32)
+    def prepare(s, _):
+        for copy in arrivals(s):
+            copy.wait()
+        for k in range(spans * groups):
+            unit, piece = s * spans + k // groups, k % groups
+            wide = q_ref[unit, piece].astype(F32)
             total = jnp.sum(wide * wide, axis=1, keepdims=True)
             inv = lax.rsqrt(total * fold + 1e-06 * HD * fold)
-            inv_ref[b] = jnp.broadcast_to(inv, (BLOCK, HD))
-        return 0
-
-    lax.fori_loop(0, units * groups // PREP_STEP, prepare, 0)
+            inv_ref[unit * groups + piece] = jnp.broadcast_to(inv, (BLOCK, HD))
+        return 0
+
+    lax.fori_loop(0, shards, prepare, 0)
 
     def tiles(x):
         return x.reshape(x.shape[0] // 8, 8, x.shape[1])
@@ -371,7 +411,7 @@
         gram = lax.dot_general(
             q_ref[key // groups, lax.rem(key, groups)],
             q_ref[unit, me],
-            contract,
+            (((1,), (1,)), ((), ())),
             preferred_element_type=F32,
         )
         shift = jnp.where(first, 0, 2 * BLOCK)
@@ -389,52 +429,46 @@
             x_ref[:, lane] = jnp.broadcast_to(most, (8, HD))
 
     def weigh(j, s_ref, x_ref, slot, at):
-        unit = unit_ref[LEAD + j]
-        first = unit_ref[LEAD + j - 1] != unit
+        first = unit_ref[LEAD + j - 1] != unit_ref[LEAD + j]
         old = jnp.where(first, 2 * NEG, top_ref[...])
         new = jnp.maximum(old, x_ref[...])
         top_ref[...] = new
-        scale = jnp.exp2(old - new)
-        scale_ref[pl.ds(j, 1), :] = scale[0:1]
-        total = sum_ref[unit] * scale
+        scale_ref[pl.ds(j, 1), :] = jnp.exp2(old - new)[0:1]
         for lane in lanes:
             prob = jnp.exp2(tiles(s_ref[:, lane]) - new[None, :, lane])
-            sum_ref[unit, :, lane] = total[:, lane] + jnp.sum(prob, axis=0)
             p_buf[slot, at, :, lane] = prob.reshape(BLOCK, HD).astype(BF16)
 
-    ring = p_buf.shape[0]
-
     def out_copy(chunk):
-        slot = lax.rem(chunk, ring)
+        slot = lax.rem(chunk, OUT_RING)
         return pltpu.make_async_copy(
             p_buf.at[slot], p_out.at[pl.ds(chunk * CHUNK, CHUNK)], p_sem.at[slot]
         )
 
-    score(0, s0, x0)
-    score(1, s1, x1)
+    for i in range(SCORE_STEP):
+        score(i, s_refs[i], x_refs[i])
     chunks = (count_ref[0] + CHUNK - 1) // CHUNK
 
     def chunk_step(chunk, _):
-        slot = lax.rem(chunk, ring)
-
-        @pl.when(chunk >= ring)
+        slot = lax.rem(chunk, OUT_RING)
+
+        @pl.when(chunk >= OUT_RING)
         def _():
-            out_copy(chunk - ring).wait()
+            out_copy(chunk - OUT_RING).wait()
 
         def step(k, _):
-            j = chunk * CHUNK + 2 * k
-            weigh(j, s0, x0, slot, 2 * k)
-            weigh(j + 1, s1, x1, slot, 2 * k + 1)
-            score(j + 2, s0, x0)
-            score(j + 3, s1, x1)
+            j = chunk * CHUNK + SCORE_STEP * k
+            for i in range(SCORE_STEP):
+                weigh(j + i, s_refs[i], x_refs[i], slot, SCORE_STEP * k + i)
+            for i in range(SCORE_STEP):
+                score(j + SCORE_STEP + i, s_refs[i], x_refs[i])
             return 0
 
-        lax.fori_loop(0, CHUNK // 2, step, 0)
+        lax.fori_loop(0, CHUNK // SCORE_STEP, step, 0)
         out_copy(chunk).start()
         return 0
 
     lax.fori_loop(0, chunks, chunk_step, 0)
-    for back in range(ring, 0, -1):
+    for back in range(OUT_RING, 0, -1):
 
         @pl.when(chunks >= back)
         def _():
@@ -448,25 +482,23 @@
     nblk = units * groups
     room = jobs[1].shape[0] // CHUNK * CHUNK
     work = 3 * units
-    vmem = pl.BlockSpec(memory_space=pltpu.VMEM)
     return pl.pallas_call(
         functools.partial(scores_kernel, groups),
         in_specs=[SMEM] * 4 + [HBM] * groups,
-        out_specs=[HBM, vmem, vmem],
+        out_specs=[HBM, pl.BlockSpec(memory_space=pltpu.VMEM)],
         out_shape=[
             jax.ShapeDtypeStruct((room, BLOCK, rows), BF16),
             jax.ShapeDtypeStruct((room, rows), F32),
-            jax.ShapeDtypeStruct((units + 1, 8, rows), F32),
         ],
         scratch_shapes=[
             pltpu.VMEM((units, groups, rows, HD), BF16),
             pltpu.VMEM((nblk, BLOCK, HD), F32),
-            pltpu.VMEM((BLOCK, rows), F32),
-            pltpu.VMEM((BLOCK, rows), F32),
-            *[pltpu.VMEM((8, rows), F32)] * 3,
+            pltpu.VMEM((8, rows), F32),
             pltpu.VMEM((OUT_RING, CHUNK, BLOCK, rows), BF16),
-            pltpu.SemaphoreType.DMA,
+            pltpu.SemaphoreType.DMA((shards,)),
             pltpu.SemaphoreType.DMA((OUT_RING,)),
+            *[pltpu.VMEM((BLOCK, rows), F32)] * SCORE_STEP,
+            *[pltpu.VMEM((8, rows), F32)] * SCORE_STEP,
         ],
         cost_estimate=pl.CostEstimate(
             flops=2 * work * rows * BLOCK * HD,
@@ -479,33 +511,20 @@
 
 def values_kernel(groups, spot_ref, count_ref, unit_ref, key_ref, *refs):
     pieces = refs[:groups]
-    p_in, scale_ref, sum_ref, o_ref, vt_ref, acc_ref, p_buf, v_sem, p_sem = refs[groups:]
-    shards, spans, _, _ = pieces[0].shape
-    units = shards * spans
+    p_in, scale_in, o_out, acc_ref, p_buf, o_ref, scale_ref, p_sem, o_sem, scale_sem = refs[groups:]
+    units, _, _ = pieces[0].shape
     me = spot_ref[0]
-
-    copies = []
-    for r in range(groups):
-        piece = lax.rem(me + r, groups)
-        for s in range(shards):
-            copies.append(
-                pltpu.make_async_copy(
-                    pieces[r].at[s], vt_ref.at[pl.ds(s * spans, spans), piece], v_sem
-                )
-            )
-    for copy in copies:
-        copy.start()
-
-    ring = p_buf.shape[0]
     chunks = (count_ref[0] + CHUNK - 1) // CHUNK
 
     def in_copy(chunk):
-        slot = lax.rem(chunk, ring)
+        slot = lax.rem(chunk, IN_RING)
         return pltpu.make_async_copy(
             p_in.at[pl.ds(chunk * CHUNK, CHUNK)], p_buf.at[slot], p_sem.at[slot]
         )
 
-    for ahead in range(ring - 1):
+    scale_copy = pltpu.make_async_copy(scale_in, scale_ref, scale_sem)
+    scale_copy.start()
+    for ahead in range(IN_RING - 1):
 
         @pl.when(ahead < chunks)
         def _():
@@ -516,72 +535,89 @@
         return 0
 
     lax.fori_loop(0, units + 1, clear, 0)
-    for copy in copies:
-        copy.wait()
-
-    def gather(j, slot, at):
+    scale_copy.wait()
+    ones = jnp.ones((ONES, BLOCK), BF16)
+
+    def gather(j, prob):
         unit, key = unit_ref[LEAD + j], key_ref[LEAD + j]
+        source = lax.rem(key + groups - me, groups)
+        turned = pieces[0][key // groups]
+        for r in range(1, groups):
+            turned = jnp.where(source == r, pieces[r][key // groups], turned)
         part = jnp.dot(
-            vt_ref[key // groups, lax.rem(key, groups)],
-            p_buf[slot, at],
-            preferred_element_type=F32,
+            jnp.concatenate([turned, ones], axis=0), prob, preferred_element_type=F32
         )
-        acc_ref[unit] = acc_ref[unit] * scale_ref[pl.ds(j, 1), :] + part
+        acc_ref[unit] = acc_ref[unit] * scale_ref[pl.ds(j, 1), :] + part[: HD + 8]
 
     def chunk_step(chunk, _):
-        slot = lax.rem(chunk, ring)
-
-        @pl.when(chunk + ring - 1 < chunks)
+        slot = lax.rem(chunk, IN_RING)
+
+        @pl.when(chunk + IN_RING - 1 < chunks)
         def _():
-            in_copy(chunk + ring - 1).start()
+            in_copy(chunk + IN_RING - 1).start()
 
         in_copy(chunk).wait()
 
         def step(k, _):
             for i in range(VALUE_STEP):
-                gather(chunk * CHUNK + VALUE_STEP * k + i, slot, VALUE_STEP * k + i)
+                at = VALUE_STEP * k + i
+                gather(chunk * CHUNK + at, p_buf[slot, at])
             return 0
 
         lax.fori_loop(0, CHUNK // VALUE_STEP, step, 0)
         return 0
 
     lax.fori_loop(0, chunks, chunk_step, 0)
+
+    def result(i):
+        some = pl.ds(i * FINISH_STEP, FINISH_STEP)
+        return pltpu.make_async_copy(o_ref.at[some], o_out.at[some], o_sem.at[i])
 
     def finish(i, _):
         for k in range(FINISH_STEP):
             unit = i * FINISH_STEP + k
-            total = 1.0 / jnp.sum(sum_ref[unit], axis=0, keepdims=True)
-            o_ref[unit] = (acc_ref[unit] * total).astype(BF16).T
+            inverse = 1.0 / acc_ref[unit, HD : HD + 1, :]
+            o_ref[unit] = (acc_ref[unit, 0:HD, :] * inverse).astype(BF16).T
+        result(i).start()
         return 0
 
     lax.fori_loop(0, units // FINISH_STEP, finish, 0)
-
-
-def attend_values(spot, jobs, pieces, probs, scales, sums):
+    for i in range(units // FINISH_STEP):
+        result(i).wait()
+
+
+def attend_values(spot, jobs, pieces, probs, scales):
     groups = len(pieces)
     shards, spans, _, rows = pieces[0].shape
     units = shards * spans
     work = 3 * units
     vmem = pl.BlockSpec(memory_space=pltpu.VMEM)
+    pieces = [
+        pltpu.with_memory_space_constraint(x.reshape(units, HD, rows), pltpu.VMEM)
+        for x in pieces
+    ]
     return pl.pallas_call(
         functools.partial(values_kernel, groups),
-        in_specs=[SMEM] * 4 + [HBM] * (groups + 1) + [vmem, vmem],
-        out_specs=vmem,
-        out_shape=jax.ShapeDtypeStruct((units, rows, HD), BF16),
+        in_specs=[SMEM] * 4 + [vmem] * groups + [HBM] * 2,
+        out_specs=pl.BlockSpec(memory_space=pltpu.HBM),
+        out_shape=pltpu.HBM((units, rows, HD), BF16),
         scratch_shapes=[
-            pltpu.VMEM((units, groups, HD, rows), BF16),
-            pltpu.VMEM((units + 1, HD, rows), F32),
+            pltpu.VMEM((units + 1, HD + 8, rows), F32),
             pltpu.VMEM((IN_RING, CHUNK, BLOCK, rows), BF16),
+            pltpu.VMEM((units, rows, HD), BF16),
+            pltpu.VMEM(scales.shape, F32),
+            pltpu.SemaphoreType.DMA((IN_RING,)),
+            pltpu.SemaphoreType.DMA((units // FINISH_STEP,)),
             pltpu.SemaphoreType.DMA,
-            pltpu.SemaphoreType.DMA((IN_RING,)),
         ],
+        compiler_params=pltpu.CompilerParams(vmem_limit_bytes=24 * MIB),
         cost_estimate=pl.CostEstimate(
             flops=2 * work * rows * BLOCK * HD,
             bytes_accessed=2 * units * groups * rows * HD + 2 * work * rows * BLOCK,
             transcendentals=0,
         ),
         name="attend_values",
-    )(spot, *jobs, *pieces, probs, scales, sums)
+    )(spot, *jobs, *pieces, probs, pltpu.with_memory_space_constraint(scales, pltpu.HBM))
 
 
 def group_shift(x, shards, groups, r):
@@ -688,7 +724,7 @@
     slots = pair_row.shape[2]
     here, z = lax.axis_index("seq"), lax.axis_index("head")
     head, member = here // groups, lax.rem(here, groups)
-    spot = jnp.stack([member, z, here]).astype(jnp.int32)
+    spot = jnp.stack([member, z, here, z * heads + head]).astype(jnp.int32)
 
     shares = ring_weights(w_out, groups, member)
     units = shards * spans
@@ -704,13 +740,11 @@
     q_pieces = send(qk, False)
     v_pieces = send(values, turned)
     tables = gather_tables(pair_row, pair_col, pair_count, shards)
-    buckets = lax.dynamic_slice_in_dim(bucket, z * heads + head, 1, 1).reshape(-1)
     jobs = job_lists(
-        tables, buckets, spot, shards, slots, blocks, units, tokens // spans, rows
+        tables, bucket, spot, shards, slots, blocks, units, tokens // spans, rows
     )
     if turned:
         weights = attend_scores(spot, jobs, q_pieces)
-        v_pieces = [pltpu.with_memory_space_constraint(x, pltpu.HBM) for x in v_pieces]
         attn = attend_values(spot, jobs, v_pieces, *weights)
     else:
         attn = attend(spot, jobs, q_pieces, v_pieces)

time: 260 us -> 249 us (0.958)
  Pallas kernels: 57.6 us -> 48.3 us
    pallas_call x1, Pallas kernels: 21.2 us -> 15.8 us  [attend_scores(): pl.pallas_call(functools.partial(scores_kernel, groups), in_specs=[SMEM]...]
    pallas_call x1, Pallas kernels: 14.3 us -> 11.3 us  [attend_values(): pl.pallas_call(functools.partial(values_kernel, groups), in_specs=[SMEM]...]
  transfers between devices with their start and end apart: 21 -> 21, of which waited for: 12 -> 12; matrix products, arithmetic and copies ran while one was open for 2% -> 2% of each run, Pallas kernels for 18% -> 15%
where the time goes in v5:
time: 249 us; the launch traced here: 247 us
  waiting for transfers between devices  156 us (63%)
  Pallas kernels  48.3 us (19%)
  starting transfers between devices  33.6 us (13%)
  local copies, waits for them, and re-layouts  5.75 us (2%)
  other arithmetic  2.57 us (1%)
    ppermute x3, waiting for transfers between devices, ring_weights(): lax.ppermute(down, 'head', [(i, i - 1) for i in range(1, count - k + 1)])  89.2 us
    all_to_all x2, waiting for transfers between devices, send(): got = lax.all_to_all(sent, 'seq', 0, 0, tiled=True)  45.9 us
    ppermute x7, waiting for transfers between devices, gather_tables(): lax.ppermute(mine, 'seq', [((i + r) % shards, i) for i in range(shards)])  20.5 us
    pallas_call x1, Pallas kernels, attend_scores(): pl.pallas_call(functools.partial(scores_kernel, groups), in_specs=[SMEM]...  15.8 us
    pallas_call x1, Pallas kernels, attend_values(): pl.pallas_call(functools.partial(values_kernel, groups), in_specs=[SMEM]...  11.3 us
    all_to_all x2, starting transfers between devices, send(): got = lax.all_to_all(sent, 'seq', 0, 0, tiled=True)  9.29 us
    all_to_all x1, starting transfers between devices, body(): mixed = lax.all_to_all(attn, ('seq', 'head'), 0, 0, tiled=True)  9.04 us
    pallas_call x1, Pallas kernels, project(): pl.pallas_call(project_kernel, grid=(width // tile,), in_specs=[SMEM, pl....  8.16 us
  transfers between devices with their start and end apart: 21, of which 12 were waited for; matrix products, arithmetic and copies ran while one was open for 2% of the time, Pallas kernels for 15%

profile of v5, /device:TPU:2, one launch (start us, length us, event | category | flops | bytes accessed | tf_op | source)
XLA Modules:
  0.0 246.9 jit_solution(16178519646393652890)
XLA Ops:
  0.0 2.6 %pack.1 = bf16[4,2,4,256,128]{4,3,2,1,0:T(8,128)(2,1)} custom-call(bf16[2048,512]{1,0:T(8,128)(2,1)} %x_ref.3), custom_call_target="tpu_custom_call" | custom-call | bytes 4194304 | tf_op jit(solution)/shard_map/pack/pallas_call | solution.py:81
  2.6 4.3 %all-to-all-start.1 = ((bf16[8,4,256,128]{3,2,1,0:T(8,128)(2,1)}), bf16[8,4,256,128]{3,2,1,0:T(8,128)(2,1)S(1)}, u32[]{:S(2)}, u32[]{:S(2)}) async-start(bf16[8,4,256,128]{3,2,1,0:T(8,128)(2,1)} %bitcast.14), calls=%async_computation.1 | async-start | bytes 4194304 | tf_op jit(solution)/shard_map/all_to_all | solution.py:737
  6.9 4.1 %turn.1 = bf16[4,2,4,128,256]{4,3,2,1,0:T(8,128)(2,1)} custom-call(bf16[2048,512]{1,0:T(8,128)(2,1)} %x_ref.2), custom_call_target="tpu_custom_call" | custom-call | bytes 4194304 | tf_op jit(solution)/shard_map/turn/pallas_call | solution.py:72
  11.0 21.0 %all-to-all-done.1.refs_0_ = bf16[8,4,256,128]{3,2,1,0:T(8,128)(2,1)S(1)} async-done(((bf16[8,4,256,128]{3,2,1,0:T(8,128)(2,1)}), bf16[8,4,256,128]{3,2,1,0:T(8,128)(2,1)S(1)}, u32[]{:S(2)}, u32[]{:S(2)}) %all-to-all-start.1) | async-done | bytes 2097184 | tf_op jit(solution)/shard_map/all_to_all | solution.py:737
  32.0 1.4 copy-done.3
  33.4 5.0 %all-to-all-start = ((bf16[8,4,128,256]{3,2,1,0:T(8,128)(2,1)}), bf16[8,4,128,256]{3,2,1,0:T(8,128)(2,1)S(1)}, u32[]{:S(2)}, u32[]{:S(2)}) async-start(bf16[8,4,128,256]{3,2,1,0:T(8,128)(2,1)} %bitcast.13), calls=%async_computation | async-start | bytes 4194304 | tf_op jit(solution)/shard_map/all_to_all | solution.py:737
  38.6 24.9 %all-to-all-done = bf16[8,4,128,256]{3,2,1,0:T(8,128)(2,1)S(1)} async-done(((bf16[8,4,128,256]{3,2,1,0:T(8,128)(2,1)}), bf16[8,4,128,256]{3,2,1,0:T(8,128)(2,1)S(1)}, u32[]{:S(2)}, u32[]{:S(2)}) %all-to-all-start) | async-done | bytes 2097184 | tf_op jit(solution)/shard_map/all_to_all | solution.py:737
  64.9 4.5 %collective-permute-start.10 = (bf16[256,2048]{1,0:T(8,128)(2,1)S(1)}, bf16[256,2048]{1,0:T(8,128)(2,1)}, u32[]{:S(2)}, u32[]{:S(2)}) collective-permute-start(bf16[256,2048]{1,0:T(8,128)(2,1)S(1)} %constant_dynamic-slice_fusion), channel_id=1, source_target_pairs={{0,1},{1,2},{2,3},{4,5},{5,6},{6,7},{8,9},{9,10},{10,11},{12,13},{... | collective-permute-start | bytes 3145736 | tf_op jit(solution)/shard_map/ppermute | solution.py:635
  74.3 3.9 %collective-permute-done.1 = s32[56]{0:T(128)S(1)} collective-permute-done((s32[56]{0:T(128)S(1)}, s32[56]{0:T(128)S(1)}, u32[]{:S(2)}, u32[]{:S(2)}) %collective-permute-start.1) | collective-permute-done | bytes 256 | tf_op jit(solution)/shard_map/ppermute | solution.py:101
  78.8 3.3 %collective-permute-done.2 = s32[56]{0:T(128)S(1)} collective-permute-done((s32[56]{0:T(128)S(1)}, s32[56]{0:T(128)S(1)}, u32[]{:S(2)}, u32[]{:S(2)}) %collective-permute-start.2) | collective-permute-done | bytes 256 | tf_op jit(solution)/shard_map/ppermute | solution.py:101
  82.6 3.0 %collective-permute-done.3 = s32[56]{0:T(128)S(1)} collective-permute-done((s32[56]{0:T(128)S(1)}, s32[56]{0:T(128)S(1)}, u32[]{:S(2)}, u32[]{:S(2)}) %collective-permute-start.3) | collective-permute-done | bytes 256 | tf_op jit(solution)/shard_map/ppermute | solution.py:101
  85.7 3.0 %collective-permute-done.4 = s32[56]{0:T(128)S(1)} collective-permute-done((s32[56]{0:T(128)S(1)}, s32[56]{0:T(128)S(1)}, u32[]{:S(2)}, u32[]{:S(2)}) %collective-permute-start.4) | collective-permute-done | bytes 256 | tf_op jit(solution)/shard_map/ppermute | solution.py:101
  88.7 3.6 %collective-permute-done.5 = s32[56]{0:T(128)S(1)} collective-permute-done((s32[56]{0:T(128)S(1)}, s32[56]{0:T(128)S(1)}, u32[]{:S(2)}, u32[]{:S(2)}) %collective-permute-start.5) | collective-permute-done | bytes 256 | tf_op jit(solution)/shard_map/ppermute | solution.py:101
  92.8 2.4 collective-permute-done.6
  95.9 6.3 %job_lists.1 = (s32[1]{0:T(128)}, s32[432]{0:T(512)}, s32[432]{0:T(512)}) custom-call(s32[448]{0:T(512)} %concatenate.8.tab_ref, s32[16,64]{1,0:T(8,128)} %bitcast.15, s32[4]{0:T(128)} %pad_add_fusion.spot_ref), custom_call_target="tpu_custom_call" | custom-call | bytes 33554432 | tf_op jit(solution)/shard_map/job_lists/pallas_call | solution.py:173
  102.2 1.6 collective-permute-start.11
  103.8 15.8 %attend_scores.1 = (bf16[432,256,256]{2,1,0:T(8,128)(2,1)}, f32[432,256]{1,0:T(8,128)}) custom-call(s32[4]{0:T(128)} %pad_add_fusion.spot_ref, s32[1]{0:T(128)} %get-tuple-element.10.count_ref, s32[432]{0:T(512)} %get-tuple-element.11.unit_ref, s32[432]{0:T(512)} %get-tuple-element.12.key_ref, bf16[8,4,256,128]{3,2,1,0:T(8,128)(2,1)} %copy-done.3, ...), custom_call_target="tpu_custom_call" | custom-call | flops 1610612736 | bytes 16777216 | tf_op jit(solution)/shard_map/attend_scores/pallas_call | solution.py:485
  119.7 11.3 %attend_values.1 = bf16[32,256,128]{2,1,0:T(8,128)(2,1)} custom-call(s32[4]{0:T(128)S(1)} %copy-done, s32[1]{0:T(128)} %get-tuple-element.10.count_ref, s32[432]{0:T(512)S(1)} %copy-done.1, s32[432]{0:T(512)S(1)} %copy-done.2, bf16[32,128,256]{2,1,0:T(8,128)(2,1)S(1)} %bitcast.11, bf16[32,128,256]{2,1,0:T(8,128)(2,1)} %bitcast.8.refs_1_, ...), custom_call_target="tpu_custom_call" | custom-call | flops 1610612736 | bytes 16777216 | tf_op jit(solution)/shard_map/attend_values/pallas_call | solution.py:599
  131.0 9.0 %all-to-all-start.2 = ((bf16[32,256,128]{2,1,0:T(8,128)(2,1)}), bf16[32,256,128]{2,1,0:T(8,128)(2,1)S(1)}, u32[]{:S(2)}, u32[]{:S(2)}) async-start(bf16[32,256,128]{2,1,0:T(8,128)(2,1)} %attend_values.1), calls=%async_computation.2 | async-start | bytes 4194304 | tf_op jit(solution)/shard_map/all_to_all | solution.py:751
  141.4 1.6 collective-permute-start.12
  143.0 55.8 %collective-permute-done.14 = bf16[256,2048]{1,0:T(8,128)(2,1)S(1)} collective-permute-done((bf16[256,2048]{1,0:T(8,128)(2,1)}, bf16[256,2048]{1,0:T(8,128)(2,1)S(1)}, u32[]{:S(2)}, u32[]{:S(2)}) %collective-permute-start.14) | collective-permute-done | bytes 1048608 | tf_op jit(solution)/shard_map/ppermute | solution.py:636
  200.4 1.6 broadcast_select_fusion.2.refs_0_
  202.3 33.4 %collective-permute-done.16 = bf16[256,2048]{1,0:T(8,128)(2,1)S(1)} collective-permute-done((bf16[256,2048]{1,0:T(8,128)(2,1)S(1)}, bf16[256,2048]{1,0:T(8,128)(2,1)S(1)}, u32[]{:S(2)}, u32[]{:S(2)}) %collective-permute-start.16) | collective-permute-done | bytes 1048608 | tf_op jit(solution)/shard_map/ppermute | solution.py:636
  238.7 8.2 %project.1 = bf16[512,2048]{1,0:T(8,128)(2,1)} custom-call(s32[4]{0:T(128)} %pad_add_fusion.spot_ref, bf16[4,2,4,256,128]{4,3,2,1,0:T(8,128)(2,1)S(1)} %bitcast.12, bf16[512,2048]{1,0:T(8,128)(2,1)} %w_ref.1, bf16[256,2048]{1,0:T(8,128)(2,1)} %copy-done.5, bf16[256,2048]{1,0:T(8,128)(2,1)} %copy-done.11, bf16[256,2048]{1,0:T(8,128)(2,1)} %copy-done.4, ...), custom_call_target="tpu_custom_call" | custom-call | flops 4294967296 | bytes 8388608 | tf_op jit(solution)/shard_map/project/pallas_call | solution.py:697
  (59 shorter events, 14.9 us)
Async XLA Ops:
  2.6 29.4 %all-to-all-start.1 = ((bf16[8,4,256,128]{3,2,1,0:T(8,128)(2,1)}), bf16[8,4,256,128]{3,2,1,0:T(8,128)(2,1)S(1)}, u32[]{:S(2)}, u32[]{:S(2)}) async-start(bf16[8,4,256,128]{3,2,1,0:T(8,128)(2,1)} %bitcast.14), calls=%async_computation.1 | async-start | bytes 4194304 | tf_op jit(solution)/shard_map/all_to_all | solution.py:737
  33.4 30.1 %all-to-all-start = ((bf16[8,4,128,256]{3,2,1,0:T(8,128)(2,1)}), bf16[8,4,128,256]{3,2,1,0:T(8,128)(2,1)S(1)}, u32[]{:S(2)}, u32[]{:S(2)}) async-start(bf16[8,4,128,256]{3,2,1,0:T(8,128)(2,1)} %bitcast.13), calls=%async_computation | async-start | bytes 4194304 | tf_op jit(solution)/shard_map/all_to_all | solution.py:737
  38.4 32.6 %copy-start.7 = (s32[1,8]{1,0:T(1,128)S(1)}, s32[1,8]{1,0:T(1,128)}, u32[]{:S(2)}) copy-start(s32[1,8]{1,0:T(1,128)} %param.12) | copy-start | bytes 100
  38.4 65.4 %collective-permute-start.8 = (bf16[8,4,256,128]{3,2,1,0:T(8,128)(2,1)}, bf16[8,4,256,128]{3,2,1,0:T(8,128)(2,1)}, u32[]{:S(2)}, u32[]{:S(2)}) collective-permute-start(bf16[8,4,256,128]{3,2,1,0:T(8,128)(2,1)} %copy-done.3), channel_id=1, source_target_pairs={{4,0},{0,4},{12,8},{8,12},{20,16},{16,20},{28,24},{24,28},{5,1},{1... | collective-permute-start | bytes 6291464 | tf_op jit(solution)/shard_map/ppermute | solution.py:625
  63.5 56.1 %collective-permute-start.7 = (bf16[8,4,128,256]{3,2,1,0:T(8,128)(2,1)S(1)}, bf16[8,4,128,256]{3,2,1,0:T(8,128)(2,1)}, u32[]{:S(2)}, u32[]{:S(2)}) collective-permute-start(bf16[8,4,128,256]{3,2,1,0:T(8,128)(2,1)S(1)} %all-to-all-done), channel_id=1, source_target_pairs={{4,0},{0,4},{12,8},{8,12},{20,16},{16,20},{28,24},{24,28},{5,1},{1... | collective-permute-start | bytes 6291464 | tf_op jit(solution)/shard_map/ppermute | solution.py:625
  64.9 37.3 %collective-permute-start.10 = (bf16[256,2048]{1,0:T(8,128)(2,1)S(1)}, bf16[256,2048]{1,0:T(8,128)(2,1)}, u32[]{:S(2)}, u32[]{:S(2)}) collective-permute-start(bf16[256,2048]{1,0:T(8,128)(2,1)S(1)} %constant_dynamic-slice_fusion), channel_id=1, source_target_pairs={{0,1},{1,2},{2,3},{4,5},{5,6},{6,7},{8,9},{9,10},{10,11},{12,13},{... | collective-permute-start | bytes 3145736 | tf_op jit(solution)/shard_map/ppermute | solution.py:635
  69.4 70.7 %collective-permute-start.9 = (bf16[256,2048]{1,0:T(8,128)(2,1)S(1)}, bf16[256,2048]{1,0:T(8,128)(2,1)}, u32[]{:S(2)}, u32[]{:S(2)}) collective-permute-start(bf16[256,2048]{1,0:T(8,128)(2,1)S(1)} %constant_dynamic-slice_fusion), channel_id=1, source_target_pairs={{1,0},{2,1},{3,2},{5,4},{6,5},{7,6},{9,8},{10,9},{11,10},{13,12},{... | collective-permute-start | bytes 3145736 | tf_op jit(solution)/shard_map/ppermute | solution.py:636
  71.1 2.6 %collective-permute-start = (s32[56]{0:T(128)S(1)}, s32[56]{0:T(128)S(1)}, u32[]{:S(2)}, u32[]{:S(2)}) collective-permute-start(s32[56]{0:T(128)S(1)} %pad_add_fusion.1), channel_id=1, source_target_pairs={{4,0},{8,4},{12,8},{16,12},{20,16},{24,20},{28,24},{0,28},{5,1},{9... | collective-permute-start | bytes 680 | tf_op jit(solution)/shard_map/ppermute | solution.py:101
  73.7 4.5 %collective-permute-start.1 = (s32[56]{0:T(128)S(1)}, s32[56]{0:T(128)S(1)}, u32[]{:S(2)}, u32[]{:S(2)}) collective-permute-start(s32[56]{0:T(128)S(1)} %pad_add_fusion.1), channel_id=1, source_target_pairs={{8,0},{12,4},{16,8},{20,12},{24,16},{28,20},{0,24},{4,28},{9,1},{1... | collective-permute-start | bytes 680 | tf_op jit(solution)/shard_map/ppermute | solution.py:101
  78.2 3.9 %collective-permute-start.2 = (s32[56]{0:T(128)S(1)}, s32[56]{0:T(128)S(1)}, u32[]{:S(2)}, u32[]{:S(2)}) collective-permute-start(s32[56]{0:T(128)S(1)} %pad_add_fusion.1), channel_id=1, source_target_pairs={{12,0},{16,4},{20,8},{24,12},{28,16},{0,20},{4,24},{8,28},{13,1},{... | collective-permute-start | bytes 680 | tf_op jit(solution)/shard_map/ppermute | solution.py:101
  82.1 3.6 %collective-permute-start.3 = (s32[56]{0:T(128)S(1)}, s32[56]{0:T(128)S(1)}, u32[]{:S(2)}, u32[]{:S(2)}) collective-permute-start(s32[56]{0:T(128)S(1)} %pad_add_fusion.1), channel_id=1, source_target_pairs={{16,0},{20,4},{24,8},{28,12},{0,16},{4,20},{8,24},{12,28},{17,1},{... | collective-permute-start | bytes 680 | tf_op jit(solution)/shard_map/ppermute | solution.py:101
  85.7 3.0 %collective-permute-start.4 = (s32[56]{0:T(128)S(1)}, s32[56]{0:T(128)S(1)}, u32[]{:S(2)}, u32[]{:S(2)}) collective-permute-start(s32[56]{0:T(128)S(1)} %pad_add_fusion.1), channel_id=1, source_target_pairs={{20,0},{24,4},{28,8},{0,12},{4,16},{8,20},{12,24},{16,28},{21,1},{... | collective-permute-start | bytes 680 | tf_op jit(solution)/shard_map/ppermute | solution.py:101
  88.7 3.6 %collective-permute-start.5 = (s32[56]{0:T(128)S(1)}, s32[56]{0:T(128)S(1)}, u32[]{:S(2)}, u32[]{:S(2)}) collective-permute-start(s32[56]{0:T(128)S(1)} %pad_add_fusion.1), channel_id=1, source_target_pairs={{24,0},{28,4},{0,8},{4,12},{8,16},{12,20},{16,24},{20,28},{25,1},{... | collective-permute-start | bytes 680 | tf_op jit(solution)/shard_map/ppermute | solution.py:101
  92.2 3.0 %collective-permute-start.6 = (s32[56]{0:T(128)S(1)}, s32[56]{0:T(128)S(1)}, u32[]{:S(2)}, u32[]{:S(2)}) collective-permute-start(s32[56]{0:T(128)S(1)} %pad_add_fusion.1), channel_id=1, source_target_pairs={{28,0},{0,4},{4,8},{8,12},{12,16},{16,20},{20,24},{24,28},{29,1},{... | collective-permute-start | bytes 680 | tf_op jit(solution)/shard_map/ppermute | solution.py:101
  102.2 39.2 %collective-permute-start.11 = (bf16[256,2048]{1,0:T(8,128)(2,1)}, bf16[256,2048]{1,0:T(8,128)(2,1)}, u32[]{:S(2)}, u32[]{:S(2)}) collective-permute-start(bf16[256,2048]{1,0:T(8,128)(2,1)} %collective-permute-done.10), channel_id=1, source_target_pairs={{1,2},{2,3},{5,6},{6,7},{9,10},{10,11},{13,14},{14,15},{17,18},{18... | collective-permute-start | bytes 3145736 | tf_op jit(solution)/shard_map/ppermute | solution.py:635
  131.0 107.7 %all-to-all-start.2 = ((bf16[32,256,128]{2,1,0:T(8,128)(2,1)}), bf16[32,256,128]{2,1,0:T(8,128)(2,1)S(1)}, u32[]{:S(2)}, u32[]{:S(2)}) async-start(bf16[32,256,128]{2,1,0:T(8,128)(2,1)} %attend_values.1), calls=%async_computation.2 | async-start | bytes 4194304 | tf_op jit(solution)/shard_map/all_to_all | solution.py:751
  140.1 58.7 %collective-permute-start.14 = (bf16[256,2048]{1,0:T(8,128)(2,1)}, bf16[256,2048]{1,0:T(8,128)(2,1)S(1)}, u32[]{:S(2)}, u32[]{:S(2)}) collective-permute-start(bf16[256,2048]{1,0:T(8,128)(2,1)} %collective-permute-done.9), channel_id=1, source_target_pairs={{1,0},{2,1},{5,4},{6,5},{9,8},{10,9},{13,12},{14,13},{17,16},{18,1... | collective-permute-start | bytes 3145736 | tf_op jit(solution)/shard_map/ppermute | solution.py:636
  141.4 58.9 %collective-permute-start.12 = (bf16[256,2048]{1,0:T(8,128)(2,1)}, bf16[256,2048]{1,0:T(8,128)(2,1)}, u32[]{:S(2)}, u32[]{:S(2)}) collective-permute-start(bf16[256,2048]{1,0:T(8,128)(2,1)} %collective-permute-done.11), channel_id=1, source_target_pairs={{2,3},{6,7},{10,11},{14,15},{18,19},{22,23},{26,27},{30,31}} | collective-permute-start | bytes 3145736 | tf_op jit(solution)/shard_map/ppermute | solution.py:635
  198.8 36.8 %collective-permute-start.16 = (bf16[256,2048]{1,0:T(8,128)(2,1)S(1)}, bf16[256,2048]{1,0:T(8,128)(2,1)S(1)}, u32[]{:S(2)}, u32[]{:S(2)}) collective-permute-start(bf16[256,2048]{1,0:T(8,128)(2,1)S(1)} %collective-permute-done.14), channel_id=1, source_target_pairs={{1,0},{5,4},{9,8},{13,12},{17,16},{21,20},{25,24},{29,28}} | collective-permute-start | bytes 3145736 | tf_op jit(solution)/shard_map/ppermute | solution.py:636
  200.3 35.6 %copy-start.4 = (bf16[256,2048]{1,0:T(8,128)(2,1)}, bf16[256,2048]{1,0:T(8,128)(2,1)S(1)}, u32[]{:S(2)}) copy-start(bf16[256,2048]{1,0:T(8,128)(2,1)S(1)} %broadcast_select_fusion.1.refs_2_) | copy-start | bytes 3145732
  200.3 35.7 %collective-permute-start.15 = (bf16[256,2048]{1,0:T(8,128)(2,1)S(1)}, bf16[256,2048]{1,0:T(8,128)(2,1)S(1)}, u32[]{:S(2)}, u32[]{:S(2)}) collective-permute-start(bf16[256,2048]{1,0:T(8,128)(2,1)S(1)} %broadcast_select_fusion.1.refs_2_), channel_id=1, source_target_pairs={{4,0},{0,4},{12,8},{8,12},{20,16},{16,20},{28,24},{24,28},{5,1},{1... | collective-permute-start | bytes 3145736 | tf_op jit(solution)/shard_map/ppermute | solution.py:625
  202.0 34.0 %copy-start.5 = (bf16[256,2048]{1,0:T(8,128)(2,1)}, bf16[256,2048]{1,0:T(8,128)(2,1)S(1)}, u32[]{:S(2)}) copy-start(bf16[256,2048]{1,0:T(8,128)(2,1)S(1)} %broadcast_select_fusion.2.refs_0_) | copy-start | bytes 3145732
  202.0 33.9 %collective-permute-start.13 = (bf16[256,2048]{1,0:T(8,128)(2,1)S(1)}, bf16[256,2048]{1,0:T(8,128)(2,1)S(1)}, u32[]{:S(2)}, u32[]{:S(2)}) collective-permute-start(bf16[256,2048]{1,0:T(8,128)(2,1)S(1)} %broadcast_select_fusion.2.refs_0_), channel_id=1, source_target_pairs={{4,0},{0,4},{12,8},{8,12},{20,16},{16,20},{28,24},{24,28},{5,1},{1... | collective-permute-start | bytes 3145736 | tf_op jit(solution)/shard_map/ppermute | solution.py:625
  235.8 2.9 %collective-permute-start.17 = (bf16[256,2048]{1,0:T(8,128)(2,1)S(1)}, bf16[256,2048]{1,0:T(8,128)(2,1)}, u32[]{:S(2)}, u32[]{:S(2)}) collective-permute-start(bf16[256,2048]{1,0:T(8,128)(2,1)S(1)} %broadcast_select_fusion.refs_4_), channel_id=1, source_target_pairs={{4,0},{0,4},{12,8},{8,12},{20,16},{16,20},{28,24},{24,28},{5,1},{1... | collective-permute-start | bytes 3145736 | tf_op jit(solution)/shard_map/ppermute | solution.py:625
  (9 other events, 118.7 us)

commit v6 on v5

--- a/solution.py
+++ b/solution.py
@@ -13,11 +13,11 @@
 BLOCK = 256
 NEG = -1e30
 MIB = 1024 * 1024
-LEAD, TAIL = 2, 14
+LEAD, TAIL = 2, 22
 PREP_STEP = 4
 CHUNK = 8
-OUT_RING, IN_RING = 4, 8
-SCORE_STEP = 4
+OUT_RING, IN_RING = 4, 5
+SCORE_STEP = 8
 VALUE_STEP = 8
 ONES = 16
 FINISH_STEP = 4
@@ -125,26 +125,20 @@
 
             def to_shard(other, _):
                 at = base + other * slots
-
-                def visit(slot, _):
+                live = tab_ref[base + 2 * per + other]
+                for slot in range(slots):
                     a = shard * blocks + tab_ref[at + slot]
                     b = other * blocks + tab_ref[at + per + slot]
-
-                    @pl.when(bucket_ref[head, a] == bucket_ref[head, b])
-                    def _():
-                        end_a, end_b = fill[a], fill[b]
-                        lists[a * cap + end_a] = b
-                        lists[b * cap + end_b] = a
-                        fill[a] = end_a + 1
-                        fill[b] = end_b + 1
-
-                    return 0
-
-                live = jnp.minimum(tab_ref[base + 2 * per + other], slots)
-                lax.fori_loop(0, live, visit, 0)
+                    same = bucket_ref[head, a] == bucket_ref[head, b]
+                    keep = (same & (slot < live)).astype(jnp.int32)
+                    end_a, end_b = fill[a], fill[b]
+                    lists[a * (cap + 1) + end_a] = b
+                    lists[b * (cap + 1) + end_b] = a
+                    fill[a] = end_a + keep
+                    fill[b] = end_b + keep
                 return 0
 
-            lax.fori_loop(0, shards, to_shard, 0)
+            lax.fori_loop(0, shards, to_shard, 0, unroll=4)
 
         for i in range(LEAD):
             unit_ref[i] = units
@@ -158,7 +152,7 @@
 
             def partner(j, _):
                 unit_ref[at + 1 + j] = unit
-                key_ref[at + 1 + j] = lists[own * cap + j]
+                key_ref[at + 1 + j] = lists[own * (cap + 1) + j]
                 return 0
 
             lax.fori_loop(0, n, partner, 0)
@@ -181,7 +175,7 @@
         ],
         scratch_shapes=[
             pltpu.SMEM((nblk,), jnp.int32),
-            pltpu.SMEM((nblk * cap,), jnp.int32),
+            pltpu.SMEM((nblk * (cap + 1),), jnp.int32),
         ],
         cost_estimate=pl.CostEstimate(
             flops=0, bytes_accessed=32 * 1024 * 1024, transcendentals=0

time: 249 us -> 246 us (0.988)
  Pallas kernels: 48.3 us -> 45 us
  transfers between devices with their start and end apart: 21 -> 21, of which waited for: 12 -> 12; matrix products, arithmetic and copies ran while one was open for 2% -> 2% of each run, Pallas kernels for 15% -> 14%
where the time goes in v6:
time: 246 us; the launch traced here: 243 us
  waiting for transfers between devices  156 us (63%)
  Pallas kernels  45 us (18%)
  starting transfers between devices  33.4 us (14%)
  local copies, waits for them, and re-layouts  5.67 us (2%)
  other arithmetic  2.63 us (1%)
    ppermute x3, waiting for transfers between devices, ring_weights(): lax.ppermute(down, 'head', [(i, i - 1) for i in range(1, count - k + 1)])  89.2 us
    all_to_all x2, waiting for transfers between devices, send(): got = lax.all_to_all(sent, 'seq', 0, 0, tiled=True)  45.9 us
    ppermute x7, waiting for transfers between devices, gather_tables(): lax.ppermute(mine, 'seq', [((i + r) % shards, i) for i in range(shards)])  20.4 us
    pallas_call x1, Pallas kernels, attend_scores(): pl.pallas_call(functools.partial(scores_kernel, groups), in_specs=[SMEM]...  14.5 us
    pallas_call x1, Pallas kernels, attend_values(): pl.pallas_call(functools.partial(values_kernel, groups), in_specs=[SMEM]...  10.4 us
    all_to_all x2, starting transfers between devices, send(): got = lax.all_to_all(sent, 'seq', 0, 0, tiled=True)  9.29 us
    all_to_all x1, starting transfers between devices, body(): mixed = lax.all_to_all(attn, ('seq', 'head'), 0, 0, tiled=True)  8.81 us
    pallas_call x1, Pallas kernels, project(): pl.pallas_call(project_kernel, grid=(width // tile,), in_specs=[SMEM, pl....  8.16 us
  transfers between devices with their start and end apart: 21, of which 12 were waited for; matrix products, arithmetic and copies ran while one was open for 2% of the time, Pallas kernels for 14%

profile of v6, /device:TPU:2, one launch (start us, length us, event | category | flops | bytes accessed | tf_op | source)
XLA Modules:
  0.0 243.2 jit_solution(7906434494446521176)
XLA Ops:
  0.0 2.6 %pack.1 = bf16[4,2,4,256,128]{4,3,2,1,0:T(8,128)(2,1)} custom-call(bf16[2048,512]{1,0:T(8,128)(2,1)} %x_ref.3), custom_call_target="tpu_custom_call" | custom-call | bytes 4194304 | tf_op jit(solution)/shard_map/pack/pallas_call | solution.py:81
  2.6 4.3 %all-to-all-start.1 = ((bf16[8,4,256,128]{3,2,1,0:T(8,128)(2,1)}), bf16[8,4,256,128]{3,2,1,0:T(8,128)(2,1)S(1)}, u32[]{:S(2)}, u32[]{:S(2)}) async-start(bf16[8,4,256,128]{3,2,1,0:T(8,128)(2,1)} %bitcast.14), calls=%async_computation.1 | async-start | bytes 4194304 | tf_op jit(solution)/shard_map/all_to_all | solution.py:731
  6.9 4.1 %turn.1 = bf16[4,2,4,128,256]{4,3,2,1,0:T(8,128)(2,1)} custom-call(bf16[2048,512]{1,0:T(8,128)(2,1)} %x_ref.2), custom_call_target="tpu_custom_call" | custom-call | bytes 4194304 | tf_op jit(solution)/shard_map/turn/pallas_call | solution.py:72
  11.0 21.0 %all-to-all-done.1.refs_0_ = bf16[8,4,256,128]{3,2,1,0:T(8,128)(2,1)S(1)} async-done(((bf16[8,4,256,128]{3,2,1,0:T(8,128)(2,1)}), bf16[8,4,256,128]{3,2,1,0:T(8,128)(2,1)S(1)}, u32[]{:S(2)}, u32[]{:S(2)}) %all-to-all-start.1) | async-done | bytes 2097184 | tf_op jit(solution)/shard_map/all_to_all | solution.py:731
  33.3 5.0 %all-to-all-start = ((bf16[8,4,128,256]{3,2,1,0:T(8,128)(2,1)}), bf16[8,4,128,256]{3,2,1,0:T(8,128)(2,1)S(1)}, u32[]{:S(2)}, u32[]{:S(2)}) async-start(bf16[8,4,128,256]{3,2,1,0:T(8,128)(2,1)} %bitcast.13), calls=%async_computation | async-start | bytes 4194304 | tf_op jit(solution)/shard_map/all_to_all | solution.py:731
  38.5 24.9 %all-to-all-done = bf16[8,4,128,256]{3,2,1,0:T(8,128)(2,1)S(1)} async-done(((bf16[8,4,128,256]{3,2,1,0:T(8,128)(2,1)}), bf16[8,4,128,256]{3,2,1,0:T(8,128)(2,1)S(1)}, u32[]{:S(2)}, u32[]{:S(2)}) %all-to-all-start) | async-done | bytes 2097184 | tf_op jit(solution)/shard_map/all_to_all | solution.py:731
  63.5 1.3 constant_dynamic-slice_fusion
  64.8 4.5 %collective-permute-start.10 = (bf16[256,2048]{1,0:T(8,128)(2,1)S(1)}, bf16[256,2048]{1,0:T(8,128)(2,1)}, u32[]{:S(2)}, u32[]{:S(2)}) collective-permute-start(bf16[256,2048]{1,0:T(8,128)(2,1)S(1)} %constant_dynamic-slice_fusion), channel_id=1, source_target_pairs={{0,1},{1,2},{2,3},{4,5},{5,6},{6,7},{8,9},{9,10},{10,11},{12,13},{... | collective-permute-start | bytes 3145736 | tf_op jit(solution)/shard_map/ppermute | solution.py:629
  74.2 3.9 %collective-permute-done.1 = s32[56]{0:T(128)S(1)} collective-permute-done((s32[56]{0:T(128)S(1)}, s32[56]{0:T(128)S(1)}, u32[]{:S(2)}, u32[]{:S(2)}) %collective-permute-start.1) | collective-permute-done | bytes 256 | tf_op jit(solution)/shard_map/ppermute | solution.py:101
  78.7 3.3 %collective-permute-done.2 = s32[56]{0:T(128)S(1)} collective-permute-done((s32[56]{0:T(128)S(1)}, s32[56]{0:T(128)S(1)}, u32[]{:S(2)}, u32[]{:S(2)}) %collective-permute-start.2) | collective-permute-done | bytes 256 | tf_op jit(solution)/shard_map/ppermute | solution.py:101
  82.5 3.0 %collective-permute-done.3 = s32[56]{0:T(128)S(1)} collective-permute-done((s32[56]{0:T(128)S(1)}, s32[56]{0:T(128)S(1)}, u32[]{:S(2)}, u32[]{:S(2)}) %collective-permute-start.3) | collective-permute-done | bytes 256 | tf_op jit(solution)/shard_map/ppermute | solution.py:101
  85.5 3.0 %collective-permute-done.4 = s32[56]{0:T(128)S(1)} collective-permute-done((s32[56]{0:T(128)S(1)}, s32[56]{0:T(128)S(1)}, u32[]{:S(2)}, u32[]{:S(2)}) %collective-permute-start.4) | collective-permute-done | bytes 256 | tf_op jit(solution)/shard_map/ppermute | solution.py:101
  88.5 3.6 %collective-permute-done.5 = s32[56]{0:T(128)S(1)} collective-permute-done((s32[56]{0:T(128)S(1)}, s32[56]{0:T(128)S(1)}, u32[]{:S(2)}, u32[]{:S(2)}) %collective-permute-start.5) | collective-permute-done | bytes 256 | tf_op jit(solution)/shard_map/ppermute | solution.py:101
  92.8 2.3 collective-permute-done.6
  95.8 5.2 %job_lists.1 = (s32[1]{0:T(128)}, s32[440]{0:T(512)}, s32[440]{0:T(512)}) custom-call(s32[448]{0:T(512)} %concatenate.8.tab_ref, s32[16,64]{1,0:T(8,128)} %bitcast.15, s32[4]{0:T(128)} %pad_add_fusion.spot_ref), custom_call_target="tpu_custom_call" | custom-call | bytes 33554432 | tf_op jit(solution)/shard_map/job_lists/pallas_call | solution.py:167
  101.0 1.6 collective-permute-start.11
  102.7 14.5 %attend_scores.1 = (bf16[440,256,256]{2,1,0:T(8,128)(2,1)}, f32[440,256]{1,0:T(8,128)}) custom-call(s32[4]{0:T(128)} %pad_add_fusion.spot_ref, s32[1]{0:T(128)} %get-tuple-element.10.count_ref, s32[440]{0:T(512)} %get-tuple-element.11.unit_ref, s32[440]{0:T(512)} %get-tuple-element.12.key_ref, bf16[8,4,256,128]{3,2,1,0:T(8,128)(2,1)} %copy-done.3, ...), custom_call_target="tpu_custom_call" | custom-call | flops 1610612736 | bytes 16777216 | tf_op jit(solution)/shard_map/attend_scores/pallas_call | solution.py:479
  117.2 10.4 %attend_values.1 = bf16[32,256,128]{2,1,0:T(8,128)(2,1)} custom-call(s32[4]{0:T(128)S(1)} %copy-done, s32[1]{0:T(128)} %get-tuple-element.10.count_ref, s32[440]{0:T(512)S(1)} %copy-done.1, s32[440]{0:T(512)S(1)} %copy-done.2, bf16[32,128,256]{2,1,0:T(8,128)(2,1)S(1)} %bitcast.11, bf16[32,128,256]{2,1,0:T(8,128)(2,1)} %bitcast.8.refs_1_, ...), custom_call_target="tpu_custom_call" | custom-call | flops 1610612736 | bytes 16777216 | tf_op jit(solution)/shard_map/attend_values/pallas_call | solution.py:593
  127.6 8.8 %all-to-all-start.2 = ((bf16[32,256,128]{2,1,0:T(8,128)(2,1)}), bf16[32,256,128]{2,1,0:T(8,128)(2,1)S(1)}, u32[]{:S(2)}, u32[]{:S(2)}) async-start(bf16[32,256,128]{2,1,0:T(8,128)(2,1)} %attend_values.1), calls=%async_computation.2 | async-start | bytes 4194304 | tf_op jit(solution)/shard_map/all_to_all | solution.py:745
  137.8 1.6 collective-permute-start.12
  139.4 55.8 %collective-permute-done.14 = bf16[256,2048]{1,0:T(8,128)(2,1)S(1)} collective-permute-done((bf16[256,2048]{1,0:T(8,128)(2,1)}, bf16[256,2048]{1,0:T(8,128)(2,1)S(1)}, u32[]{:S(2)}, u32[]{:S(2)}) %collective-permute-start.14) | collective-permute-done | bytes 1048608 | tf_op jit(solution)/shard_map/ppermute | solution.py:630
  196.7 1.6 broadcast_select_fusion.2.refs_0_
  198.6 33.4 %collective-permute-done.16 = bf16[256,2048]{1,0:T(8,128)(2,1)S(1)} collective-permute-done((bf16[256,2048]{1,0:T(8,128)(2,1)S(1)}, bf16[256,2048]{1,0:T(8,128)(2,1)S(1)}, u32[]{:S(2)}, u32[]{:S(2)}) %collective-permute-start.16) | collective-permute-done | bytes 1048608 | tf_op jit(solution)/shard_map/ppermute | solution.py:630
  235.1 8.2 %project.1 = bf16[512,2048]{1,0:T(8,128)(2,1)} custom-call(s32[4]{0:T(128)} %pad_add_fusion.spot_ref, bf16[4,2,4,256,128]{4,3,2,1,0:T(8,128)(2,1)S(1)} %bitcast.12, bf16[512,2048]{1,0:T(8,128)(2,1)} %w_ref.1, bf16[256,2048]{1,0:T(8,128)(2,1)} %copy-done.5, bf16[256,2048]{1,0:T(8,128)(2,1)} %copy-done.11, bf16[256,2048]{1,0:T(8,128)(2,1)} %copy-done.4, ...), custom_call_target="tpu_custom_call" | custom-call | flops 4294967296 | bytes 8388608 | tf_op jit(solution)/shard_map/project/pallas_call | solution.py:691
  (59 shorter events, 14.9 us)
Async XLA Ops:
  2.6 29.4 %all-to-all-start.1 = ((bf16[8,4,256,128]{3,2,1,0:T(8,128)(2,1)}), bf16[8,4,256,128]{3,2,1,0:T(8,128)(2,1)S(1)}, u32[]{:S(2)}, u32[]{:S(2)}) async-start(bf16[8,4,256,128]{3,2,1,0:T(8,128)(2,1)} %bitcast.14), calls=%async_computation.1 | async-start | bytes 4194304 | tf_op jit(solution)/shard_map/all_to_all | solution.py:731
  33.3 30.1 %all-to-all-start = ((bf16[8,4,128,256]{3,2,1,0:T(8,128)(2,1)}), bf16[8,4,128,256]{3,2,1,0:T(8,128)(2,1)S(1)}, u32[]{:S(2)}, u32[]{:S(2)}) async-start(bf16[8,4,128,256]{3,2,1,0:T(8,128)(2,1)} %bitcast.13), calls=%async_computation | async-start | bytes 4194304 | tf_op jit(solution)/shard_map/all_to_all | solution.py:731
  38.3 32.6 %copy-start.7 = (s32[1,8]{1,0:T(1,128)S(1)}, s32[1,8]{1,0:T(1,128)}, u32[]{:S(2)}) copy-start(s32[1,8]{1,0:T(1,128)} %param.12) | copy-start | bytes 100
  38.3 64.3 %collective-permute-start.8 = (bf16[8,4,256,128]{3,2,1,0:T(8,128)(2,1)}, bf16[8,4,256,128]{3,2,1,0:T(8,128)(2,1)}, u32[]{:S(2)}, u32[]{:S(2)}) collective-permute-start(bf16[8,4,256,128]{3,2,1,0:T(8,128)(2,1)} %copy-done.3), channel_id=1, source_target_pairs={{4,0},{0,4},{12,8},{8,12},{20,16},{16,20},{28,24},{24,28},{5,1},{1... | collective-permute-start | bytes 6291464 | tf_op jit(solution)/shard_map/ppermute | solution.py:619
  63.4 53.7 %collective-permute-start.7 = (bf16[8,4,128,256]{3,2,1,0:T(8,128)(2,1)S(1)}, bf16[8,4,128,256]{3,2,1,0:T(8,128)(2,1)}, u32[]{:S(2)}, u32[]{:S(2)}) collective-permute-start(bf16[8,4,128,256]{3,2,1,0:T(8,128)(2,1)S(1)} %all-to-all-done), channel_id=1, source_target_pairs={{4,0},{0,4},{12,8},{8,12},{20,16},{16,20},{28,24},{24,28},{5,1},{1... | collective-permute-start | bytes 6291464 | tf_op jit(solution)/shard_map/ppermute | solution.py:619
  64.8 36.2 %collective-permute-start.10 = (bf16[256,2048]{1,0:T(8,128)(2,1)S(1)}, bf16[256,2048]{1,0:T(8,128)(2,1)}, u32[]{:S(2)}, u32[]{:S(2)}) collective-permute-start(bf16[256,2048]{1,0:T(8,128)(2,1)S(1)} %constant_dynamic-slice_fusion), channel_id=1, source_target_pairs={{0,1},{1,2},{2,3},{4,5},{5,6},{6,7},{8,9},{9,10},{10,11},{12,13},{... | collective-permute-start | bytes 3145736 | tf_op jit(solution)/shard_map/ppermute | solution.py:629
  69.3 67.2 %collective-permute-start.9 = (bf16[256,2048]{1,0:T(8,128)(2,1)S(1)}, bf16[256,2048]{1,0:T(8,128)(2,1)}, u32[]{:S(2)}, u32[]{:S(2)}) collective-permute-start(bf16[256,2048]{1,0:T(8,128)(2,1)S(1)} %constant_dynamic-slice_fusion), channel_id=1, source_target_pairs={{1,0},{2,1},{3,2},{5,4},{6,5},{7,6},{9,8},{10,9},{11,10},{13,12},{... | collective-permute-start | bytes 3145736 | tf_op jit(solution)/shard_map/ppermute | solution.py:630
  71.0 2.6 %collective-permute-start = (s32[56]{0:T(128)S(1)}, s32[56]{0:T(128)S(1)}, u32[]{:S(2)}, u32[]{:S(2)}) collective-permute-start(s32[56]{0:T(128)S(1)} %pad_add_fusion.1), channel_id=1, source_target_pairs={{4,0},{8,4},{12,8},{16,12},{20,16},{24,20},{28,24},{0,28},{5,1},{9... | collective-permute-start | bytes 680 | tf_op jit(solution)/shard_map/ppermute | solution.py:101
  73.6 4.5 %collective-permute-start.1 = (s32[56]{0:T(128)S(1)}, s32[56]{0:T(128)S(1)}, u32[]{:S(2)}, u32[]{:S(2)}) collective-permute-start(s32[56]{0:T(128)S(1)} %pad_add_fusion.1), channel_id=1, source_target_pairs={{8,0},{12,4},{16,8},{20,12},{24,16},{28,20},{0,24},{4,28},{9,1},{1... | collective-permute-start | bytes 680 | tf_op jit(solution)/shard_map/ppermute | solution.py:101
  78.1 3.9 %collective-permute-start.2 = (s32[56]{0:T(128)S(1)}, s32[56]{0:T(128)S(1)}, u32[]{:S(2)}, u32[]{:S(2)}) collective-permute-start(s32[56]{0:T(128)S(1)} %pad_add_fusion.1), channel_id=1, source_target_pairs={{12,0},{16,4},{20,8},{24,12},{28,16},{0,20},{4,24},{8,28},{13,1},{... | collective-permute-start | bytes 680 | tf_op jit(solution)/shard_map/ppermute | solution.py:101
  82.0 3.6 %collective-permute-start.3 = (s32[56]{0:T(128)S(1)}, s32[56]{0:T(128)S(1)}, u32[]{:S(2)}, u32[]{:S(2)}) collective-permute-start(s32[56]{0:T(128)S(1)} %pad_add_fusion.1), channel_id=1, source_target_pairs={{16,0},{20,4},{24,8},{28,12},{0,16},{4,20},{8,24},{12,28},{17,1},{... | collective-permute-start | bytes 680 | tf_op jit(solution)/shard_map/ppermute | solution.py:101
  85.5 3.0 %collective-permute-start.4 = (s32[56]{0:T(128)S(1)}, s32[56]{0:T(128)S(1)}, u32[]{:S(2)}, u32[]{:S(2)}) collective-permute-start(s32[56]{0:T(128)S(1)} %pad_add_fusion.1), channel_id=1, source_target_pairs={{20,0},{24,4},{28,8},{0,12},{4,16},{8,20},{12,24},{16,28},{21,1},{... | collective-permute-start | bytes 680 | tf_op jit(solution)/shard_map/ppermute | solution.py:101
  88.5 3.6 %collective-permute-start.5 = (s32[56]{0:T(128)S(1)}, s32[56]{0:T(128)S(1)}, u32[]{:S(2)}, u32[]{:S(2)}) collective-permute-start(s32[56]{0:T(128)S(1)} %pad_add_fusion.1), channel_id=1, source_target_pairs={{24,0},{28,4},{0,8},{4,12},{8,16},{12,20},{16,24},{20,28},{25,1},{... | collective-permute-start | bytes 680 | tf_op jit(solution)/shard_map/ppermute | solution.py:101
  92.1 3.0 %collective-permute-start.6 = (s32[56]{0:T(128)S(1)}, s32[56]{0:T(128)S(1)}, u32[]{:S(2)}, u32[]{:S(2)}) collective-permute-start(s32[56]{0:T(128)S(1)} %pad_add_fusion.1), channel_id=1, source_target_pairs={{28,0},{0,4},{4,8},{8,12},{12,16},{16,20},{20,24},{24,28},{29,1},{... | collective-permute-start | bytes 680 | tf_op jit(solution)/shard_map/ppermute | solution.py:101
  101.0 36.8 %collective-permute-start.11 = (bf16[256,2048]{1,0:T(8,128)(2,1)}, bf16[256,2048]{1,0:T(8,128)(2,1)}, u32[]{:S(2)}, u32[]{:S(2)}) collective-permute-start(bf16[256,2048]{1,0:T(8,128)(2,1)} %collective-permute-done.10), channel_id=1, source_target_pairs={{1,2},{2,3},{5,6},{6,7},{9,10},{10,11},{13,14},{14,15},{17,18},{18... | collective-permute-start | bytes 3145736 | tf_op jit(solution)/shard_map/ppermute | solution.py:629
  127.6 107.4 %all-to-all-start.2 = ((bf16[32,256,128]{2,1,0:T(8,128)(2,1)}), bf16[32,256,128]{2,1,0:T(8,128)(2,1)S(1)}, u32[]{:S(2)}, u32[]{:S(2)}) async-start(bf16[32,256,128]{2,1,0:T(8,128)(2,1)} %attend_values.1), calls=%async_computation.2 | async-start | bytes 4194304 | tf_op jit(solution)/shard_map/all_to_all | solution.py:745
  136.5 58.7 %collective-permute-start.14 = (bf16[256,2048]{1,0:T(8,128)(2,1)}, bf16[256,2048]{1,0:T(8,128)(2,1)S(1)}, u32[]{:S(2)}, u32[]{:S(2)}) collective-permute-start(bf16[256,2048]{1,0:T(8,128)(2,1)} %collective-permute-done.9), channel_id=1, source_target_pairs={{1,0},{2,1},{5,4},{6,5},{9,8},{10,9},{13,12},{14,13},{17,16},{18,1... | collective-permute-start | bytes 3145736 | tf_op jit(solution)/shard_map/ppermute | solution.py:630
  137.8 58.9 %collective-permute-start.12 = (bf16[256,2048]{1,0:T(8,128)(2,1)}, bf16[256,2048]{1,0:T(8,128)(2,1)}, u32[]{:S(2)}, u32[]{:S(2)}) collective-permute-start(bf16[256,2048]{1,0:T(8,128)(2,1)} %collective-permute-done.11), channel_id=1, source_target_pairs={{2,3},{6,7},{10,11},{14,15},{18,19},{22,23},{26,27},{30,31}} | collective-permute-start | bytes 3145736 | tf_op jit(solution)/shard_map/ppermute | solution.py:629
  195.2 36.8 %collective-permute-start.16 = (bf16[256,2048]{1,0:T(8,128)(2,1)S(1)}, bf16[256,2048]{1,0:T(8,128)(2,1)S(1)}, u32[]{:S(2)}, u32[]{:S(2)}) collective-permute-start(bf16[256,2048]{1,0:T(8,128)(2,1)S(1)} %collective-permute-done.14), channel_id=1, source_target_pairs={{1,0},{5,4},{9,8},{13,12},{17,16},{21,20},{25,24},{29,28}} | collective-permute-start | bytes 3145736 | tf_op jit(solution)/shard_map/ppermute | solution.py:630
  196.6 35.6 %copy-start.4 = (bf16[256,2048]{1,0:T(8,128)(2,1)}, bf16[256,2048]{1,0:T(8,128)(2,1)S(1)}, u32[]{:S(2)}) copy-start(bf16[256,2048]{1,0:T(8,128)(2,1)S(1)} %broadcast_select_fusion.1.refs_2_) | copy-start | bytes 3145732
  196.6 35.7 %collective-permute-start.15 = (bf16[256,2048]{1,0:T(8,128)(2,1)S(1)}, bf16[256,2048]{1,0:T(8,128)(2,1)S(1)}, u32[]{:S(2)}, u32[]{:S(2)}) collective-permute-start(bf16[256,2048]{1,0:T(8,128)(2,1)S(1)} %broadcast_select_fusion.1.refs_2_), channel_id=1, source_target_pairs={{4,0},{0,4},{12,8},{8,12},{20,16},{16,20},{28,24},{24,28},{5,1},{1... | collective-permute-start | bytes 3145736 | tf_op jit(solution)/shard_map/ppermute | solution.py:619
  198.4 34.0 %copy-start.5 = (bf16[256,2048]{1,0:T(8,128)(2,1)}, bf16[256,2048]{1,0:T(8,128)(2,1)S(1)}, u32[]{:S(2)}) copy-start(bf16[256,2048]{1,0:T(8,128)(2,1)S(1)} %broadcast_select_fusion.2.refs_0_) | copy-start | bytes 3145732
  198.4 33.9 %collective-permute-start.13 = (bf16[256,2048]{1,0:T(8,128)(2,1)S(1)}, bf16[256,2048]{1,0:T(8,128)(2,1)S(1)}, u32[]{:S(2)}, u32[]{:S(2)}) collective-permute-start(bf16[256,2048]{1,0:T(8,128)(2,1)S(1)} %broadcast_select_fusion.2.refs_0_), channel_id=1, source_target_pairs={{4,0},{0,4},{12,8},{8,12},{20,16},{16,20},{28,24},{24,28},{5,1},{1... | collective-permute-start | bytes 3145736 | tf_op jit(solution)/shard_map/ppermute | solution.py:619
  232.2 2.9 %collective-permute-start.17 = (bf16[256,2048]{1,0:T(8,128)(2,1)S(1)}, bf16[256,2048]{1,0:T(8,128)(2,1)}, u32[]{:S(2)}, u32[]{:S(2)}) collective-permute-start(bf16[256,2048]{1,0:T(8,128)(2,1)S(1)} %broadcast_select_fusion.refs_4_), channel_id=1, source_target_pairs={{4,0},{0,4},{12,8},{8,12},{20,16},{16,20},{28,24},{24,28},{5,1},{1... | collective-permute-start | bytes 3145736 | tf_op jit(solution)/shard_map/ppermute | solution.py:619
  (9 other events, 114.6 us)

commit v7 on v6

--- a/solution.py
+++ b/solution.py
@@ -13,12 +13,12 @@
 BLOCK = 256
 NEG = -1e30
 MIB = 1024 * 1024
-LEAD, TAIL = 2, 22
+LEAD, TAIL = 2, 30
 PREP_STEP = 4
-CHUNK = 8
-OUT_RING, IN_RING = 4, 5
+CHUNK = 16
+OUT_RING, IN_RING = 3, 3
 SCORE_STEP = 8
-VALUE_STEP = 8
+VALUE_STEP = 16
 ONES = 16
 FINISH_STEP = 4
 PROJECT_TILE = 512
@@ -138,7 +138,7 @@
                     fill[b] = end_b + keep
                 return 0
 
-            lax.fori_loop(0, shards, to_shard, 0, unroll=4)
+            lax.fori_loop(0, shards, to_shard, 0)
 
         for i in range(LEAD):
             unit_ref[i] = units

time: 246 us -> 247 us (level)
  no operation moved by 1% of the time
where the time goes in v7:
time: 247 us; the launch traced here: 244 us
  waiting for transfers between devices  156 us (63%)
  Pallas kernels  45.4 us (18%)
  starting transfers between devices  34.1 us (14%)
  local copies, waits for them, and re-layouts  5.74 us (2%)
  other arithmetic  2.59 us (1%)
    ppermute x3, waiting for transfers between devices, ring_weights(): lax.ppermute(down, 'head', [(i, i - 1) for i in range(1, count - k + 1)])  89.2 us
    all_to_all x2, waiting for transfers between devices, send(): got = lax.all_to_all(sent, 'seq', 0, 0, tiled=True)  45.9 us
    ppermute x7, waiting for transfers between devices, gather_tables(): lax.ppermute(mine, 'seq', [((i + r) % shards, i) for i in range(shards)])  20.4 us
    pallas_call x1, Pallas kernels, attend_scores(): pl.pallas_call(functools.partial(scores_kernel, groups), in_specs=[SMEM]...  14.9 us
    pallas_call x1, Pallas kernels, attend_values(): pl.pallas_call(functools.partial(values_kernel, groups), in_specs=[SMEM]...  10.4 us
    all_to_all x1, starting transfers between devices, body(): mixed = lax.all_to_all(attn, ('seq', 'head'), 0, 0, tiled=True)  9.54 us
    all_to_all x2, starting transfers between devices, send(): got = lax.all_to_all(sent, 'seq', 0, 0, tiled=True)  9.29 us
    pallas_call x1, Pallas kernels, project(): pl.pallas_call(project_kernel, grid=(width // tile,), in_specs=[SMEM, pl....  8.16 us
  transfers between devices with their start and end apart: 21, of which 12 were waited for; matrix products, arithmetic and copies ran while one was open for 2% of the time, Pallas kernels for 14%

profile of v7, /device:TPU:2, one launch (start us, length us, event | category | flops | bytes accessed | tf_op | source)
XLA Modules:
  0.0 244.5 jit_solution(15959070812620045668)
XLA Ops:
  0.0 2.6 %pack.1 = bf16[4,2,4,256,128]{4,3,2,1,0:T(8,128)(2,1)} custom-call(bf16[2048,512]{1,0:T(8,128)(2,1)} %x_ref.3), custom_call_target="tpu_custom_call" | custom-call | bytes 4194304 | tf_op jit(solution)/shard_map/pack/pallas_call | solution.py:81
  2.6 4.3 %all-to-all-start.1 = ((bf16[8,4,256,128]{3,2,1,0:T(8,128)(2,1)}), bf16[8,4,256,128]{3,2,1,0:T(8,128)(2,1)S(1)}, u32[]{:S(2)}, u32[]{:S(2)}) async-start(bf16[8,4,256,128]{3,2,1,0:T(8,128)(2,1)} %bitcast.14), calls=%async_computation.1 | async-start | bytes 4194304 | tf_op jit(solution)/shard_map/all_to_all | solution.py:731
  6.9 4.1 %turn.1 = bf16[4,2,4,128,256]{4,3,2,1,0:T(8,128)(2,1)} custom-call(bf16[2048,512]{1,0:T(8,128)(2,1)} %x_ref.2), custom_call_target="tpu_custom_call" | custom-call | bytes 4194304 | tf_op jit(solution)/shard_map/turn/pallas_call | solution.py:72
  11.0 21.0 %all-to-all-done.1.refs_0_ = bf16[8,4,256,128]{3,2,1,0:T(8,128)(2,1)S(1)} async-done(((bf16[8,4,256,128]{3,2,1,0:T(8,128)(2,1)}), bf16[8,4,256,128]{3,2,1,0:T(8,128)(2,1)S(1)}, u32[]{:S(2)}, u32[]{:S(2)}) %all-to-all-start.1) | async-done | bytes 2097184 | tf_op jit(solution)/shard_map/all_to_all | solution.py:731
  32.0 1.3 copy-done.3
  33.4 5.0 %all-to-all-start = ((bf16[8,4,128,256]{3,2,1,0:T(8,128)(2,1)}), bf16[8,4,128,256]{3,2,1,0:T(8,128)(2,1)S(1)}, u32[]{:S(2)}, u32[]{:S(2)}) async-start(bf16[8,4,128,256]{3,2,1,0:T(8,128)(2,1)} %bitcast.13), calls=%async_computation | async-start | bytes 4194304 | tf_op jit(solution)/shard_map/all_to_all | solution.py:731
  38.6 24.9 %all-to-all-done = bf16[8,4,128,256]{3,2,1,0:T(8,128)(2,1)S(1)} async-done(((bf16[8,4,128,256]{3,2,1,0:T(8,128)(2,1)}), bf16[8,4,128,256]{3,2,1,0:T(8,128)(2,1)S(1)}, u32[]{:S(2)}, u32[]{:S(2)}) %all-to-all-start) | async-done | bytes 2097184 | tf_op jit(solution)/shard_map/all_to_all | solution.py:731
  64.9 4.5 %collective-permute-start.10 = (bf16[256,2048]{1,0:T(8,128)(2,1)S(1)}, bf16[256,2048]{1,0:T(8,128)(2,1)}, u32[]{:S(2)}, u32[]{:S(2)}) collective-permute-start(bf16[256,2048]{1,0:T(8,128)(2,1)S(1)} %constant_dynamic-slice_fusion), channel_id=1, source_target_pairs={{0,1},{1,2},{2,3},{4,5},{5,6},{6,7},{8,9},{9,10},{10,11},{12,13},{... | collective-permute-start | bytes 3145736 | tf_op jit(solution)/shard_map/ppermute | solution.py:629
  74.3 3.9 %collective-permute-done.1 = s32[56]{0:T(128)S(1)} collective-permute-done((s32[56]{0:T(128)S(1)}, s32[56]{0:T(128)S(1)}, u32[]{:S(2)}, u32[]{:S(2)}) %collective-permute-start.1) | collective-permute-done | bytes 256 | tf_op jit(solution)/shard_map/ppermute | solution.py:101
  78.7 3.3 %collective-permute-done.2 = s32[56]{0:T(128)S(1)} collective-permute-done((s32[56]{0:T(128)S(1)}, s32[56]{0:T(128)S(1)}, u32[]{:S(2)}, u32[]{:S(2)}) %collective-permute-start.2) | collective-permute-done | bytes 256 | tf_op jit(solution)/shard_map/ppermute | solution.py:101
  82.6 3.0 %collective-permute-done.3 = s32[56]{0:T(128)S(1)} collective-permute-done((s32[56]{0:T(128)S(1)}, s32[56]{0:T(128)S(1)}, u32[]{:S(2)}, u32[]{:S(2)}) %collective-permute-start.3) | collective-permute-done | bytes 256 | tf_op jit(solution)/shard_map/ppermute | solution.py:101
  85.6 3.0 %collective-permute-done.4 = s32[56]{0:T(128)S(1)} collective-permute-done((s32[56]{0:T(128)S(1)}, s32[56]{0:T(128)S(1)}, u32[]{:S(2)}, u32[]{:S(2)}) %collective-permute-start.4) | collective-permute-done | bytes 256 | tf_op jit(solution)/shard_map/ppermute | solution.py:101
  88.6 3.6 %collective-permute-done.5 = s32[56]{0:T(128)S(1)} collective-permute-done((s32[56]{0:T(128)S(1)}, s32[56]{0:T(128)S(1)}, u32[]{:S(2)}, u32[]{:S(2)}) %collective-permute-start.5) | collective-permute-done | bytes 256 | tf_op jit(solution)/shard_map/ppermute | solution.py:101
  92.8 2.4 collective-permute-done.6
  95.8 5.2 %job_lists.1 = (s32[1]{0:T(128)}, s32[448]{0:T(512)}, s32[448]{0:T(512)}) custom-call(s32[448]{0:T(512)} %concatenate.8.tab_ref, s32[16,64]{1,0:T(8,128)} %bitcast.15, s32[4]{0:T(128)} %pad_add_fusion.spot_ref), custom_call_target="tpu_custom_call" | custom-call | bytes 33554432 | tf_op jit(solution)/shard_map/job_lists/pallas_call | solution.py:167
  101.1 1.7 collective-permute-start.11
  102.8 14.9 %attend_scores.1 = (bf16[448,256,256]{2,1,0:T(8,128)(2,1)}, f32[448,256]{1,0:T(8,128)}) custom-call(s32[4]{0:T(128)} %pad_add_fusion.spot_ref, s32[1]{0:T(128)} %get-tuple-element.10.count_ref, s32[448]{0:T(512)} %get-tuple-element.11.unit_ref, s32[448]{0:T(512)} %get-tuple-element.12.key_ref, bf16[8,4,256,128]{3,2,1,0:T(8,128)(2,1)} %copy-done.3, ...), custom_call_target="tpu_custom_call" | custom-call | flops 1610612736 | bytes 16777216 | tf_op jit(solution)/shard_map/attend_scores/pallas_call | solution.py:479
  117.8 10.4 %attend_values.1 = bf16[32,256,128]{2,1,0:T(8,128)(2,1)} custom-call(s32[4]{0:T(128)S(1)} %copy-done, s32[1]{0:T(128)} %get-tuple-element.10.count_ref, s32[448]{0:T(512)S(1)} %copy-done.1, s32[448]{0:T(512)S(1)} %copy-done.2, bf16[32,128,256]{2,1,0:T(8,128)(2,1)S(1)} %bitcast.11, bf16[32,128,256]{2,1,0:T(8,128)(2,1)} %bitcast.8.refs_1_, ...), custom_call_target="tpu_custom_call" | custom-call | flops 1610612736 | bytes 16777216 | tf_op jit(solution)/shard_map/attend_values/pallas_call | solution.py:593
  128.2 9.5 %all-to-all-start.2 = ((bf16[32,256,128]{2,1,0:T(8,128)(2,1)}), bf16[32,256,128]{2,1,0:T(8,128)(2,1)S(1)}, u32[]{:S(2)}, u32[]{:S(2)}) async-start(bf16[32,256,128]{2,1,0:T(8,128)(2,1)} %attend_values.1), calls=%async_computation.2 | async-start | bytes 4194304 | tf_op jit(solution)/shard_map/all_to_all | solution.py:745
  139.0 1.6 collective-permute-start.12
  140.7 55.8 %collective-permute-done.14 = bf16[256,2048]{1,0:T(8,128)(2,1)S(1)} collective-permute-done((bf16[256,2048]{1,0:T(8,128)(2,1)}, bf16[256,2048]{1,0:T(8,128)(2,1)S(1)}, u32[]{:S(2)}, u32[]{:S(2)}) %collective-permute-start.14) | collective-permute-done | bytes 1048608 | tf_op jit(solution)/shard_map/ppermute | solution.py:630
  198.0 1.6 broadcast_select_fusion.2.refs_0_
  199.9 33.4 %collective-permute-done.16 = bf16[256,2048]{1,0:T(8,128)(2,1)S(1)} collective-permute-done((bf16[256,2048]{1,0:T(8,128)(2,1)S(1)}, bf16[256,2048]{1,0:T(8,128)(2,1)S(1)}, u32[]{:S(2)}, u32[]{:S(2)}) %collective-permute-start.16) | collective-permute-done | bytes 1048608 | tf_op jit(solution)/shard_map/ppermute | solution.py:630
  236.3 8.2 %project.1 = bf16[512,2048]{1,0:T(8,128)(2,1)} custom-call(s32[4]{0:T(128)} %pad_add_fusion.spot_ref, bf16[4,2,4,256,128]{4,3,2,1,0:T(8,128)(2,1)S(1)} %bitcast.12, bf16[512,2048]{1,0:T(8,128)(2,1)} %w_ref.1, bf16[256,2048]{1,0:T(8,128)(2,1)} %copy-done.5, bf16[256,2048]{1,0:T(8,128)(2,1)} %copy-done.11, bf16[256,2048]{1,0:T(8,128)(2,1)} %copy-done.4, ...), custom_call_target="tpu_custom_call" | custom-call | flops 4294967296 | bytes 8388608 | tf_op jit(solution)/shard_map/project/pallas_call | solution.py:691
  (59 shorter events, 14.9 us)
Async XLA Ops:
  2.6 29.4 %all-to-all-start.1 = ((bf16[8,4,256,128]{3,2,1,0:T(8,128)(2,1)}), bf16[8,4,256,128]{3,2,1,0:T(8,128)(2,1)S(1)}, u32[]{:S(2)}, u32[]{:S(2)}) async-start(bf16[8,4,256,128]{3,2,1,0:T(8,128)(2,1)} %bitcast.14), calls=%async_computation.1 | async-start | bytes 4194304 | tf_op jit(solution)/shard_map/all_to_all | solution.py:731
  33.4 30.1 %all-to-all-start = ((bf16[8,4,128,256]{3,2,1,0:T(8,128)(2,1)}), bf16[8,4,128,256]{3,2,1,0:T(8,128)(2,1)S(1)}, u32[]{:S(2)}, u32[]{:S(2)}) async-start(bf16[8,4,128,256]{3,2,1,0:T(8,128)(2,1)} %bitcast.13), calls=%async_computation | async-start | bytes 4194304 | tf_op jit(solution)/shard_map/all_to_all | solution.py:731
  38.4 32.6 %copy-start.7 = (s32[1,8]{1,0:T(1,128)S(1)}, s32[1,8]{1,0:T(1,128)}, u32[]{:S(2)}) copy-start(s32[1,8]{1,0:T(1,128)} %param.12) | copy-start | bytes 100
  38.4 64.4 %collective-permute-start.8 = (bf16[8,4,256,128]{3,2,1,0:T(8,128)(2,1)}, bf16[8,4,256,128]{3,2,1,0:T(8,128)(2,1)}, u32[]{:S(2)}, u32[]{:S(2)}) collective-permute-start(bf16[8,4,256,128]{3,2,1,0:T(8,128)(2,1)} %copy-done.3), channel_id=1, source_target_pairs={{4,0},{0,4},{12,8},{8,12},{20,16},{16,20},{28,24},{24,28},{5,1},{1... | collective-permute-start | bytes 6291464 | tf_op jit(solution)/shard_map/ppermute | solution.py:619
  63.5 54.2 %collective-permute-start.7 = (bf16[8,4,128,256]{3,2,1,0:T(8,128)(2,1)S(1)}, bf16[8,4,128,256]{3,2,1,0:T(8,128)(2,1)}, u32[]{:S(2)}, u32[]{:S(2)}) collective-permute-start(bf16[8,4,128,256]{3,2,1,0:T(8,128)(2,1)S(1)} %all-to-all-done), channel_id=1, source_target_pairs={{4,0},{0,4},{12,8},{8,12},{20,16},{16,20},{28,24},{24,28},{5,1},{1... | collective-permute-start | bytes 6291464 | tf_op jit(solution)/shard_map/ppermute | solution.py:619
  64.9 36.2 %collective-permute-start.10 = (bf16[256,2048]{1,0:T(8,128)(2,1)S(1)}, bf16[256,2048]{1,0:T(8,128)(2,1)}, u32[]{:S(2)}, u32[]{:S(2)}) collective-permute-start(bf16[256,2048]{1,0:T(8,128)(2,1)S(1)} %constant_dynamic-slice_fusion), channel_id=1, source_target_pairs={{0,1},{1,2},{2,3},{4,5},{5,6},{6,7},{8,9},{9,10},{10,11},{12,13},{... | collective-permute-start | bytes 3145736 | tf_op jit(solution)/shard_map/ppermute | solution.py:629
  69.4 68.3 %collective-permute-start.9 = (bf16[256,2048]{1,0:T(8,128)(2,1)S(1)}, bf16[256,2048]{1,0:T(8,128)(2,1)}, u32[]{:S(2)}, u32[]{:S(2)}) collective-permute-start(bf16[256,2048]{1,0:T(8,128)(2,1)S(1)} %constant_dynamic-slice_fusion), channel_id=1, source_target_pairs={{1,0},{2,1},{3,2},{5,4},{6,5},{7,6},{9,8},{10,9},{11,10},{13,12},{... | collective-permute-start | bytes 3145736 | tf_op jit(solution)/shard_map/ppermute | solution.py:630
  71.1 2.6 %collective-permute-start = (s32[56]{0:T(128)S(1)}, s32[56]{0:T(128)S(1)}, u32[]{:S(2)}, u32[]{:S(2)}) collective-permute-start(s32[56]{0:T(128)S(1)} %pad_add_fusion.1), channel_id=1, source_target_pairs={{4,0},{8,4},{12,8},{16,12},{20,16},{24,20},{28,24},{0,28},{5,1},{9... | collective-permute-start | bytes 680 | tf_op jit(solution)/shard_map/ppermute | solution.py:101
  73.7 4.5 %collective-permute-start.1 = (s32[56]{0:T(128)S(1)}, s32[56]{0:T(128)S(1)}, u32[]{:S(2)}, u32[]{:S(2)}) collective-permute-start(s32[56]{0:T(128)S(1)} %pad_add_fusion.1), channel_id=1, source_target_pairs={{8,0},{12,4},{16,8},{20,12},{24,16},{28,20},{0,24},{4,28},{9,1},{1... | collective-permute-start | bytes 680 | tf_op jit(solution)/shard_map/ppermute | solution.py:101
  78.1 3.9 %collective-permute-start.2 = (s32[56]{0:T(128)S(1)}, s32[56]{0:T(128)S(1)}, u32[]{:S(2)}, u32[]{:S(2)}) collective-permute-start(s32[56]{0:T(128)S(1)} %pad_add_fusion.1), channel_id=1, source_target_pairs={{12,0},{16,4},{20,8},{24,12},{28,16},{0,20},{4,24},{8,28},{13,1},{... | collective-permute-start | bytes 680 | tf_op jit(solution)/shard_map/ppermute | solution.py:101
  82.0 3.6 %collective-permute-start.3 = (s32[56]{0:T(128)S(1)}, s32[56]{0:T(128)S(1)}, u32[]{:S(2)}, u32[]{:S(2)}) collective-permute-start(s32[56]{0:T(128)S(1)} %pad_add_fusion.1), channel_id=1, source_target_pairs={{16,0},{20,4},{24,8},{28,12},{0,16},{4,20},{8,24},{12,28},{17,1},{... | collective-permute-start | bytes 680 | tf_op jit(solution)/shard_map/ppermute | solution.py:101
  85.6 3.0 %collective-permute-start.4 = (s32[56]{0:T(128)S(1)}, s32[56]{0:T(128)S(1)}, u32[]{:S(2)}, u32[]{:S(2)}) collective-permute-start(s32[56]{0:T(128)S(1)} %pad_add_fusion.1), channel_id=1, source_target_pairs={{20,0},{24,4},{28,8},{0,12},{4,16},{8,20},{12,24},{16,28},{21,1},{... | collective-permute-start | bytes 680 | tf_op jit(solution)/shard_map/ppermute | solution.py:101
  88.6 3.6 %collective-permute-start.5 = (s32[56]{0:T(128)S(1)}, s32[56]{0:T(128)S(1)}, u32[]{:S(2)}, u32[]{:S(2)}) collective-permute-start(s32[56]{0:T(128)S(1)} %pad_add_fusion.1), channel_id=1, source_target_pairs={{24,0},{28,4},{0,8},{4,12},{8,16},{12,20},{16,24},{20,28},{25,1},{... | collective-permute-start | bytes 680 | tf_op jit(solution)/shard_map/ppermute | solution.py:101
  92.2 3.0 %collective-permute-start.6 = (s32[56]{0:T(128)S(1)}, s32[56]{0:T(128)S(1)}, u32[]{:S(2)}, u32[]{:S(2)}) collective-permute-start(s32[56]{0:T(128)S(1)} %pad_add_fusion.1), channel_id=1, source_target_pairs={{28,0},{0,4},{4,8},{8,12},{12,16},{16,20},{20,24},{24,28},{29,1},{... | collective-permute-start | bytes 680 | tf_op jit(solution)/shard_map/ppermute | solution.py:101
  101.1 37.9 %collective-permute-start.11 = (bf16[256,2048]{1,0:T(8,128)(2,1)}, bf16[256,2048]{1,0:T(8,128)(2,1)}, u32[]{:S(2)}, u32[]{:S(2)}) collective-permute-start(bf16[256,2048]{1,0:T(8,128)(2,1)} %collective-permute-done.10), channel_id=1, source_target_pairs={{1,2},{2,3},{5,6},{6,7},{9,10},{10,11},{13,14},{14,15},{17,18},{18... | collective-permute-start | bytes 3145736 | tf_op jit(solution)/shard_map/ppermute | solution.py:629
  128.2 108.2 %all-to-all-start.2 = ((bf16[32,256,128]{2,1,0:T(8,128)(2,1)}), bf16[32,256,128]{2,1,0:T(8,128)(2,1)S(1)}, u32[]{:S(2)}, u32[]{:S(2)}) async-start(bf16[32,256,128]{2,1,0:T(8,128)(2,1)} %attend_values.1), calls=%async_computation.2 | async-start | bytes 4194304 | tf_op jit(solution)/shard_map/all_to_all | solution.py:745
  137.7 58.7 %collective-permute-start.14 = (bf16[256,2048]{1,0:T(8,128)(2,1)}, bf16[256,2048]{1,0:T(8,128)(2,1)S(1)}, u32[]{:S(2)}, u32[]{:S(2)}) collective-permute-start(bf16[256,2048]{1,0:T(8,128)(2,1)} %collective-permute-done.9), channel_id=1, source_target_pairs={{1,0},{2,1},{5,4},{6,5},{9,8},{10,9},{13,12},{14,13},{17,16},{18,1... | collective-permute-start | bytes 3145736 | tf_op jit(solution)/shard_map/ppermute | solution.py:630
  139.0 58.9 %collective-permute-start.12 = (bf16[256,2048]{1,0:T(8,128)(2,1)}, bf16[256,2048]{1,0:T(8,128)(2,1)}, u32[]{:S(2)}, u32[]{:S(2)}) collective-permute-start(bf16[256,2048]{1,0:T(8,128)(2,1)} %collective-permute-done.11), channel_id=1, source_target_pairs={{2,3},{6,7},{10,11},{14,15},{18,19},{22,23},{26,27},{30,31}} | collective-permute-start | bytes 3145736 | tf_op jit(solution)/shard_map/ppermute | solution.py:629
  196.5 36.8 %collective-permute-start.16 = (bf16[256,2048]{1,0:T(8,128)(2,1)S(1)}, bf16[256,2048]{1,0:T(8,128)(2,1)S(1)}, u32[]{:S(2)}, u32[]{:S(2)}) collective-permute-start(bf16[256,2048]{1,0:T(8,128)(2,1)S(1)} %collective-permute-done.14), channel_id=1, source_target_pairs={{1,0},{5,4},{9,8},{13,12},{17,16},{21,20},{25,24},{29,28}} | collective-permute-start | bytes 3145736 | tf_op jit(solution)/shard_map/ppermute | solution.py:630
  197.9 35.6 %copy-start.4 = (bf16[256,2048]{1,0:T(8,128)(2,1)}, bf16[256,2048]{1,0:T(8,128)(2,1)S(1)}, u32[]{:S(2)}) copy-start(bf16[256,2048]{1,0:T(8,128)(2,1)S(1)} %broadcast_select_fusion.1.refs_2_) | copy-start | bytes 3145732
  197.9 35.7 %collective-permute-start.15 = (bf16[256,2048]{1,0:T(8,128)(2,1)S(1)}, bf16[256,2048]{1,0:T(8,128)(2,1)S(1)}, u32[]{:S(2)}, u32[]{:S(2)}) collective-permute-start(bf16[256,2048]{1,0:T(8,128)(2,1)S(1)} %broadcast_select_fusion.1.refs_2_), channel_id=1, source_target_pairs={{4,0},{0,4},{12,8},{8,12},{20,16},{16,20},{28,24},{24,28},{5,1},{1... | collective-permute-start | bytes 3145736 | tf_op jit(solution)/shard_map/ppermute | solution.py:619
  199.6 34.0 %copy-start.5 = (bf16[256,2048]{1,0:T(8,128)(2,1)}, bf16[256,2048]{1,0:T(8,128)(2,1)S(1)}, u32[]{:S(2)}) copy-start(bf16[256,2048]{1,0:T(8,128)(2,1)S(1)} %broadcast_select_fusion.2.refs_0_) | copy-start | bytes 3145732
  199.6 33.9 %collective-permute-start.13 = (bf16[256,2048]{1,0:T(8,128)(2,1)S(1)}, bf16[256,2048]{1,0:T(8,128)(2,1)S(1)}, u32[]{:S(2)}, u32[]{:S(2)}) collective-permute-start(bf16[256,2048]{1,0:T(8,128)(2,1)S(1)} %broadcast_select_fusion.2.refs_0_), channel_id=1, source_target_pairs={{4,0},{0,4},{12,8},{8,12},{20,16},{16,20},{28,24},{24,28},{5,1},{1... | collective-permute-start | bytes 3145736 | tf_op jit(solution)/shard_map/ppermute | solution.py:619
  233.5 2.9 %collective-permute-start.17 = (bf16[256,2048]{1,0:T(8,128)(2,1)S(1)}, bf16[256,2048]{1,0:T(8,128)(2,1)}, u32[]{:S(2)}, u32[]{:S(2)}) collective-permute-start(bf16[256,2048]{1,0:T(8,128)(2,1)S(1)} %broadcast_select_fusion.refs_4_), channel_id=1, source_target_pairs={{4,0},{0,4},{12,8},{8,12},{20,16},{16,20},{28,24},{24,28},{5,1},{1... | collective-permute-start | bytes 3145736 | tf_op jit(solution)/shard_map/ppermute | solution.py:619
  (9 other events, 115.9 us)
